TPU v7x, 256 devices: a whole 4x4x8 slice. The times are simulated.
256 devices in a mesh: grp: 2 (over y_lo), seq: 128 (over x, y_hi, z, core).
Axes of the slice: x: 4, y: 4 (y_hi: 2, y_lo: 2; y = y_hi * 2 + y_lo), z: 8, core: 2. Of those that a mesh axis runs over, the one named last changes fastest.
Arguments:
- q_inv: bfloat16 [4, 32768, 2048], P('grp', 'seq'), may hold values from -4.5 to 4.5
- k_inv: bfloat16 [4, 32768, 2048], P('grp', 'seq'), may hold values from -4.5 to 4.5
- v_inv: bfloat16 [4, 32768, 2048], P('grp', 'seq'), may hold values from -6 to 6
- group_ids: int32 [4], replicated, may hold values from 0 to 3, each once
- w_attr: bfloat16 [4, 2048, 64], replicated, may hold values from -2.390625 to 2.390625
- env_ids: int32 [4, 32768], P('grp', 'seq'), may hold values from 0 to 4095
- env_table: bfloat16 [4096, 128], replicated, may hold values from -6 to 6
- w_embed_attr: bfloat16 [4, 64, 4096], replicated, may hold values from -1.5 to 1.5
- w_embed_env: bfloat16 [128, 4096], replicated, may hold values from -1.5 to 1.5
- mod_scale: bfloat16 [4, 4096], P('grp'), may hold values from -3 to 3
- mod_shift: bfloat16 [4, 4096], P('grp'), may hold values from -3 to 3
- w_final: bfloat16 [4096, 64], replicated, may hold values from -0.09375 to 0.09375
Outputs:
- attributes: bfloat16 [4, 32768, 64], P('grp', 'seq')
- rendered: bfloat16 [4, 32768, 64], P('grp', 'seq')
Inputs may be any that keep to these rules, and one draw needn't show every extreme that they name: `group_ids`: each kind 0 to 3 appears once.
All inputs are finite; a program needn't handle non-finite values.
Results may differ from a plain program's by a relative error of at most 0.012.
Values may be sent and summed in bfloat16 or wider, within the bound.
No kernel may reach another device: no remote copies, remote signals or barrier semaphores. Data moves between devices by JAX's collectives and lax.ppermute only.
A program may use at most 128 MiB of HBM per device.

v0:
```python
import jax
import jax.numpy as jnp
from jax import lax
from jax.sharding import PartitionSpec as P

HEADS = 16
HD = 128
SP = 4


def from_partner(block, axis, apart):
    count = lax.axis_size(axis)
    route = []
    for low in range(count):
        high = low | 1 << apart
        if high != low and high < count:
            route += [(low, high), (high, low)]
    return lax.ppermute(block, axis, route)


def absorb(carry_state, queries, kv_block, factor):
    running_max, totals, weighted = carry_state
    scores = (
        jnp.einsum("gqhd,gkhd->ghqk", queries, kv_block[0], preferred_element_type=jnp.float32)
        * factor
    )
    new_max = jnp.maximum(running_max, jnp.max(scores, axis=-1))
    rescale = jnp.exp(running_max - new_max)
    powers = jnp.exp(scores - new_max[..., None])
    totals = totals * rescale + jnp.sum(powers, axis=-1)
    weighted = weighted * rescale[..., None] + jnp.einsum(
        "ghqk,gkhd->ghqd",
        powers.astype(jnp.bfloat16),
        kv_block[1],
        preferred_element_type=jnp.float32,
    )
    return (new_max, totals, weighted)


def empty_state(local_groups, head_count, row_count):
    return (
        jnp.full((local_groups, head_count, row_count), -jnp.inf, jnp.float32),
        jnp.zeros((local_groups, head_count, row_count), jnp.float32),
        jnp.zeros((local_groups, head_count, row_count, HD), jnp.float32),
    )


def finish(carry_state):
    running_max, totals, weighted = carry_state
    attended = weighted / totals[..., None]
    return jnp.transpose(attended, (0, 2, 1, 3)).astype(jnp.bfloat16)


def on_device(
    q_inv,
    k_inv,
    v_inv,
    group_ids,
    w_attr,
    env_ids,
    env_table,
    w_embed_attr,
    w_embed_env,
    mod_scale,
    mod_shift,
    w_final,
):
    local_groups, tok_rows, feature_width = q_inv.shape
    factor = HD ** (-0.5)
    heads_q = q_inv.reshape(local_groups, tok_rows, HEADS, HD)
    keys_vals = jnp.stack((k_inv, v_inv)).reshape(2, local_groups, tok_rows, HEADS, HD)
    sections = SP.bit_length() - 1
    carry_state = absorb(empty_state(local_groups, HEADS, tok_rows), heads_q, keys_vals, factor)
    current = keys_vals
    for section in range(sections):
        received = from_partner(current, "seq", section)
        carry_state = absorb(carry_state, heads_q, received, factor)
        if section + 1 < sections:
            current = jnp.concatenate((current, received), axis=2)
    attended = finish(carry_state)
    attended = attended.reshape(local_groups, tok_rows, feature_width)
    first_group = lax.axis_index("grp") * local_groups
    readouts = []
    for group in range(local_groups):
        attr_kind = group_ids[first_group + group]
        weight = lax.dynamic_index_in_dim(w_attr, attr_kind, 0, keepdims=False)
        readouts.append(
            jnp.dot(attended[group], weight, preferred_element_type=jnp.float32).astype(
                jnp.bfloat16
            )
        )
    attributes = jnp.stack(readouts)
    everything = lax.all_gather(attributes, "grp", axis=0, tiled=True)
    kind_count = everything.shape[0]
    patch_width = everything.shape[2]
    selector = (group_ids[:, None] == jnp.arange(kind_count, dtype=jnp.int32)[None, :]).astype(
        jnp.bfloat16
    )
    arranged = jnp.einsum(
        "gk,gtc->tkc", selector, everything, preferred_element_type=jnp.float32
    ).astype(jnp.bfloat16)
    arranged = arranged.reshape(tok_rows, kind_count * patch_width)
    embedded = jnp.dot(
        arranged,
        w_embed_attr.reshape(kind_count * patch_width, -1),
        preferred_element_type=jnp.float32,
    )
    lighting = jnp.take(env_table, env_ids, axis=0)
    state = embedded[None] + jnp.einsum(
        "ltc,cd->ltd", lighting, w_embed_env, preferred_element_type=jnp.float32
    )
    average = jnp.mean(state, axis=-1, keepdims=True)
    centred = state - average
    spread = jnp.mean(centred * centred, axis=-1, keepdims=True)
    normed = centred * lax.rsqrt(spread + 1e-06)
    modulated = normed * (1.0 + mod_scale[:, None, :].astype(jnp.float32)) + mod_shift[
        :, None, :
    ].astype(jnp.float32)
    modulated = modulated.astype(jnp.bfloat16)
    rendered = jnp.einsum(
        "ltd,dp->ltp", modulated, w_final, preferred_element_type=jnp.float32
    ).astype(jnp.bfloat16)
    return (attributes, rendered)


def solution(mesh):
    in_specs = (
        P("grp", "seq", None),
        P("grp", "seq", None),
        P("grp", "seq", None),
        P(),
        P(),
        P("grp", "seq"),
        P(),
        P(),
        P(),
        P("grp", None),
        P("grp", None),
        P(),
    )
    out_specs = (P("grp", "seq", None), P("grp", "seq", None))
    return jax.shard_map(
        on_device, mesh=mesh, in_specs=in_specs, out_specs=out_specs, check_vma=False
    )
```

profile of v0, /device:TPU:1, one launch (start us, length us, event | category | flops | bytes accessed | tf_op | source)
XLA Modules:
  0.0 269.2 jit_solution(525536236555951763)
XLA Ops:
  0.6 0.0 copy-start
  0.6 4.1 %copy.59 = bf16[2,256,2048]{1,2,0:T(8,128)(2,1)} copy(bf16[2,256,2048]{2,1,0:T(8,128)(2,1)} %param.14) | data formatting | bytes 4194304 | tf_op jit(solution)/shard_map/squeeze | solution.py:34
  4.8 3.9 %copy.45 = bf16[1,2,256,16,128]{4,2,3,1,0:T(8,128)(2,1)} copy(bf16[1,2,256,16,128]{2,4,3,1,0:T(8,128)(2,1)} %bitcast.173) | data formatting | bytes 4194304 | tf_op jit(solution)/shard_map/stack | solution.py:71
  8.7 3.9 %copy.42 = bf16[2,256,2048]{1,2,0:T(8,128)(2,1)} copy(bf16[2,256,2048]{2,1,0:T(8,128)(2,1)} %param.13) | data formatting | bytes 4194304 | tf_op args[1]
  12.6 4.0 %copy.44 = bf16[1,2,256,16,128]{4,2,3,1,0:T(8,128)(2,1)} copy(bf16[1,2,256,16,128]{2,4,3,1,0:T(8,128)(2,1)} %bitcast.175) | data formatting | bytes 4194304 | tf_op jit(solution)/shard_map/stack | solution.py:71
  16.6 2.8 %pad_maximum_fusion.1 = bf16[2,2,256,16,128]{4,2,3,1,0:T(8,128)(2,1)S(1)} fusion(bf16[1,2,256,16,128]{4,2,3,1,0:T(8,128)(2,1)} %copy.45, bf16[1,2,256,16,128]{4,2,3,1,0:T(8,128)(2,1)} %copy.44), kind=kLoop, calls=%fused_computation.28 | loop fusion | flops 2097152 | bytes 8388608 | tf_op jit(solution)/shard_map/stack | solution.py:71
  19.4 0.0 copy-start.16
  19.4 3.3 %collective-permute-start = (bf16[2,2,256,16,128]{4,2,3,1,0:T(8,128)(2,1)S(1)}, bf16[2,2,256,16,128]{4,2,3,1,0:T(8,128)(2,1)S(1)}, u32[]{:S(2)}, u32[]{:S(2)}) collective-permute-start(bf16[2,2,256,16,128]{4,2,3,1,0:T(8,128)(2,1)S(1)} %pad_maximum_fusion.1), channel_id=1, source_target_pairs={{0,1},{1,0},{2,3},{3,2},{4,5},{5,4},{6,7},{7,6},{8,9},{9,8},{10,11... | collective-permute-start | bytes 12582920 | tf_op jit(solution)/shard_map/ppermute | solution.py:18
  22.7 6.8 %collective-permute-done = bf16[2,2,256,16,128]{4,2,3,1,0:T(8,128)(2,1)S(1)} collective-permute-done((bf16[2,2,256,16,128]{4,2,3,1,0:T(8,128)(2,1)S(1)}, bf16[2,2,256,16,128]{4,2,3,1,0:T(8,128)(2,1)S(1)}, u32[]{:S(2)}, u32[]{:S(2)}) %collective-permute-start) | collective-permute-done | bytes 4194336 | tf_op jit(solution)/shard_map/ppermute | solution.py:18
  29.5 4.5 %pad_maximum_fusion = bf16[2,2,512,16,128]{4,2,3,1,0:T(8,128)(2,1)} fusion(bf16[2,2,256,16,128]{4,2,3,1,0:T(8,128)(2,1)S(1)} %collective-permute-done, bf16[1,2,256,16,128]{4,2,3,1,0:T(8,128)(2,1)S(1)} %copy-done.4, bf16[1,2,256,16,128]{4,2,3,1,0:T(8,128)(2,1)S(1)} %copy-done.5), kind=kLoop, calls=%fused_computation.7 | loop fusion | flops 25165824 | bytes 16777216 | tf_op jit(solution)/shard_map/concatenate | solution.py:79
  34.0 0.6 fusion.74
  38.6 1.3 gather_fusion
  39.9 2.9 %multiply_reduce_fusion.1 = (f32[2,16,256]{2,1,0:T(8,128)S(1)}, f32[2,16,256,256]{2,3,1,0:T(8,128)S(1)}) fusion(bf16[2,256,2048]{2,1,0:T(8,128)(2,1)} %param.13, bf16[2,256,2048]{2,1,0:T(8,128)(2,1)S(1)} %copy-done), kind=kOutput, calls=%fused_computation.16 | convolution fusion | flops 541057024 | bytes 12615680 | tf_op jit(solution)/shard_map/gqhd,gkhd->ghqk/dot_general | solution.py:24
  42.8 1.6 fusion.8
  44.5 3.6 %fusion.14 = f32[2,16,256,128]{2,3,1,0:T(8,128)} fusion(bf16[2,256,16,128]{1,3,2,0:T(8,128)(2,1)S(1)} %bitcast.174, f32[2,16,256,256]{2,3,1,0:T(8,128)S(1)} %get-tuple-element.15, f32[2,16,256]{2,1,0:T(8,128)S(1)} %get-tuple-element.14), kind=kOutput, calls=%fused_computation.24 | convolution fusion | flops 543162368 | bytes 14712832 | tf_op jit(solution)/shard_map/ghqk,gkhd->ghqd/dot_general | solution.py:31
  48.1 1.4 bitcast_reduce_fusion.1
  49.5 166.5 %collective-permute-done.1 = bf16[2,2,512,16,128]{4,2,3,1,0:T(8,128)(2,1)} collective-permute-done((bf16[2,2,512,16,128]{4,2,3,1,0:T(8,128)(2,1)}, bf16[2,2,512,16,128]{4,2,3,1,0:T(8,128)(2,1)}, u32[]{:S(2)}, u32[]{:S(2)}) %collective-permute-start.1) | collective-permute-done | bytes 8388640 | tf_op jit(solution)/shard_map/ppermute | solution.py:18
  216.0 10.3 %bitcast_reduce_fusion = (f32[2,16,256]{2,1,0:T(8,128)S(1)}, f32[2,16,512,256]{3,2,1,0:T(8,128)}) fusion(bf16[2,2,512,16,128]{4,2,3,1,0:T(8,128)(2,1)} %collective-permute-done.1, bf16[2,256,2048]{2,1,0:T(8,128)(2,1)S(1)} %copy-done), kind=kOutput, calls=%fused_computation.2 | convolution fusion | flops 1082122240 | bytes 23101440 | tf_op jit(solution)/shard_map/gqhd,gkhd->ghqk/dot_general | solution.py:24
  226.2 2.9 %fusion.10 = f32[2,16,256]{2,1,0:T(8,128)S(1)} fusion(f32[2,16,256,256]{2,3,1,0:T(8,128)S(1)} %get-tuple-element.17, f32[2,16,256]{2,1,0:T(8,128)S(1)} %get-tuple-element.6), kind=kLoop, calls=%fused_computation.20 | loop fusion | flops 6283264 | bytes 8454144 | tf_op jit(solution)/shard_map/reduce_sum | solution.py:30
  229.2 8.8 %fusion.1 = f32[2,16,256]{2,1,0:T(8,128)S(1)} fusion(f32[2,16,512,256]{3,2,1,0:T(8,128)} %get-tuple-element.13, f32[2,16,256]{2,1,0:T(8,128)S(1)} %get-tuple-element.5), kind=kLoop, calls=%fused_computation.4 | loop fusion | flops 12574720 | bytes 16842752 | tf_op jit(solution)/shard_map/reduce_sum | solution.py:30
  238.0 6.9 %fusion.12 = f32[2,16,256,128]{2,3,1,0:T(8,128)} fusion(f32[2,16,256,256]{2,3,1,0:T(8,128)} %copy-done.2, f32[2,16,256]{2,1,0:T(8,128)S(1)} %get-tuple-element.6, bf16[2,2,256,16,128]{4,2,3,1,0:T(8,128)(2,1)} %copy-done.6), kind=kOutput, calls=%fused_computation.23 | convolution fusion | flops 543162368 | bytes 14712832 | tf_op jit(solution)/shard_map/ghqk,gkhd->ghqd/dot_general | solution.py:31
  244.9 12.1 %fusion.18 = bf16[2,256,16,128]{1,3,2,0:T(8,128)(2,1)S(1)} fusion(f32[2,16,256,128]{2,3,1,0:T(8,128)} %fusion.12, f32[2,16,256,128]{2,3,1,0:T(8,128)} %fusion.14, f32[2,256,16]{1,2,0:T(8,128)S(1)} %get-tuple-element.2, f32[2,256,16]{1,2,0:T(8,128)S(1)} %get-tuple-element.4, f32[2,256,16]{1,2,0:T(8,128)S(1)} %get-tuple-element.3, ...), kind=kOutput, calls=%fused_computation.31 | convolution fusion | flops 1093664768 | bytes 31621120 | tf_op jit(solution)/shard_map/ghqk,gkhd->ghqd/dot_general | solution.py:31
  257.0 0.2 fusion.73
  257.2 1.0 copy-done.11
  258.2 0.3 fusion.38
  258.5 0.3 fusion.39
  258.9 3.8 %all_gather.3 = bf16[4,256,64]{1,2,0:T(8,128)(2,1)S(1)} all-gather(bf16[2,256,64]{1,2,0:T(8,128)(2,1)S(1)} %pad_maximum_fusion.2), channel_id=1, replica_groups=mesh['grp'=2,'seq'=128] {'grp'}, dimensions={0}, use_global_device_ids=true | all-gather | bytes 196608 | tf_op jit(solution)/shard_map/all_gather | solution.py:93
  262.6 0.2 fusion.36
  262.9 0.7 convolution_bitcast_fusion
  263.6 1.5 add_reduce_fusion
  265.1 1.4 multiply_reduce_fusion
  266.5 2.7 %fusion.37 = bf16[2,256,64]{1,2,0:T(8,128)(2,1)} fusion(f32[2,256,4096]{2,1,0:T(8,128)S(1)} %get-tuple-element.19, f32[2,4096]{1,0:T(2,128)S(1)} %convert_element_type.48, f32[2,4096]{1,0:T(2,128)S(1)} %convert_add_fusion, f32[2,256]{1,0:T(2,128)S(1)} %add_rsqrt_fusion, f32[2,256]{1,0:T(2,128)S(1)} %broadcast_multiply_fusion, ...), kind=kOutput, calls=%fused_computation.55 | convolution fusion | flops 281051136 | bytes 13242368 | tf_op jit(solution)/shard_map/ltd,dp->ltp/dot_general | solution.py:120
  (45 shorter events, 0.2 us)
Async XLA Ops:
  0.6 39.3 %copy-start = (bf16[2,256,2048]{2,1,0:T(8,128)(2,1)S(1)}, bf16[2,256,2048]{2,1,0:T(8,128)(2,1)}, u32[]{:S(2)}) copy-start(bf16[2,256,2048]{2,1,0:T(8,128)(2,1)} %param.12) | copy-start | bytes 6291460
  16.6 12.9 %copy-start.4 = (bf16[1,2,256,16,128]{4,2,3,1,0:T(8,128)(2,1)S(1)}, bf16[1,2,256,16,128]{4,2,3,1,0:T(8,128)(2,1)}, u32[]{:S(2)}) copy-start(bf16[1,2,256,16,128]{4,2,3,1,0:T(8,128)(2,1)} %copy.45) | copy-start | bytes 6291460
  16.6 12.9 %copy-start.5 = (bf16[1,2,256,16,128]{4,2,3,1,0:T(8,128)(2,1)S(1)}, bf16[1,2,256,16,128]{4,2,3,1,0:T(8,128)(2,1)}, u32[]{:S(2)}) copy-start(bf16[1,2,256,16,128]{4,2,3,1,0:T(8,128)(2,1)} %copy.44) | copy-start | bytes 6291460
  19.4 14.7 %copy-start.16 = (s32[4]{0:T(128)S(1)}, s32[4]{0:T(128)}, u32[]{:S(2)}) copy-start(s32[4]{0:T(128)} %param.15) | copy-start | bytes 52
  19.4 17.8 %copy-start.15 = (s32[2,256]{1,0:T(2,128)S(1)}, s32[2,256]{1,0:T(2,128)}, u32[]{:S(2)}) copy-start(s32[2,256]{1,0:T(2,128)} %param.17) | copy-start | bytes 6148
  19.4 17.8 %copy-start.13 = (bf16[2,4096]{1,0:T(2,128)(2,1)S(1)}, bf16[2,4096]{1,0:T(2,128)(2,1)}, u32[]{:S(2)}) copy-start(bf16[2,4096]{1,0:T(2,128)(2,1)} %param.22) | copy-start | bytes 49156
  19.4 19.2 %copy-start.10 = (bf16[4096,128]{1,0:T(8,128)(2,1)S(1)}, bf16[4096,128]{1,0:T(8,128)(2,1)}, u32[]{:S(2)}) copy-start(bf16[4096,128]{1,0:T(8,128)(2,1)} %param.18) | copy-start | bytes 3145732
  19.4 10.1 %collective-permute-start = (bf16[2,2,256,16,128]{4,2,3,1,0:T(8,128)(2,1)S(1)}, bf16[2,2,256,16,128]{4,2,3,1,0:T(8,128)(2,1)S(1)}, u32[]{:S(2)}, u32[]{:S(2)}) collective-permute-start(bf16[2,2,256,16,128]{4,2,3,1,0:T(8,128)(2,1)S(1)} %pad_maximum_fusion.1), channel_id=1, source_target_pairs={{0,1},{1,0},{2,3},{3,2},{4,5},{5,4},{6,7},{7,6},{8,9},{9,8},{10,11... | collective-permute-start | bytes 12582920 | tf_op jit(solution)/shard_map/ppermute | solution.py:18
  29.5 4.5 %copy-start.6 = (bf16[2,2,256,16,128]{4,2,3,1,0:T(8,128)(2,1)}, bf16[2,2,256,16,128]{4,2,3,1,0:T(8,128)(2,1)S(1)}, u32[]{:S(2)}) copy-start(bf16[2,2,256,16,128]{4,2,3,1,0:T(8,128)(2,1)S(1)} %collective-permute-done) | copy-start | bytes 12582916
  34.0 182.0 %collective-permute-start.1 = (bf16[2,2,512,16,128]{4,2,3,1,0:T(8,128)(2,1)}, bf16[2,2,512,16,128]{4,2,3,1,0:T(8,128)(2,1)}, u32[]{:S(2)}, u32[]{:S(2)}) collective-permute-start(bf16[2,2,512,16,128]{4,2,3,1,0:T(8,128)(2,1)} %pad_maximum_fusion), channel_id=1, source_target_pairs={{0,2},{2,0},{1,3},{3,1},{4,6},{6,4},{5,7},{7,5},{8,10},{10,8},{9,1... | collective-permute-start | bytes 25165832 | tf_op jit(solution)/shard_map/ppermute | solution.py:18
  42.8 1.6 copy-start.3
  44.4 3.6 %copy-start.14 = (bf16[2,4096]{1,0:T(2,128)(2,1)S(1)}, bf16[2,4096]{1,0:T(2,128)(2,1)}, u32[]{:S(2)}) copy-start(bf16[2,4096]{1,0:T(2,128)(2,1)} %param.21) | copy-start | bytes 49156
  44.5 3.6 %copy-start.7 = (bf16[2,2,256,16,128]{4,2,3,1,0:T(8,128)(2,1)S(1)}, bf16[2,2,256,16,128]{4,2,3,1,0:T(8,128)(2,1)}, u32[]{:S(2)}) copy-start(bf16[2,2,256,16,128]{4,2,3,1,0:T(8,128)(2,1)} %copy-done.6) | copy-start | bytes 12582916
  49.4 176.8 %copy-start.2 = (f32[2,16,256,256]{2,3,1,0:T(8,128)}, f32[2,16,256,256]{2,3,1,0:T(8,128)S(1)}, u32[]{:S(2)}) copy-start(f32[2,16,256,256]{2,3,1,0:T(8,128)S(1)} %get-tuple-element.17) | copy-start | bytes 25165828
  257.0 1.2 copy-start.11
  257.0 5.9 %copy-start.8 = (bf16[4,64,4096]{2,1,0:T(8,128)(2,1)S(1)}, bf16[4,64,4096]{2,1,0:T(8,128)(2,1)}, u32[]{:S(2)}) copy-start(bf16[4,64,4096]{2,1,0:T(8,128)(2,1)} %param.19) | copy-start | bytes 6291460
  258.5 5.1 %copy-start.9 = (bf16[128,4096]{1,0:T(8,128)(2,1)S(1)}, bf16[128,4096]{1,0:T(8,128)(2,1)}, u32[]{:S(2)}) copy-start(bf16[128,4096]{1,0:T(8,128)(2,1)} %param.20) | copy-start | bytes 3145732
  258.9 6.2 %copy-start.12 = (bf16[2,256,64]{1,2,0:T(8,128)(2,1)}, bf16[2,256,64]{1,2,0:T(8,128)(2,1)S(1)}, u32[]{:S(2)}) copy-start(bf16[2,256,64]{1,2,0:T(8,128)(2,1)S(1)} %pad_maximum_fusion.2) | copy-start | bytes 196612
  265.1 1.4 copy-start.17
  266.5 2.8 %copy-start.1 = (bf16[2,256,2048]{2,1,0:T(8,128)(2,1)S(1)}, bf16[2,256,2048]{2,1,0:T(8,128)(2,1)}, u32[]{:S(2)}) copy-start(bf16[2,256,2048]{2,1,0:T(8,128)(2,1)} %param.12) | copy-start | bytes 6291460
where the time goes:
time: 270 us; the launch traced here: 269 us
  waiting for transfers between devices  173 us (64%)
  matrix products  42.8 us (16%)
  other arithmetic  22 us (8%)
  local copies, waits for them, and re-layouts  19.2 us (7%)
  between operations  4.87 us (2%)
  blocking collectives  3.78 us (1%)
  starting transfers between devices  3.29 us (1%)
    ppermute x2, waiting for transfers between devices, from_partner(): return lax.ppermute(block, axis, route)  173 us
    dot_general x3, matrix products, absorb(): jnp.einsum('ghqk,gkhd->ghqd', powers.astype(jnp.bfloat16), kv_block[1], p...  22.6 us
    dot_general x3, matrix products, absorb(): jnp.einsum('gqhd,gkhd->ghqk', queries, kv_block[0], preferred_element_typ...  14.5 us
    reduce_sum x3, other arithmetic, absorb(): totals = totals * rescale + jnp.sum(powers, axis=-1)  13.3 us
    another operation x2, local copies, waits for them, and re-layouts, on_device(): jnp.stack((k_inv, v_inv)).reshape(2, local_groups, tok_rows, HEADS, HD)  7.9 us
  transfers between devices with their start and end apart: 2, of which 2 were waited for; matrix products, arithmetic and copies ran while one was open for 4% of the time, Pallas kernels for 0%

commit v1 on v0

v1 whole, which is shorter than its diff:
```python
import math

import jax
import jax.numpy as jnp
from jax import lax
from jax.experimental import pallas as pl
from jax.experimental.pallas import tpu as pltpu
from jax.sharding import PartitionSpec as P

HD = 128
PARTS = 2
STEP_HEADS = 2
TILE = 512
EPS = 1e-06
SCALE = HD ** (-0.5) * math.log2(math.e)


def seq_swap(block, flip):
    count = lax.axis_size("seq")
    return lax.ppermute(block, "seq", [(i, i ^ flip) for i in range(count)])


def grp_swap(block):
    return lax.ppermute(block, "grp", [(0, 1), (1, 0)])


def both_swap(block):
    count = lax.axis_size("seq")
    route = [
        (g * count + i, (1 - g) * count + (i ^ 1)) for g in range(2) for i in range(count)
    ]
    return lax.ppermute(block, ("grp", "seq"), route)


def head_scores(keys, queries, values):
    scores = lax.dot_general(
        keys, queries, (((1,), (1,)), ((), ())), preferred_element_type=jnp.float32
    )
    top = jnp.max(scores, axis=0, keepdims=True)
    powers = jnp.exp2((scores - top) * SCALE).astype(jnp.bfloat16)
    summed = jnp.dot(values, powers, preferred_element_type=jnp.float32)
    return summed, top * SCALE


def local_kernel(ids, q, qx, k, kx, v, vx, w, vw, mean, level):
    step = pl.program_id(0)
    rows = q.shape[0]
    part = rows // PARTS
    for i in range(STEP_HEADS):
        cols = slice(i * HD, (i + 1) * HD)
        keys = jnp.concatenate((k[:, cols], kx[:, cols]), axis=0)
        values = jnp.concatenate((v[:, cols], vx[:, cols]), axis=0)
        read = lax.dot_general(
            w[cols, :], values, (((0,), (1,)), ((), ())), preferred_element_type=jnp.float32
        )
        read = jnp.concatenate(
            (read.astype(jnp.bfloat16), jnp.ones((16, read.shape[1]), jnp.bfloat16)), axis=0
        )
        vw[i] = read
        for j in range(PARTS):
            span = slice(j * part, (j + 1) * part)
            queries = jnp.concatenate((q[span, cols], qx[span, cols]), axis=0)
            summed, top = head_scores(keys, queries, read)
            total = summed[64:65]
            mean[j, i] = summed[:64] * (1.0 / total)
            level[j, pl.ds(step * STEP_HEADS + i, 1), :] = top + jnp.log2(total)


def remote_kernel(ids, qs, qd, k, kx, vw, home, out, acc, share):
    step = pl.program_id(0)

    @pl.when(step == 0)
    def _():
        acc[...] = jnp.zeros_like(acc)

    gathered = acc[...]
    for i in range(STEP_HEADS):
        cols = slice(i * HD, (i + 1) * HD)
        keys = jnp.concatenate((k[:, cols], kx[:, cols]), axis=0)
        queries = jnp.concatenate((qs[:, cols], qd[:, cols]), axis=0)
        summed, top = head_scores(keys, queries, vw[i])
        total = summed[64:65]
        row = pl.ds(step * STEP_HEADS + i, 1)
        mine = 1.0 / (1.0 + jnp.exp2(home[row, :] - (top + jnp.log2(total))))
        mine = mine.astype(jnp.bfloat16).astype(jnp.float32)
        share[row, :] = mine
        gathered = gathered + summed[:64] * (mine / total)
    acc[...] = gathered

    @pl.when(step == pl.num_programs(0) - 1)
    def _():
        out[:64] = acc[...].astype(jnp.bfloat16)
        out[64:] = share[...].astype(jnp.bfloat16)


def merge_kernel(remote, mean, own, other):
    acc = remote[:64].astype(jnp.float32)
    for h in range(mean.shape[0]):
        keep = 1.0 - remote[64 + h : 65 + h].astype(jnp.float32)
        acc = acc + mean[h] * keep
    acc = acc.astype(jnp.bfloat16)
    half = acc.shape[1] // 2
    own[...] = acc[:, :half]
    other[...] = acc[:, half:]


def render_kernel(
    ids, a0, a1, a2, a3, w0, w1, w2, w3, light, w_env, scale, shift, w_final, attrs, rendered, state
):
    lights, rows, width = state.shape
    me = ids[0]
    first = a0[...].astype(jnp.float32).T.astype(jnp.bfloat16)
    second = a1[...].astype(jnp.float32).T.astype(jnp.bfloat16)
    attrs[pl.ds(me, 1)] = first[None]
    attrs[pl.ds(1 - me, 1)] = second[None]
    latents = jnp.concatenate((a0[...], a1[...], a2[...], a3[...]), axis=0)
    latents = latents.astype(jnp.float32).T.astype(jnp.bfloat16)
    sums = [jnp.zeros((rows, 128), jnp.float32) for _ in range(lights)]

    def fold(block):
        total = block[:, :128]
        for s in range(1, block.shape[1] // 128):
            total = total + block[:, s * 128 : (s + 1) * 128]
        return total

    for t in range(width // TILE):
        cols = slice(t * TILE, (t + 1) * TILE)
        weight = jnp.concatenate((w0[:, cols], w1[:, cols], w2[:, cols], w3[:, cols]), axis=0)
        embedded = jnp.dot(latents, weight, preferred_element_type=jnp.float32)
        for l in range(lights):
            block = embedded + jnp.dot(
                light[l], w_env[:, cols], preferred_element_type=jnp.float32
            )
            state[l, :, cols] = block
            sums[l] = sums[l] + fold(block)
    for l in range(lights):
        average = jnp.sum(sums[l], axis=1, keepdims=True) * (1.0 / width)
        square = jnp.zeros((rows, 128), jnp.float32)
        for t in range(width // TILE):
            cols = slice(t * TILE, (t + 1) * TILE)
            centred = state[l, :, cols] - average
            square = square + fold(centred * centred)
        spread = jnp.sum(square, axis=1, keepdims=True) * (1.0 / width)
        invert = lax.rsqrt(spread + EPS)
        acc = jnp.zeros((rows, w_final.shape[1]), jnp.float32)
        for t in range(width // TILE):
            cols = slice(t * TILE, (t + 1) * TILE)
            gain = 1.0 + scale[l : l + 1, cols].astype(jnp.float32)
            bias = shift[l : l + 1, cols].astype(jnp.float32)
            normed = (state[l, :, cols] - average) * invert
            modulated = (normed * gain + bias).astype(jnp.bfloat16)
            acc = acc + jnp.dot(modulated, w_final[cols, :], preferred_element_type=jnp.float32)
        rendered[l] = acc.astype(jnp.bfloat16)


def whole(shape):
    return pl.BlockSpec(shape, lambda *_: (0,) * len(shape))


def on_device(
    q_inv,
    k_inv,
    v_inv,
    group_ids,
    w_attr,
    env_ids,
    env_table,
    w_embed_attr,
    w_embed_env,
    mod_scale,
    mod_shift,
    w_final,
):
    groups, rows, width = q_inv.shape
    heads = width // HD
    part = rows // PARTS
    wide = 2 * part
    patch = w_attr.shape[2]
    me = lax.axis_index("seq") % 2
    grp = lax.axis_index("grp")
    mine = 2 * grp + me
    others = jnp.stack((mine, 2 * grp + 1 - me, 2 * (1 - grp) + me, 2 * (1 - grp) + 1 - me))
    kinds = group_ids[others]
    ids = jnp.concatenate((me[None], kinds)).astype(jnp.int32)

    def pick(array, group, start=0, count=rows):
        return lax.dynamic_slice(array, (group, start, 0), (1, count, width))[0]

    same, cross = [], []
    for j in range(PARTS):
        same.append(seq_swap(pick(q_inv, me, j * part, part), 2))
        cross.append(seq_swap(pick(q_inv, 1 - me, j * part, part), 3))
    kx = seq_swap(pick(k_inv, 1 - me), 1)
    vx = seq_swap(pick(v_inv, 1 - me), 1)
    qx = seq_swap(pick(q_inv, 1 - me), 1)

    cols = STEP_HEADS * HD
    steps = heads // STEP_HEADS
    picked = pl.BlockSpec((None, rows, cols), lambda g, s: (s[0], 0, g))
    plain = pl.BlockSpec((rows, cols), lambda g, s: (0, g))
    vw, mean, level = pl.pallas_call(
        local_kernel,
        grid_spec=pltpu.PrefetchScalarGridSpec(
            num_scalar_prefetch=1,
            grid=(steps,),
            in_specs=[
                picked,
                plain,
                picked,
                plain,
                picked,
                plain,
                pl.BlockSpec((None, cols, patch), lambda g, s: (s[1], g, 0)),
            ],
            out_specs=[
                pl.BlockSpec((STEP_HEADS, 80, 2 * rows), lambda g, s: (g, 0, 0)),
                pl.BlockSpec((PARTS, STEP_HEADS, 64, wide), lambda g, s: (0, g, 0, 0)),
                whole((PARTS, heads, wide)),
            ],
        ),
        out_shape=[
            jax.ShapeDtypeStruct((heads, 80, 2 * rows), jnp.bfloat16),
            jax.ShapeDtypeStruct((PARTS, heads, 64, wide), jnp.float32),
            jax.ShapeDtypeStruct((PARTS, heads, wide), jnp.float32),
        ],
        name="local",
    )(ids, q_inv, qx, k_inv, kx, v_inv, vx, w_attr)
    home = seq_swap(level, 2)
    lighting = jnp.take(env_table, env_ids, axis=0)

    remote = []
    for j in range(PARTS):
        block = pl.BlockSpec((part, cols), lambda g, s: (0, g))
        sent = pl.pallas_call(
            remote_kernel,
            grid_spec=pltpu.PrefetchScalarGridSpec(
                num_scalar_prefetch=1,
                grid=(steps,),
                in_specs=[
                    block,
                    block,
                    picked,
                    plain,
                    pl.BlockSpec((STEP_HEADS, 80, 2 * rows), lambda g, s: (g, 0, 0)),
                    pl.BlockSpec((None, heads, wide), lambda g, s, j=j: (j, 0, 0)),
                ],
                out_specs=whole((64 + heads, wide)),
                scratch_shapes=[
                    pltpu.VMEM((64, wide), jnp.float32),
                    pltpu.VMEM((heads, wide), jnp.float32),
                ],
            ),
            out_shape=jax.ShapeDtypeStruct((64 + heads, wide), jnp.bfloat16),
            name="remote",
        )(ids, same[j], cross[j], k_inv, kx, vw, home)
        remote.append(seq_swap(sent, 2))

    attrs, renders = [], []
    lights = mod_scale.shape[0]
    model = w_final.shape[0]
    channels = w_embed_env.shape[0]
    for j in range(PARTS):
        own, other = pl.pallas_call(
            merge_kernel,
            grid=(1,),
            in_specs=[
                whole((64 + heads, wide)),
                pl.BlockSpec((None, heads, 64, wide), lambda g, j=j: (j, 0, 0, 0)),
            ],
            out_specs=[whole((64, part)), whole((64, part))],
            out_shape=[jax.ShapeDtypeStruct((64, part), jnp.bfloat16)] * 2,
            name="merge",
        )(remote[j], mean)
        a1 = seq_swap(other, 1)
        a2 = grp_swap(own)
        a3 = both_swap(other)
        weights = [
            pl.BlockSpec((None, patch, model), lambda g, s, n=n: (s[1 + n], 0, 0))
            for n in range(4)
        ]
        attr, render = pl.pallas_call(
            render_kernel,
            grid_spec=pltpu.PrefetchScalarGridSpec(
                num_scalar_prefetch=1,
                grid=(1,),
                in_specs=[whole((64, part))] * 4
                + weights
                + [
                    pl.BlockSpec((lights, part, channels), lambda g, s, j=j: (0, j, 0)),
                    whole((channels, model)),
                    whole((lights, model)),
                    whole((lights, model)),
                    whole((model, patch)),
                ],
                out_specs=[whole((groups, part, patch)), whole((lights, part, patch))],
                scratch_shapes=[pltpu.VMEM((lights, part, model), jnp.float32)],
            ),
            out_shape=[
                jax.ShapeDtypeStruct((groups, part, patch), jnp.bfloat16),
                jax.ShapeDtypeStruct((lights, part, patch), jnp.bfloat16),
            ],
            name="render",
        )(
            ids,
            own,
            a1,
            a2,
            a3,
            w_embed_attr,
            w_embed_attr,
            w_embed_attr,
            w_embed_attr,
            lighting,
            w_embed_env,
            mod_scale,
            mod_shift,
            w_final,
        )
        attrs.append(attr)
        renders.append(render)
    return (jnp.concatenate(attrs, axis=1), jnp.concatenate(renders, axis=1))


def solution(mesh):
    in_specs = (
        P("grp", "seq", None),
        P("grp", "seq", None),
        P("grp", "seq", None),
        P(),
        P(),
        P("grp", "seq"),
        P(),
        P(),
        P(),
        P("grp", None),
        P("grp", None),
        P(),
    )
    out_specs = (P("grp", "seq", None), P("grp", "seq", None))
    return jax.shard_map(
        on_device, mesh=mesh, in_specs=in_specs, out_specs=out_specs, check_vma=False
    )
```

time: 270 us -> 113 us (0.42)
  waiting for transfers between devices: 173 us -> 22.2 us
  Pallas kernels: 0 us -> 55.5 us
  matrix products: 42.8 us -> 0 us
  other arithmetic: 22 us -> 2.48 us
  starting transfers between devices: 3.29 us -> 14 us
  between operations: 4.87 us -> 0.89 us
  blocking collectives: 3.78 us -> 0 us
    ppermute x2 -> x16, waiting for transfers between devices: 173 us -> 22.2 us  [the longest x12 22.2 us: seq_swap(): return lax.ppermute(block, 'seq', [(i, i ^ flip) for i in range(count)])]
    pallas_call x0 -> x7, Pallas kernels: none -> 55.5 us  [the longest x2 21.2 us: on_device(): pl.pallas_call(remote_kernel, grid_spec=pltpu.PrefetchScalarGridSpec(num_...]
    dot_general x12 -> x0, matrix products: 42.8 us -> none  [the longest x3 22.6 us: absorb(): jnp.einsum('ghqk,gkhd->ghqd', powers.astype(jnp.bfloat16), kv_block[1], p...]
    reduce_sum x4 -> x0, other arithmetic: 14.6 us -> none  [the longest x3 13.3 us: absorb(): totals = totals * rescale + jnp.sum(powers, axis=-1)]
    ppermute x2 -> x16, starting transfers between devices: 3.29 us -> 14 us  [the longest x12 10.8 us: seq_swap(): return lax.ppermute(block, 'seq', [(i, i ^ flip) for i in range(count)])]
    another operation x2 -> x0, local copies, waits for them, and re-layouts: 7.9 us -> none  [on_device(): jnp.stack((k_inv, v_inv)).reshape(2, local_groups, tok_rows, HEADS, HD)]
    unnamed x38 -> x49, local copies, waits for them, and re-layouts: 5.02 us -> 9.78 us
    all_gather x1 -> x0, blocking collectives: 3.78 us -> none  [on_device(): everything = lax.all_gather(attributes, 'grp', axis=0, tiled=True)]
  transfers between devices with their start and end apart: 2 -> 16, of which waited for: 2 -> 1; matrix products, arithmetic and copies ran while one was open for 4% -> 10% of each run, Pallas kernels for 0% -> 44%
where the time goes in v1:
time: 113 us
  Pallas kernels  55.5 us (49%)
  waiting for transfers between devices  22.2 us (20%)
  local copies, waits for them, and re-layouts  17.7 us (16%)
  starting transfers between devices  14 us (12%)
  other arithmetic  2.48 us (2%)
    ppermute x12, waiting for transfers between devices, seq_swap(): return lax.ppermute(block, 'seq', [(i, i ^ flip) for i in range(count)])  22.2 us
    pallas_call x2, Pallas kernels, on_device(): pl.pallas_call(remote_kernel, grid_spec=pltpu.PrefetchScalarGridSpec(num_...  21.2 us
    pallas_call x1, Pallas kernels, on_device(): pl.pallas_call(local_kernel, grid_spec=pltpu.PrefetchScalarGridSpec(num_s...  17.7 us
    pallas_call x2, Pallas kernels, on_device(): pl.pallas_call(render_kernel, grid_spec=pltpu.PrefetchScalarGridSpec(num_...  12.7 us
    ppermute x12, starting transfers between devices, seq_swap(): return lax.ppermute(block, 'seq', [(i, i ^ flip) for i in range(count)])  10.8 us
    unnamed x49, local copies, waits for them, and re-layouts  9.78 us
    squeeze x4, local copies, waits for them, and re-layouts, pick(): return lax.dynamic_slice(array, (group, start, 0), (1, count, width))[0]  5.98 us
    pallas_call x2, Pallas kernels, on_device(): pl.pallas_call(merge_kernel, grid=(1,), in_specs=[whole((64 + heads, wide...  3.87 us
  transfers between devices with their start and end apart: 16, of which 1 were waited for; matrix products, arithmetic and copies ran while one was open for 10% of the time, Pallas kernels for 44%

profile of v1, /device:TPU:1, one launch (start us, length us, event | category | flops | bytes accessed | tf_op | source)
XLA Modules:
  0.0 112.7 jit_solution(11395128582220884127)
XLA Ops:
  0.7 2.5 %dynamic-slice_bitcast_fusion.2 = bf16[256,2048]{1,0:T(8,128)(2,1)} fusion(bf16[2,256,2048]{2,1,0:T(8,128)(2,1)} %k.5, s32[]{:T(128)S(6)} %select_n.40), kind=kLoop, calls=%fused_computation.4 | loop fusion | bytes 2097156 | tf_op jit(solution)/shard_map/squeeze | solution.py:187
  3.2 3.2 %collective-permute-start.2 = (bf16[256,2048]{1,0:T(8,128)(2,1)}, bf16[256,2048]{1,0:T(8,128)(2,1)}, u32[]{:S(2)}, u32[]{:S(2)}) collective-permute-start(bf16[256,2048]{1,0:T(8,128)(2,1)} %dynamic-slice_bitcast_fusion.2), channel_id=1, source_target_pairs={{0,1},{1,0},{2,3},{3,2},{4,5},{5,4},{6,7},{7,6},{8,9},{9,8},{10,11... | collective-permute-start | bytes 3145736 | tf_op jit(solution)/shard_map/ppermute | solution.py:20
  6.4 1.1 dynamic-slice_bitcast_fusion.1
  7.4 1.1 dynamic-slice_bitcast_fusion
  9.0 1.4 %dynamic-slice_bitcast_fusion.5 = (bf16[128,2048]{1,0:T(8,128)(2,1)}, bf16[128,2048]{1,0:T(8,128)(2,1)}, bf16[128,2048]{1,0:T(8,128)(2,1)}, bf16[128,2048]{1,0:T(8,128)(2,1)}) fusion(bf16[2,256,2048]{2,1,0:T(8,128)(2,1)S(1)} %copy-done.2, s32[]{:T(128)S(6)} %select_n.40, s32[]{:T(128)S(6)} %select_n.39), kind=kLoop, calls=%fused_computation.7 | loop fusion | bytes 4194312 | tf_op jit(solution)/shard_map/squeeze | solution.py:187
  10.4 1.6 %collective-permute-start.1 = (bf16[128,2048]{1,0:T(8,128)(2,1)}, bf16[128,2048]{1,0:T(8,128)(2,1)S(1)}, u32[]{:S(2)}, u32[]{:S(2)}) collective-permute-start(bf16[128,2048]{1,0:T(8,128)(2,1)} %get-tuple-element.28), channel_id=1, source_target_pairs={{0,3},{1,2},{2,1},{3,0},{4,7},{5,6},{6,5},{7,4},{8,11},{9,10},{10,... | collective-permute-start | bytes 1572872 | tf_op jit(solution)/shard_map/ppermute | solution.py:20
  12.1 2.7 %copy.19.w = bf16[4,2048,64]{2,1,0:T(8,128)(2,1)} copy(bf16[4,2048,64]{1,2,0:T(8,128)(2,1)} %param.16) | data formatting | bytes 2097152 | tf_op args[4]
  14.9 0.6 gather_fusion
  15.6 1.8 %collective-permute-start.11 = (bf16[128,2048]{1,0:T(8,128)(2,1)S(1)}, bf16[128,2048]{1,0:T(8,128)(2,1)}, u32[]{:S(2)}, u32[]{:S(2)}) collective-permute-start(bf16[128,2048]{1,0:T(8,128)(2,1)S(1)} %copy-done.5), channel_id=1, source_target_pairs={{0,3},{1,2},{2,1},{3,0},{4,7},{5,6},{6,5},{7,4},{8,11},{9,10},{10,... | collective-permute-start | bytes 1572872 | tf_op jit(solution)/shard_map/ppermute | solution.py:20
  17.5 0.7 pad_add_fusion.ids
  18.1 17.7 %local.1 = (bf16[16,80,512]{2,1,0:T(8,128)(2,1)}, f32[2,16,64,256]{3,2,1,0:T(8,128)}, f32[2,16,256]{2,1,0:T(8,128)}) custom-call(s32[5]{0:T(128)} %pad_add_fusion.ids, bf16[2,256,2048]{2,1,0:T(8,128)(2,1)} %q.1, bf16[256,2048]{1,0:T(8,128)(2,1)} %collective-permute-done.3.qx, bf16[2,256,2048]{2,1,0:T(8,128)(2,1)} %k.5, ...), custom_call_target="tpu_custom_call" | custom-call | tf_op jit(solution)/shard_map/local/pallas_call | solution.py:201
  36.1 22.2 %collective-permute-done.5.home = f32[2,16,256]{2,1,0:T(8,128)S(1)} collective-permute-done((f32[2,16,256]{2,1,0:T(8,128)}, f32[2,16,256]{2,1,0:T(8,128)S(1)}, u32[]{:S(2)}, u32[]{:S(2)}) %collective-permute-start.5) | collective-permute-done | bytes 32800 | tf_op jit(solution)/shard_map/ppermute | solution.py:20
  58.2 0.6 copy-done.9
  58.8 10.6 %remote.2 = bf16[80,256]{1,0:T(8,128)(2,1)} custom-call(s32[5]{0:T(128)} %pad_add_fusion.ids, bf16[128,2048]{1,0:T(8,128)(2,1)} %copy-done.7, bf16[128,2048]{1,0:T(8,128)(2,1)} %copy-done.8, bf16[2,256,2048]{2,1,0:T(8,128)(2,1)} %k.5, bf16[256,2048]{1,0:T(8,128)(2,1)} %collective-permute-done.2.kx, bf16[16,80,512]{2,1,0:T(8,128)(2,1)} %get-tuple-element.13.vw, ...), custom_call_target="tpu_custom_call" | custom-call | tf_op jit(solution)/shard_map/remote/pallas_call | solution.py:234
  69.5 10.6 %remote.3 = bf16[80,256]{1,0:T(8,128)(2,1)} custom-call(s32[5]{0:T(128)} %pad_add_fusion.ids, bf16[128,2048]{1,0:T(8,128)(2,1)} %collective-permute-done.10.qs, bf16[128,2048]{1,0:T(8,128)(2,1)} %collective-permute-done.11.qd, bf16[2,256,2048]{2,1,0:T(8,128)(2,1)} %k.5, bf16[256,2048]{1,0:T(8,128)(2,1)} %collective-permute-done.2.kx, ...), custom_call_target="tpu_custom_call" | custom-call | tf_op jit(solution)/shard_map/remote/pallas_call | solution.py:234
  80.2 1.4 %collective-permute-start.12 = (bf16[80,256]{1,0:T(8,128)(2,1)}, bf16[80,256]{1,0:T(8,128)(2,1)S(1)}, u32[]{:S(2)}, u32[]{:S(2)}) collective-permute-start(bf16[80,256]{1,0:T(8,128)(2,1)} %remote.3), channel_id=1, source_target_pairs={{0,2},{1,3},{2,0},{3,1},{4,6},{5,7},{6,4},{7,5},{8,10},{9,11},{10,... | collective-permute-start | bytes 122888 | tf_op jit(solution)/shard_map/ppermute | solution.py:20
  81.5 0.6 copy-done.12
  82.2 1.9 %merge.2 = (bf16[64,128]{1,0:T(8,128)(2,1)}, bf16[64,128]{1,0:T(8,128)(2,1)}) custom-call(bf16[80,256]{1,0:T(8,128)(2,1)} %copy-done.12, f32[2,16,64,256]{3,2,1,0:T(8,128)} %get-tuple-element.15.mean), custom_call_target="tpu_custom_call" | custom-call | tf_op jit(solution)/shard_map/merge/pallas_call | solution.py:263
  84.1 1.7 %collective-permute-start.7 = (bf16[64,128]{1,0:T(8,128)(2,1)}, bf16[64,128]{1,0:T(8,128)(2,1)S(1)}, u32[]{:S(2)}, u32[]{:S(2)}) collective-permute-start(bf16[64,128]{1,0:T(8,128)(2,1)} %get-tuple-element.17), channel_id=1, source_target_pairs={{0,1},{1,0},{2,3},{3,2},{4,5},{5,4},{6,7},{7,6},{8,9},{9,8},{10,11... | collective-permute-start | bytes 49160 | tf_op jit(solution)/shard_map/ppermute | solution.py:20
  85.8 1.3 %gather_fusion.1 = bf16[512,128]{1,0:T(8,128)(2,1)S(1)} fusion(bf16[4096,128]{1,0:T(8,128)(2,1)S(1)} %copy-done, s32[1024]{0:T(1024)S(1)} %pad_clamp_fusion), kind=kCustom, calls=%fused_computation.1 | custom fusion | bytes 264192 | tf_op jit(solution)/shard_map/jit(_take)/gather | solution.py:229
  87.3 0.6 copy-done.13
  87.9 1.9 %merge.3 = (bf16[64,128]{1,0:T(8,128)(2,1)}, bf16[64,128]{1,0:T(8,128)(2,1)}) custom-call(bf16[80,256]{1,0:T(8,128)(2,1)} %copy-done.13, f32[2,16,64,256]{3,2,1,0:T(8,128)} %get-tuple-element.15.mean), custom_call_target="tpu_custom_call" | custom-call | tf_op jit(solution)/shard_map/merge/pallas_call | solution.py:263
  90.0 1.6 %collective-permute-start.15 = (bf16[64,128]{1,0:T(8,128)(2,1)}, bf16[64,128]{1,0:T(8,128)(2,1)S(1)}, u32[]{:S(2)}, u32[]{:S(2)}) collective-permute-start(bf16[64,128]{1,0:T(8,128)(2,1)} %get-tuple-element.20), channel_id=1, source_target_pairs={{0,129},{1,128},{2,131},{3,130},{4,133},{5,132},{6,135},{7,134},{8... | collective-permute-start | bytes 49160 | tf_op jit(solution)/shard_map/ppermute | solution.py:32
  91.7 1.3 %collective-permute-start.14 = (bf16[64,128]{1,0:T(8,128)(2,1)}, bf16[64,128]{1,0:T(8,128)(2,1)S(1)}, u32[]{:S(2)}, u32[]{:S(2)}) collective-permute-start(bf16[64,128]{1,0:T(8,128)(2,1)} %get-tuple-element.19.a0), channel_id=1, source_target_pairs={{0,128},{128,0},{1,129},{129,1},{2,130},{130,2},{3,131},{131,3},{4... | collective-permute-start | bytes 49160 | tf_op jit(solution)/shard_map/ppermute | solution.py:24
  93.1 0.8 broadcast_select_fusion.light
  93.9 1.3 %copy.20.w_final = bf16[4096,64]{1,0:T(8,128)(2,1)} copy(bf16[4096,64]{0,1:T(8,128)(2,1)S(1)} %copy-done.4) | data formatting | bytes 1048576 | tf_op args[11]
  96.4 6.4 %render.2 = (bf16[2,128,64]{2,1,0:T(8,128)(2,1)}, bf16[2,128,64]{2,1,0:T(8,128)(2,1)}) custom-call(s32[5]{0:T(128)} %pad_add_fusion.ids, bf16[64,128]{1,0:T(8,128)(2,1)} %get-tuple-element.16.a0, bf16[64,128]{1,0:T(8,128)(2,1)} %copy-done.15, bf16[64,128]{1,0:T(8,128)(2,1)} %copy-done.20, bf16[64,128]{1,0:T(8,128)(2,1)} %copy-done.18, ...), custom_call_target="tpu_custom_call" | custom-call | tf_op jit(solution)/shard_map/render/pallas_call | solution.py:281
  103.4 0.6 copy-done.17
  104.0 6.3 %render.3 = (bf16[2,128,64]{2,1,0:T(8,128)(2,1)}, bf16[2,128,64]{2,1,0:T(8,128)(2,1)}) custom-call(s32[5]{0:T(128)} %pad_add_fusion.ids, bf16[64,128]{1,0:T(8,128)(2,1)} %get-tuple-element.19.a0, bf16[64,128]{1,0:T(8,128)(2,1)} %copy-done.16, bf16[64,128]{1,0:T(8,128)(2,1)} %copy-done.19, bf16[64,128]{1,0:T(8,128)(2,1)} %copy-done.17, ...), custom_call_target="tpu_custom_call" | custom-call | tf_op jit(solution)/shard_map/render/pallas_call | solution.py:281
  110.3 0.9 pad_maximum_fusion
  111.3 0.7 copy.22
  112.0 0.7 copy.23
  (70 shorter events, 3.2 us)
Async XLA Ops:
  0.6 85.2 %copy-start = (bf16[4096,128]{1,0:T(8,128)(2,1)S(1)}, bf16[4096,128]{1,0:T(8,128)(2,1)}, u32[]{:S(2)}) copy-start(bf16[4096,128]{1,0:T(8,128)(2,1)} %param.18) | copy-start | bytes 3145732
  0.6 5.7 %copy-start.2 = (bf16[2,256,2048]{2,1,0:T(8,128)(2,1)S(1)}, bf16[2,256,2048]{2,1,0:T(8,128)(2,1)}, u32[]{:S(2)}) copy-start(bf16[2,256,2048]{2,1,0:T(8,128)(2,1)} %q.1) | copy-start | bytes 6291460
  0.7 6.8 %copy-start.3 = (bf16[2,256,2048]{2,1,0:T(8,128)(2,1)S(1)}, bf16[2,256,2048]{2,1,0:T(8,128)(2,1)}, u32[]{:S(2)}) copy-start(bf16[2,256,2048]{2,1,0:T(8,128)(2,1)} %v.1) | copy-start | bytes 6291460
  3.2 12.4 %collective-permute-start.2 = (bf16[256,2048]{1,0:T(8,128)(2,1)}, bf16[256,2048]{1,0:T(8,128)(2,1)}, u32[]{:S(2)}, u32[]{:S(2)}) collective-permute-start(bf16[256,2048]{1,0:T(8,128)(2,1)} %dynamic-slice_bitcast_fusion.2), channel_id=1, source_target_pairs={{0,1},{1,0},{2,3},{3,2},{4,5},{5,4},{6,7},{7,6},{8,9},{9,8},{10,11... | collective-permute-start | bytes 3145736 | tf_op jit(solution)/shard_map/ppermute | solution.py:20
  7.4 8.2 %collective-permute-start.3 = (bf16[256,2048]{1,0:T(8,128)(2,1)}, bf16[256,2048]{1,0:T(8,128)(2,1)}, u32[]{:S(2)}, u32[]{:S(2)}) collective-permute-start(bf16[256,2048]{1,0:T(8,128)(2,1)} %dynamic-slice_bitcast_fusion.1), channel_id=1, source_target_pairs={{0,1},{1,0},{2,3},{3,2},{4,5},{5,4},{6,7},{7,6},{8,9},{9,8},{10,11... | collective-permute-start | bytes 3145736 | tf_op jit(solution)/shard_map/ppermute | solution.py:20
  8.5 9.6 %collective-permute-start.4 = (bf16[256,2048]{1,0:T(8,128)(2,1)}, bf16[256,2048]{1,0:T(8,128)(2,1)}, u32[]{:S(2)}, u32[]{:S(2)}) collective-permute-start(bf16[256,2048]{1,0:T(8,128)(2,1)} %dynamic-slice_bitcast_fusion), channel_id=1, source_target_pairs={{0,1},{1,0},{2,3},{3,2},{4,5},{5,4},{6,7},{7,6},{8,9},{9,8},{10,11... | collective-permute-start | bytes 3145736 | tf_op jit(solution)/shard_map/ppermute | solution.py:20
  10.4 4.5 %copy-start.1 = (s32[4]{0:T(128)S(1)}, s32[4]{0:T(128)}, u32[]{:S(2)}) copy-start(s32[4]{0:T(128)} %param.15) | copy-start | bytes 52
  10.4 5.1 %copy-start.6 = (bf16[128,2048]{1,0:T(8,128)(2,1)S(1)}, bf16[128,2048]{1,0:T(8,128)(2,1)}, u32[]{:S(2)}) copy-start(bf16[128,2048]{1,0:T(8,128)(2,1)} %get-tuple-element.31) | copy-start | bytes 1572868
  10.4 5.2 %copy-start.5 = (bf16[128,2048]{1,0:T(8,128)(2,1)S(1)}, bf16[128,2048]{1,0:T(8,128)(2,1)}, u32[]{:S(2)}) copy-start(bf16[128,2048]{1,0:T(8,128)(2,1)} %get-tuple-element.30) | copy-start | bytes 1572868
  10.4 25.6 %collective-permute-start = (bf16[128,2048]{1,0:T(8,128)(2,1)}, bf16[128,2048]{1,0:T(8,128)(2,1)S(1)}, u32[]{:S(2)}, u32[]{:S(2)}) collective-permute-start(bf16[128,2048]{1,0:T(8,128)(2,1)} %get-tuple-element.29), channel_id=1, source_target_pairs={{0,2},{1,3},{2,0},{3,1},{4,6},{5,7},{6,4},{7,5},{8,10},{9,11},{10,... | collective-permute-start | bytes 1572872 | tf_op jit(solution)/shard_map/ppermute | solution.py:20
  10.4 25.6 %collective-permute-start.1 = (bf16[128,2048]{1,0:T(8,128)(2,1)}, bf16[128,2048]{1,0:T(8,128)(2,1)S(1)}, u32[]{:S(2)}, u32[]{:S(2)}) collective-permute-start(bf16[128,2048]{1,0:T(8,128)(2,1)} %get-tuple-element.28), channel_id=1, source_target_pairs={{0,3},{1,2},{2,1},{3,0},{4,7},{5,6},{6,5},{7,4},{8,11},{9,10},{10,... | collective-permute-start | bytes 1572872 | tf_op jit(solution)/shard_map/ppermute | solution.py:20
  15.5 54.0 %collective-permute-start.10 = (bf16[128,2048]{1,0:T(8,128)(2,1)S(1)}, bf16[128,2048]{1,0:T(8,128)(2,1)}, u32[]{:S(2)}, u32[]{:S(2)}) collective-permute-start(bf16[128,2048]{1,0:T(8,128)(2,1)S(1)} %copy-done.6), channel_id=1, source_target_pairs={{0,2},{1,3},{2,0},{3,1},{4,6},{5,7},{6,4},{7,5},{8,10},{9,11},{10,... | collective-permute-start | bytes 1572872 | tf_op jit(solution)/shard_map/ppermute | solution.py:20
  15.6 53.9 %collective-permute-start.11 = (bf16[128,2048]{1,0:T(8,128)(2,1)S(1)}, bf16[128,2048]{1,0:T(8,128)(2,1)}, u32[]{:S(2)}, u32[]{:S(2)}) collective-permute-start(bf16[128,2048]{1,0:T(8,128)(2,1)S(1)} %copy-done.5), channel_id=1, source_target_pairs={{0,3},{1,2},{2,1},{3,0},{4,7},{5,6},{6,5},{7,4},{8,11},{9,10},{10,... | collective-permute-start | bytes 1572872 | tf_op jit(solution)/shard_map/ppermute | solution.py:20
  18.1 17.9 %copy-start.21 = (s32[2,256]{1,0:T(2,128)S(1)}, s32[2,256]{1,0:T(2,128)}, u32[]{:S(2)}) copy-start(s32[2,256]{1,0:T(2,128)} %param.17) | copy-start | bytes 6148
  35.8 22.4 %collective-permute-start.5 = (f32[2,16,256]{2,1,0:T(8,128)}, f32[2,16,256]{2,1,0:T(8,128)S(1)}, u32[]{:S(2)}, u32[]{:S(2)}) collective-permute-start(f32[2,16,256]{2,1,0:T(8,128)} %get-tuple-element.14), channel_id=1, source_target_pairs={{0,2},{1,3},{2,0},{3,1},{4,6},{5,7},{6,4},{7,5},{8,10},{9,11},{10,... | collective-permute-start | bytes 98312 | tf_op jit(solution)/shard_map/ppermute | solution.py:20
  36.0 22.2 %copy-start.7 = (bf16[128,2048]{1,0:T(8,128)(2,1)}, bf16[128,2048]{1,0:T(8,128)(2,1)S(1)}, u32[]{:S(2)}) copy-start(bf16[128,2048]{1,0:T(8,128)(2,1)S(1)} %collective-permute-done.qs) | copy-start | bytes 1572868
  36.1 22.2 %copy-start.8 = (bf16[128,2048]{1,0:T(8,128)(2,1)}, bf16[128,2048]{1,0:T(8,128)(2,1)S(1)}, u32[]{:S(2)}) copy-start(bf16[128,2048]{1,0:T(8,128)(2,1)S(1)} %collective-permute-done.1.qd) | copy-start | bytes 1572868
  69.4 12.1 %collective-permute-start.6 = (bf16[80,256]{1,0:T(8,128)(2,1)}, bf16[80,256]{1,0:T(8,128)(2,1)S(1)}, u32[]{:S(2)}, u32[]{:S(2)}) collective-permute-start(bf16[80,256]{1,0:T(8,128)(2,1)} %remote.2), channel_id=1, source_target_pairs={{0,2},{1,3},{2,0},{3,1},{4,6},{5,7},{6,4},{7,5},{8,10},{9,11},{10,... | collective-permute-start | bytes 122888 | tf_op jit(solution)/shard_map/ppermute | solution.py:20
  80.2 7.1 %collective-permute-start.12 = (bf16[80,256]{1,0:T(8,128)(2,1)}, bf16[80,256]{1,0:T(8,128)(2,1)S(1)}, u32[]{:S(2)}, u32[]{:S(2)}) collective-permute-start(bf16[80,256]{1,0:T(8,128)(2,1)} %remote.3), channel_id=1, source_target_pairs={{0,2},{1,3},{2,0},{3,1},{4,6},{5,7},{6,4},{7,5},{8,10},{9,11},{10,... | collective-permute-start | bytes 122888 | tf_op jit(solution)/shard_map/ppermute | solution.py:20
  81.5 0.6 copy-start.12
  84.1 7.5 %copy-start.14 = (bf16[64,128]{1,0:T(8,128)(2,1)S(1)}, bf16[64,128]{1,0:T(8,128)(2,1)}, u32[]{:S(2)}) copy-start(bf16[64,128]{1,0:T(8,128)(2,1)} %get-tuple-element.16.a0) | copy-start | bytes 49156
  84.1 9.8 %copy-start.4 = (bf16[4096,64]{0,1:T(8,128)(2,1)S(1)}, bf16[4096,64]{0,1:T(8,128)(2,1)}, u32[]{:S(2)}) copy-start(bf16[4096,64]{0,1:T(8,128)(2,1)} %param.23) | copy-start | bytes 1572868
  84.1 7.6 %collective-permute-start.7 = (bf16[64,128]{1,0:T(8,128)(2,1)}, bf16[64,128]{1,0:T(8,128)(2,1)S(1)}, u32[]{:S(2)}, u32[]{:S(2)}) collective-permute-start(bf16[64,128]{1,0:T(8,128)(2,1)} %get-tuple-element.17), channel_id=1, source_target_pairs={{0,1},{1,0},{2,3},{3,2},{4,5},{5,4},{6,7},{7,6},{8,9},{9,8},{10,11... | collective-permute-start | bytes 49160 | tf_op jit(solution)/shard_map/ppermute | solution.py:20
  87.2 8.0 %collective-permute-start.9 = (bf16[64,128]{1,0:T(8,128)(2,1)}, bf16[64,128]{1,0:T(8,128)(2,1)S(1)}, u32[]{:S(2)}, u32[]{:S(2)}) collective-permute-start(bf16[64,128]{1,0:T(8,128)(2,1)} %get-tuple-element.17), channel_id=1, source_target_pairs={{0,129},{1,128},{2,131},{3,130},{4,133},{5,132},{6,135},{7,134},{8... | collective-permute-start | bytes 49160 | tf_op jit(solution)/shard_map/ppermute | solution.py:32
  87.3 0.6 copy-start.13
  89.9 12.9 %collective-permute-start.13 = (bf16[64,128]{1,0:T(8,128)(2,1)}, bf16[64,128]{1,0:T(8,128)(2,1)S(1)}, u32[]{:S(2)}, u32[]{:S(2)}) collective-permute-start(bf16[64,128]{1,0:T(8,128)(2,1)} %get-tuple-element.20), channel_id=1, source_target_pairs={{0,1},{1,0},{2,3},{3,2},{4,5},{5,4},{6,7},{7,6},{8,9},{9,8},{10,11... | collective-permute-start | bytes 49160 | tf_op jit(solution)/shard_map/ppermute | solution.py:20
  90.0 12.8 %collective-permute-start.15 = (bf16[64,128]{1,0:T(8,128)(2,1)}, bf16[64,128]{1,0:T(8,128)(2,1)S(1)}, u32[]{:S(2)}, u32[]{:S(2)}) collective-permute-start(bf16[64,128]{1,0:T(8,128)(2,1)} %get-tuple-element.20), channel_id=1, source_target_pairs={{0,129},{1,128},{2,131},{3,130},{4,133},{5,132},{6,135},{7,134},{8... | collective-permute-start | bytes 49160 | tf_op jit(solution)/shard_map/ppermute | solution.py:32
  91.6 3.6 %collective-permute-start.8 = (bf16[64,128]{1,0:T(8,128)(2,1)S(1)}, bf16[64,128]{1,0:T(8,128)(2,1)S(1)}, u32[]{:S(2)}, u32[]{:S(2)}) collective-permute-start(bf16[64,128]{1,0:T(8,128)(2,1)S(1)} %copy-done.14), channel_id=1, source_target_pairs={{0,128},{128,0},{1,129},{129,1},{2,130},{130,2},{3,131},{131,3},{4... | collective-permute-start | bytes 49160 | tf_op jit(solution)/shard_map/ppermute | solution.py:24
  91.7 3.5 %copy-start.15 = (bf16[64,128]{1,0:T(8,128)(2,1)}, bf16[64,128]{1,0:T(8,128)(2,1)S(1)}, u32[]{:S(2)}) copy-start(bf16[64,128]{1,0:T(8,128)(2,1)S(1)} %collective-permute-done.7.a1) | copy-start | bytes 49156
  91.7 11.1 %collective-permute-start.14 = (bf16[64,128]{1,0:T(8,128)(2,1)}, bf16[64,128]{1,0:T(8,128)(2,1)S(1)}, u32[]{:S(2)}, u32[]{:S(2)}) collective-permute-start(bf16[64,128]{1,0:T(8,128)(2,1)} %get-tuple-element.19.a0), channel_id=1, source_target_pairs={{0,128},{128,0},{1,129},{129,1},{2,130},{130,2},{3,131},{131,3},{4... | collective-permute-start | bytes 49160 | tf_op jit(solution)/shard_map/ppermute | solution.py:24
  102.7 7.6 %copy-start.10 = (bf16[2,128,64]{2,1,0:T(8,128)(2,1)S(1)}, bf16[2,128,64]{2,1,0:T(8,128)(2,1)}, u32[]{:S(2)}) copy-start(bf16[2,128,64]{2,1,0:T(8,128)(2,1)} %get-tuple-element.18) | copy-start | bytes 98308
  102.7 7.6 %copy-start.11 = (bf16[2,128,64]{2,1,0:T(8,128)(2,1)S(1)}, bf16[2,128,64]{2,1,0:T(8,128)(2,1)}, u32[]{:S(2)}) copy-start(bf16[2,128,64]{2,1,0:T(8,128)(2,1)} %get-tuple-element.22) | copy-start | bytes 98308
  (6 other events, 3.6 us)

commit v2 on v1

v2 whole, which is shorter than its diff:
```python
import math

import jax
import jax.numpy as jnp
from jax import lax
from jax.experimental import pallas as pl
from jax.experimental.pallas import tpu as pltpu
from jax.sharding import PartitionSpec as P


HD = 128
STEP_HEADS = 4
EPS = 1e-06
SCALE = HD ** (-0.5) * math.log2(math.e)
SAFE = 60.0
CHUNK = 1024
OVER_LANES = (((1,), (1,)), ((), ()))


def seq_swap(block, flip):
    count = lax.axis_size("seq")
    return lax.ppermute(block, "seq", [(i, i ^ flip) for i in range(count)])


def grp_swap(block):
    return lax.ppermute(block, "grp", [(0, 1), (1, 0)])


def both_swap(block):
    count = lax.axis_size("seq")
    route = [
        (g * count + i, (1 - g) * count + (i ^ 1)) for g in range(2) for i in range(count)
    ]
    return lax.ppermute(block, ("grp", "seq"), route)


def dot_lanes(left, right):
    return lax.dot_general(left, right, OVER_LANES, preferred_element_type=jnp.float32)


def split(block):
    high = block.astype(jnp.bfloat16)
    return high, (block - high.astype(jnp.float32)).astype(jnp.bfloat16)


def dot_split(left, right):
    high, low = split(left)
    return dot_lanes(high, right) + dot_lanes(low, right)


def plain_softmax(keys, queries, values):
    powers = jnp.exp2(dot_lanes(keys, queries) * SCALE).astype(jnp.bfloat16)
    summed = jnp.dot(values, powers, preferred_element_type=jnp.float32)
    total = summed[64:65]
    return summed[:64], total, jnp.log2(total)


def shifted_softmax(keys, queries, values):
    scores = dot_lanes(keys, queries)
    top = jnp.max(scores, axis=0, keepdims=True)
    powers = jnp.exp2((scores - top) * SCALE).astype(jnp.bfloat16)
    summed = jnp.dot(values, powers, preferred_element_type=jnp.float32)
    total = summed[64:65]
    return summed[:64], total, top * SCALE + jnp.log2(total)


def worst(levels):
    largest = jnp.abs(levels[0])
    for level in levels[1:]:
        largest = jnp.maximum(largest, jnp.abs(level))
    return jnp.max(largest)


def local_kernel(ids, q, qx, k, kx, v, vx, w, vw, mean, level):
    step = pl.program_id(0)

    for i in range(STEP_HEADS):
        cols = slice(i * HD, (i + 1) * HD)
        values = jnp.concatenate((v[:, cols], vx[:, cols]), axis=0)
        read = dot_lanes(w[:, cols], values).astype(jnp.bfloat16)
        vw[i, :64] = read
        vw[i, 64:] = jnp.ones((16, read.shape[1]), jnp.bfloat16)

    def attend(softmax):
        levels = []
        for i in range(STEP_HEADS):
            cols = slice(i * HD, (i + 1) * HD)
            keys = jnp.concatenate((k[:, cols], kx[:, cols]), axis=0)
            rows = []
            for lanes, spans in ((0, ((0, 128),)), (256, ((128, 192), (192, 256)))):
                pieces = []
                for a, b in spans:
                    pieces += [q[a:b, cols], qx[a:b, cols]]
                summed, total, row = softmax(keys, jnp.concatenate(pieces, axis=0), vw[i])
                mean[i, :, lanes : lanes + 256] = summed * (1.0 / total)
                rows.append(row)
            row = jnp.concatenate(rows, axis=1)
            level[pl.ds(step * STEP_HEADS + i, 1), :] = row
            levels.append(row)
        return worst(levels)

    reach = attend(plain_softmax)

    @pl.when(jnp.logical_not(reach < SAFE))
    def _():
        attend(shifted_softmax)


def remote_kernel(spans, ids, qs, qd, k, kx, vw, home, out, acc, share):
    step = pl.program_id(0)

    @pl.when(step == 0)
    def _():
        acc[...] = jnp.zeros_like(acc)

    before = acc[...]

    def attend(softmax):
        gathered = [before[:, a * 2 : b * 2] for a, b in spans]
        levels = []
        for i in range(STEP_HEADS):
            cols = slice(i * HD, (i + 1) * HD)
            keys = jnp.concatenate((k[:, cols], kx[:, cols]), axis=0)
            row = pl.ds(step * STEP_HEADS + i, 1)
            theirs = home[row, :]
            rows, mines = [], []
            for n, (a, b) in enumerate(spans):
                queries = jnp.concatenate((qs[a:b, cols], qd[a:b, cols]), axis=0)
                summed, total, level = softmax(keys, queries, vw[i])
                mine = 1.0 / (1.0 + jnp.exp2(theirs[:, 2 * a : 2 * b] - level))
                mine = mine.astype(jnp.bfloat16).astype(jnp.float32)
                gathered[n] = gathered[n] + summed * (mine / total)
                mines.append(mine)
                rows.append(level)
            share[row, :] = jnp.concatenate(mines, axis=1)
            levels.append(jnp.concatenate(rows, axis=1))
        for n, (a, b) in enumerate(spans):
            acc[:, 2 * a : 2 * b] = gathered[n]
        return worst(levels)

    reach = attend(plain_softmax)

    @pl.when(jnp.logical_not(reach < SAFE))
    def _():
        attend(shifted_softmax)

    @pl.when(step == pl.num_programs(0) - 1)
    def _():
        out[:64] = acc[...].astype(jnp.bfloat16)
        out[64:] = share[...].astype(jnp.bfloat16)


def blend(remote, mean, start):
    acc = remote[:64].astype(jnp.float32)
    for h in range(mean.shape[0]):
        keep = 1.0 - remote[64 + h : 65 + h].astype(jnp.float32)
        acc = acc + mean[h, :, start : start + acc.shape[1]] * keep
    return acc


def early_kernel(remote, mean, out):
    out[...] = blend(remote, mean, 0)


def merge_kernel(remote, mean, early, own, other):
    late = blend(remote, mean, early.shape[1])
    mixed = early[:, 256:]
    first = lax.broadcasted_iota(jnp.int32, late.shape, 1) < 64
    own[:, :128] = early[:, :128].astype(jnp.bfloat16)
    other[:, :128] = early[:, 128:256].astype(jnp.bfloat16)
    own[:, 128:] = jnp.where(first, mixed, pltpu.roll(late, 64, 1)).astype(jnp.bfloat16)
    other[:, 128:] = jnp.where(first, pltpu.roll(mixed, 64, 1), late).astype(jnp.bfloat16)


def prepare_kernel(
    ids, w0, w1, w2, w3, w_env, final, scale, shift, light,
    mixer, cross, direct, base, bias, reads, gram, column, sums, shifts,
):
    step = pl.program_id(0)
    lights = scale.shape[0]
    width = pl.num_programs(0) * w0.shape[1]

    @pl.when(step == 0)
    def _():
        for ref in (reads, gram, column, sums, shifts):
            ref[...] = jnp.zeros_like(ref)

    rows = jnp.concatenate((w0[...], w1[...], w2[...], w3[...], w_env[...]), axis=0)
    weight = final[...].astype(jnp.float32)

    def fold(block):
        total = block[:, :128]
        for s in range(1, block.shape[1] // 128):
            total = total + block[:, s * 128 : (s + 1) * 128]
        return total

    gains = []
    for l in range(lights):
        gained = weight * (1.0 + scale[l : l + 1, :].astype(jnp.float32))
        gains += split(gained)
        sums[l] = sums[l] + fold(gained)
        shifts[l] = shifts[l] + fold(weight * shift[l : l + 1, :].astype(jnp.float32))
    ones = jnp.ones((16, rows.shape[1]), jnp.bfloat16)
    reads[...] += dot_lanes(jnp.concatenate(gains + [ones], axis=0), rows)
    gram[...] += dot_lanes(rows, rows)
    column[...] += dot_lanes(rows, jnp.ones((128, rows.shape[1]), jnp.bfloat16))

    @pl.when(step == pl.num_programs(0) - 1)
    def _():
        average = reads[256:257] * (1.0 / width)
        centred = gram[...] * (1.0 / width) - (column[:, :1] * (1.0 / width)) * average
        mixer[:256], mixer[256:512] = split(centred[:256, :256])
        for l in range(lights):
            total = jnp.sum(sums[l], axis=1, keepdims=True)
            read = reads[l * 128 : l * 128 + 64] + reads[l * 128 + 64 : l * 128 + 128]
            read = read - total * average
            start = 512 + l * 128
            mixer[start : start + 64], mixer[start + 64 : start + 128] = split(read[:, :256])
            bias[l] = jnp.broadcast_to(
                jnp.sum(shifts[l], axis=1, keepdims=True), bias.shape[1:]
            )
            tokens = light[l]
            cross[l] = 2.0 * dot_split(centred[:256, 256:], tokens)
            direct[l] = dot_split(read[:, 256:], tokens)
            turned = tokens.astype(jnp.float32).T
            own = jnp.sum(dot_split(centred[256:, 256:], tokens) * turned, axis=0, keepdims=True)
            base[l] = jnp.broadcast_to(own, base.shape[1:])


def render_kernel(ids, a0, a1, a2, a3, mixer, cross, direct, base, bias, attrs, rendered):
    me = ids[0]
    attrs[pl.ds(me, 1)] = a0[...][None]
    attrs[pl.ds(1 - me, 1)] = a1[...][None]
    latents = jnp.concatenate((a0[...], a1[...], a2[...], a3[...]), axis=0)
    mixed = jnp.dot(mixer[...], latents, preferred_element_type=jnp.float32)
    square = mixed[:256] + mixed[256:512]
    wide = latents.astype(jnp.float32)
    for l in range(rendered.shape[0]):
        spread = jnp.sum(wide * (square + cross[l]), axis=0, keepdims=True) + base[l, :1]
        invert = lax.rsqrt(jnp.maximum(spread, 0.0) + EPS)
        start = 512 + l * 128
        read = mixed[start : start + 64] + mixed[start + 64 : start + 128] + direct[l]
        shift = jnp.concatenate([bias[l]] * (read.shape[1] // 128), axis=1)
        rendered[l] = (read * invert + shift).astype(jnp.bfloat16)


LIMIT = pltpu.CompilerParams(vmem_limit_bytes=24 << 20)
RESIDENT = pl.BlockSpec(memory_space=pltpu.VMEM)


def resident(*arrays):
    return [pltpu.with_memory_space_constraint(a, pltpu.VMEM) for a in arrays]


def whole(shape):
    return pl.BlockSpec(shape, lambda *_: (0,) * len(shape))


def on_device(
    q_inv,
    k_inv,
    v_inv,
    group_ids,
    w_attr,
    env_ids,
    env_table,
    w_embed_attr,
    w_embed_env,
    mod_scale,
    mod_shift,
    w_final,
):
    groups, rows, width = q_inv.shape
    heads = width // HD
    first = 3 * rows // 4
    patch = w_attr.shape[2]
    lights, model = mod_scale.shape
    channels = w_embed_env.shape[0]
    me = lax.axis_index("seq") % 2
    grp = lax.axis_index("grp")

    def pick(array, group, start=0, count=rows):
        return lax.dynamic_slice(array, (group, start, 0), (1, count, width))[0]

    same0 = seq_swap(pick(q_inv, me, 0, first), 2)
    cross0 = seq_swap(pick(q_inv, 1 - me, 0, first), 3)
    kx = seq_swap(pick(k_inv, 1 - me), 1)
    vx = seq_swap(pick(v_inv, 1 - me), 1)
    qx = seq_swap(pick(q_inv, 1 - me), 1)

    mine = 2 * grp + me
    others = (mine, 2 * grp + 1 - me, 2 * (1 - grp) + me, 2 * (1 - grp) + 1 - me)
    ids = jnp.stack([me] + [group_ids[n] for n in others]).astype(jnp.int32)

    cols = STEP_HEADS * HD
    steps = heads // STEP_HEADS
    picked = pl.BlockSpec((None, rows, cols), lambda g, s: (s[0], 0, g))
    plain = pl.BlockSpec((rows, cols), lambda g, s: (0, g))
    reads = pl.BlockSpec((STEP_HEADS, 80, 2 * rows), lambda g, s: (g, 0, 0))
    vw, mean, level = pl.pallas_call(
        local_kernel,
        grid_spec=pltpu.PrefetchScalarGridSpec(
            num_scalar_prefetch=1,
            grid=(steps,),
            in_specs=[
                picked,
                plain,
                picked,
                plain,
                picked,
                plain,
                pl.BlockSpec((None, patch, cols), lambda g, s: (s[1], 0, g)),
            ],
            out_specs=[
                reads,
                pl.BlockSpec((STEP_HEADS, 64, 2 * rows), lambda g, s: (g, 0, 0)),
                whole((heads, 2 * rows)),
            ],
        ),
        out_shape=[
            jax.ShapeDtypeStruct((heads, 80, 2 * rows), jnp.bfloat16),
            jax.ShapeDtypeStruct((heads, 64, 2 * rows), jnp.float32),
            jax.ShapeDtypeStruct((heads, 2 * rows), jnp.float32),
        ],
        compiler_params=LIMIT,
        name="local",
    )(ids, q_inv, qx, k_inv, kx, v_inv, vx, jnp.swapaxes(w_attr, 1, 2))

    late_same = pick(q_inv, me, first, rows - first)
    late_cross = pick(q_inv, 1 - me, first, rows - first)
    level, late_same, late_cross = lax.optimization_barrier((level, late_same, late_cross))
    home = seq_swap(level, 2)
    same1 = seq_swap(late_same, 2)
    cross1 = seq_swap(late_cross, 3)

    lighting = jnp.take(env_table, env_ids, axis=0)
    strips = model // CHUNK
    weights = [
        pl.BlockSpec((None, patch, CHUNK), lambda g, s, n=n: (s[1 + n], 0, g))
        for n in range(4)
    ]
    strip = lambda count: pl.BlockSpec((count, CHUNK), lambda g, s: (0, g))
    kinds = 4 * patch
    inputs = kinds + channels
    out_shapes = [
        pltpu.VMEM((2 * kinds + 2 * lights * patch, kinds), jnp.bfloat16),
        pltpu.VMEM((lights, kinds, rows), jnp.float32),
        pltpu.VMEM((lights, patch, rows), jnp.float32),
        pltpu.VMEM((lights, 8, rows), jnp.float32),
        pltpu.VMEM((lights, patch, 128), jnp.float32),
    ]
    prepared = pl.pallas_call(
        prepare_kernel,
        grid_spec=pltpu.PrefetchScalarGridSpec(
            num_scalar_prefetch=1,
            grid=(strips,),
            in_specs=weights
            + [
                strip(channels),
                strip(patch),
                strip(lights),
                strip(lights),
                whole((lights, rows, channels)),
            ],
            out_specs=[whole(s.shape) for s in out_shapes],
            scratch_shapes=[
                pltpu.VMEM((2 * lights * patch + 16, inputs), jnp.float32),
                pltpu.VMEM((inputs, inputs), jnp.float32),
                pltpu.VMEM((inputs, 128), jnp.float32),
                pltpu.VMEM((lights, patch, 128), jnp.float32),
                pltpu.VMEM((lights, patch, 128), jnp.float32),
            ],
        ),
        out_shape=out_shapes,
        compiler_params=LIMIT,
        name="prepare",
    )(
        ids,
        w_embed_attr,
        w_embed_attr,
        w_embed_attr,
        w_embed_attr,
        w_embed_env,
        w_final.T,
        mod_scale,
        mod_shift,
        lighting,
    )

    def remote(same, crossed, spans, lane):
        count = same.shape[0]
        wide = 2 * count
        block = pl.BlockSpec((count, cols), lambda g, s: (0, g))
        sent = pl.pallas_call(
            lambda *refs: remote_kernel(spans, *refs),
            grid_spec=pltpu.PrefetchScalarGridSpec(
                num_scalar_prefetch=1,
                grid=(steps,),
                in_specs=[
                    block,
                    block,
                    picked,
                    plain,
                    reads,
                    pl.BlockSpec((heads, wide), lambda g, s: (0, lane)),
                ],
                out_specs=whole((64 + heads, wide)),
                scratch_shapes=[
                    pltpu.VMEM((64, wide), jnp.float32),
                    pltpu.VMEM((heads, wide), jnp.float32),
                ],
            ),
            out_shape=jax.ShapeDtypeStruct((64 + heads, wide), jnp.bfloat16),
            compiler_params=LIMIT,
            name="remote",
        )(ids, same, crossed, k_inv, kx, vw, home)
        return seq_swap(sent, 2)

    back0 = remote(same0, cross0, ((0, 128), (128, 192)), 0)
    back1 = remote(same1, cross1, ((0, 64),), 3)
    early = pl.pallas_call(
        early_kernel,
        in_specs=[RESIDENT] * 2,
        out_specs=RESIDENT,
        out_shape=pltpu.VMEM((64, 2 * first), jnp.float32),
        compiler_params=LIMIT,
        name="early",
    )(*resident(back0, mean))
    own, other = pl.pallas_call(
        merge_kernel,
        in_specs=[RESIDENT] * 3,
        out_specs=[RESIDENT] * 2,
        out_shape=[pltpu.VMEM((64, rows), jnp.bfloat16)] * 2,
        compiler_params=LIMIT,
        name="merge",
    )(*resident(back1, mean, early))
    a1 = seq_swap(other, 1)
    a2 = grp_swap(own)
    a3 = both_swap(other)
    attrs, rendered = pl.pallas_call(
        render_kernel,
        in_specs=[pl.BlockSpec(memory_space=pltpu.SMEM)] + [RESIDENT] * 9,
        out_specs=[RESIDENT] * 2,
        out_shape=[
            jax.ShapeDtypeStruct((groups, patch, rows), jnp.bfloat16),
            jax.ShapeDtypeStruct((lights, patch, rows), jnp.bfloat16),
        ],
        compiler_params=LIMIT,
        name="render",
    )(ids, *resident(own, a1, a2, a3, *prepared))
    return (jnp.swapaxes(attrs, 1, 2), jnp.swapaxes(rendered, 1, 2))


def solution(mesh):
    in_specs = (
        P("grp", "seq", None),
        P("grp", "seq", None),
        P("grp", "seq", None),
        P(),
        P(),
        P("grp", "seq"),
        P(),
        P(),
        P(),
        P("grp", None),
        P("grp", None),
        P(),
    )
    out_specs = (P("grp", "seq", None), P("grp", "seq", None))
    return jax.shard_map(
        on_device, mesh=mesh, in_specs=in_specs, out_specs=out_specs, check_vma=False
    )
```

time: 113 us -> 113 us (level)
  Pallas kernels: 55.5 us -> 67 us
  waiting for transfers between devices: 22.2 us -> 11.8 us
  local copies, waits for them, and re-layouts: 17.7 us -> 20.3 us
  other arithmetic: 2.48 us -> 0.15 us
  starting transfers between devices: 14 us -> 12.3 us
    ppermute x12 -> x11, waiting for transfers between devices: 22.2 us -> 11.8 us  [seq_swap(): return lax.ppermute(block, 'seq', [(i, i ^ flip) for i in range(count)])]
    pallas_call x1, Pallas kernels: 17.7 us -> 26.5 us  [on_device(): pl.pallas_call(local_kernel, grid_spec=pltpu.PrefetchScalarGridSpec(num_s...]
    pallas_call x6, Pallas kernels: 37.8 us -> 40.5 us  [the longest x2 32.6 us: remote(): pl.pallas_call(lambda *refs: remote_kernel(spans, *refs), grid_spec=pltpu...]
    another operation x0 -> x1, local copies, waits for them, and re-layouts: none -> 2.59 us  [on_device(): ids = jnp.stack([me] + [group_ids[n] for n in others]).astype(jnp.int32)]
    unnamed x49 -> x31, local copies, waits for them, and re-layouts: 9.78 us -> 7.38 us
    squeeze x4 -> x5, local copies, waits for them, and re-layouts: 5.98 us -> 8.37 us  [pick(): return lax.dynamic_slice(array, (group, start, 0), (1, count, width))[0]]
    concatenate x2 -> x0, other arithmetic: 1.59 us -> none  [the longest x1 0.93 us: on_device(): return (jnp.concatenate(attrs, axis=1), jnp.concatenate(renders, axis=1))]
    ppermute x2 -> x1, starting transfers between devices: 1.7 us -> 0.11 us  [both_swap(): return lax.ppermute(block, ('grp', 'seq'), route)]
  transfers between devices with their start and end apart: 16 -> 13, of which waited for: 1 -> 1; matrix products, arithmetic and copies ran while one was open for 10% -> 9% of each run, Pallas kernels for 44% -> 58%
where the time goes in v2:
time: 113 us; the launch traced here: 112 us
  Pallas kernels  67 us (59%)
  local copies, waits for them, and re-layouts  20.3 us (18%)
  starting transfers between devices  12.3 us (11%)
  waiting for transfers between devices  11.8 us (10%)
    pallas_call x2, Pallas kernels, remote(): pl.pallas_call(lambda *refs: remote_kernel(spans, *refs), grid_spec=pltpu...  32.6 us
    pallas_call x1, Pallas kernels, on_device(): pl.pallas_call(local_kernel, grid_spec=pltpu.PrefetchScalarGridSpec(num_s...  26.5 us
    ppermute x11, waiting for transfers between devices, seq_swap(): return lax.ppermute(block, 'seq', [(i, i ^ flip) for i in range(count)])  11.8 us
    ppermute x11, starting transfers between devices, seq_swap(): return lax.ppermute(block, 'seq', [(i, i ^ flip) for i in range(count)])  10.8 us
    squeeze x5, local copies, waits for them, and re-layouts, pick(): return lax.dynamic_slice(array, (group, start, 0), (1, count, width))[0]  8.37 us
    unnamed x31, local copies, waits for them, and re-layouts  7.38 us
    pallas_call x1, Pallas kernels, on_device(): pl.pallas_call(prepare_kernel, grid_spec=pltpu.PrefetchScalarGridSpec(num...  6.09 us
    another operation x1, local copies, waits for them, and re-layouts, on_device(): ids = jnp.stack([me] + [group_ids[n] for n in others]).astype(jnp.int32)  2.59 us
  transfers between devices with their start and end apart: 13, of which 1 were waited for; matrix products, arithmetic and copies ran while one was open for 9% of the time, Pallas kernels for 58%

profile of v2, /device:TPU:1, one launch (start us, length us, event | category | flops | bytes accessed | tf_op | source)
XLA Modules:
  0.0 112.5 jit_solution(16025860656931339845)
XLA Ops:
  0.7 2.5 %dynamic-slice_bitcast_fusion.2 = bf16[256,2048]{1,0:T(8,128)(2,1)} fusion(bf16[2,256,2048]{2,1,0:T(8,128)(2,1)} %q.1, s32[]{:T(128)S(6)} %select_n.44), kind=kLoop, calls=%fused_computation.3 | loop fusion | bytes 2097156 | tf_op jit(solution)/shard_map/squeeze | solution.py:283
  3.1 3.2 %collective-permute-start = (bf16[256,2048]{1,0:T(8,128)(2,1)}, bf16[256,2048]{1,0:T(8,128)(2,1)}, u32[]{:S(2)}, u32[]{:S(2)}) collective-permute-start(bf16[256,2048]{1,0:T(8,128)(2,1)} %dynamic-slice_bitcast_fusion.2), channel_id=1, source_target_pairs={{0,1},{1,0},{2,3},{3,2},{4,5},{5,4},{6,7},{7,6},{8,9},{9,8},{10,11... | collective-permute-start | bytes 3145736 | tf_op jit(solution)/shard_map/ppermute | solution.py:22
  6.3 1.1 dynamic-slice_bitcast_fusion.1
  7.4 1.1 dynamic-slice_bitcast_fusion
  8.5 0.5 collective-permute-start.2
  9.0 2.7 %dynamic-slice_bitcast_fusion.3 = (bf16[192,2048]{1,0:T(8,128)(2,1)}, bf16[192,2048]{1,0:T(8,128)(2,1)}) fusion(bf16[2,256,2048]{2,1,0:T(8,128)(2,1)} %q.1, s32[]{:T(128)S(6)} %select_n.44, s32[]{:T(128)S(6)} %select_n.45), kind=kLoop, calls=%fused_computation.4 | loop fusion | bytes 3145736 | tf_op jit(solution)/shard_map/squeeze | solution.py:283
  11.7 1.6 %collective-permute-start.8 = (bf16[192,2048]{1,0:T(8,128)(2,1)}, bf16[192,2048]{1,0:T(8,128)(2,1)}, u32[]{:S(2)}, u32[]{:S(2)}) collective-permute-start(bf16[192,2048]{1,0:T(8,128)(2,1)} %get-tuple-element.32), channel_id=1, source_target_pairs={{0,3},{1,2},{2,1},{3,0},{4,7},{5,6},{6,5},{7,4},{8,11},{9,10},{10,... | collective-permute-start | bytes 2359304 | tf_op jit(solution)/shard_map/ppermute | solution.py:22
  13.4 0.7 fusion.1
  14.0 2.6 %stack.7.ids.refs_0_ = s32[5]{0:T(128)S(1)} concatenate(s32[1]{0:T(128)} %bitcast, s32[1]{0:T(128)} %get-tuple-element.38, s32[1]{0:T(128)} %get-tuple-element.37, s32[1]{0:T(128)} %get-tuple-element.39, s32[1]{0:T(128)} %get-tuple-element.36), dimensions={0} | concatenate | bytes 40 | tf_op jit(solution)/shard_map/stack | solution.py:293
  16.6 1.1 dynamic-slice_bitcast_fusion.5
  17.7 1.6 %copy-done.3 = bf16[2,256,2048]{2,1,0:T(8,128)(2,1)S(1)} copy-done((bf16[2,256,2048]{2,1,0:T(8,128)(2,1)S(1)}, bf16[2,256,2048]{2,1,0:T(8,128)(2,1)}, u32[]{:S(2)}) %copy-start.3) | copy-done | bytes 2097176
  19.3 1.6 %copy-done.7 = bf16[2,256,2048]{2,1,0:T(8,128)(2,1)S(1)} copy-done((bf16[2,256,2048]{2,1,0:T(8,128)(2,1)S(1)}, bf16[2,256,2048]{2,1,0:T(8,128)(2,1)}, u32[]{:S(2)}) %copy-start.7) | copy-done | bytes 2097176
  20.9 1.2 %copy-done.9 = bf16[4,2048,64]{1,2,0:T(8,128)(2,1)S(1)} copy-done((bf16[4,2048,64]{1,2,0:T(8,128)(2,1)S(1)}, bf16[4,2048,64]{1,2,0:T(8,128)(2,1)}, u32[]{:S(2)}) %copy-start.9) | copy-done | bytes 1048600
  22.1 26.5 %local.1 = (bf16[16,80,512]{2,1,0:T(8,128)(2,1)S(1)}, f32[16,64,512]{2,1,0:T(8,128)S(1)}, f32[16,512]{1,0:T(8,128)S(1)}) custom-call(s32[5]{0:T(128)S(1)} %stack.7.ids.refs_0_, bf16[2,256,2048]{2,1,0:T(8,128)(2,1)S(1)} %copy-done.3, bf16[256,2048]{1,0:T(8,128)(2,1)} %collective-permute-done.qx, bf16[2,256,2048]{2,1,0:T(8,128)(2,1)S(1)} %copy-done.2, ...), custom_call_target="tpu_custom_call" | custom-call | tf_op jit(solution)/shard_map/local/pallas_call | solution.py:300
  48.6 1.3 %copy-done.4 = f32[16,64,512]{2,1,0:T(8,128)} copy-done((f32[16,64,512]{2,1,0:T(8,128)}, f32[16,64,512]{2,1,0:T(8,128)S(1)}, u32[]{:S(2)}) %copy-start.4) | copy-done | bytes 2097176
  50.0 1.8 %collective-permute-start.4 = (bf16[64,2048]{1,0:T(8,128)(2,1)S(1)}, bf16[64,2048]{1,0:T(8,128)(2,1)S(1)}, u32[]{:S(2)}, u32[]{:S(2)}) collective-permute-start(bf16[64,2048]{1,0:T(8,128)(2,1)S(1)} %get-tuple-element.19), channel_id=1, source_target_pairs={{0,3},{1,2},{2,1},{3,0},{4,7},{5,6},{6,5},{7,4},{8,11},{9,10},{10,... | collective-permute-start | bytes 786440 | tf_op jit(solution)/shard_map/ppermute | solution.py:22
  51.8 0.0 collective-permute-start.5
  51.9 11.8 %collective-permute-done.5.refs_6_ = f32[16,512]{1,0:T(8,128)S(1)} collective-permute-done((f32[16,512]{1,0:T(8,128)S(1)}, f32[16,512]{1,0:T(8,128)S(1)}, u32[]{:S(2)}, u32[]{:S(2)}) %collective-permute-start.5) | collective-permute-done | bytes 32800 | tf_op jit(solution)/shard_map/ppermute | solution.py:22
  63.6 22.4 %remote.3 = bf16[80,384]{1,0:T(8,128)(2,1)S(1)} custom-call(s32[5]{0:T(128)S(1)} %stack.7.ids.refs_0_, bf16[192,2048]{1,0:T(8,128)(2,1)} %collective-permute-done.7.refs_1_, bf16[192,2048]{1,0:T(8,128)(2,1)} %collective-permute-done.8.refs_2_, bf16[2,256,2048]{2,1,0:T(8,128)(2,1)S(1)} %copy-done.2, bf16[256,2048]{1,0:T(8,128)(2,1)} %collective-permute-done.1.kx.refs_4_, ...), custom_call_target="tpu_custom_call" | custom-call | tf_op jit(solution)/shard_map/remote/pallas_call | solution.py:394
  86.0 0.1 collective-permute-start.9
  86.2 10.2 %remote.2 = bf16[80,128]{1,0:T(8,128)(2,1)S(1)} custom-call(s32[5]{0:T(128)S(1)} %stack.7.ids.refs_0_, bf16[64,2048]{1,0:T(8,128)(2,1)S(1)} %collective-permute-done.3.refs_1_, bf16[64,2048]{1,0:T(8,128)(2,1)S(1)} %collective-permute-done.4.refs_2_, bf16[2,256,2048]{2,1,0:T(8,128)(2,1)S(1)} %copy-done.2, ...), custom_call_target="tpu_custom_call" | custom-call | tf_op jit(solution)/shard_map/remote/pallas_call | solution.py:394
  96.4 1.5 %collective-permute-start.6 = (bf16[80,128]{1,0:T(8,128)(2,1)S(1)}, bf16[80,128]{1,0:T(8,128)(2,1)S(1)}, u32[]{:S(2)}, u32[]{:S(2)}) collective-permute-start(bf16[80,128]{1,0:T(8,128)(2,1)S(1)} %remote.2), channel_id=1, source_target_pairs={{0,2},{1,3},{2,0},{3,1},{4,6},{5,7},{6,4},{7,5},{8,10},{9,11},{10,... | collective-permute-start | bytes 61448 | tf_op jit(solution)/shard_map/ppermute | solution.py:22
  97.9 1.3 %gather_fusion = bf16[512,128]{1,0:T(8,128)(2,1)S(1)} fusion(bf16[4096,128]{1,0:T(8,128)(2,1)S(1)} %copy-done, s32[1024]{0:T(1024)S(1)} %pad_clamp_fusion), kind=kCustom, calls=%fused_computation | custom fusion | bytes 264192 | tf_op jit(solution)/shard_map/jit(_take)/gather | solution.py:336
  99.3 1.6 %copy-done.5 = f32[16,64,512]{2,1,0:T(8,128)S(1)} copy-done((f32[16,64,512]{2,1,0:T(8,128)S(1)}, f32[16,64,512]{2,1,0:T(8,128)}, u32[]{:S(2)}) %copy-start.5) | copy-done | bytes 2097176
  100.9 0.1 early.1
  101.0 0.2 merge.1
  101.2 2.0 %collective-permute-start.10 = (bf16[64,256]{1,0:T(8,128)(2,1)S(1)}, bf16[64,256]{1,0:T(8,128)(2,1)S(1)}, u32[]{:S(2)}, u32[]{:S(2)}) collective-permute-start(bf16[64,256]{1,0:T(8,128)(2,1)S(1)} %get-tuple-element.24), channel_id=1, source_target_pairs={{0,1},{1,0},{2,3},{3,2},{4,5},{5,4},{6,7},{7,6},{8,9},{9,8},{10,11... | collective-permute-start | bytes 98312 | tf_op jit(solution)/shard_map/ppermute | solution.py:22
  103.2 0.1 collective-permute-start.12
  103.3 1.3 %collective-permute-start.11 = (bf16[64,256]{1,0:T(8,128)(2,1)S(1)}, bf16[64,256]{1,0:T(8,128)(2,1)S(1)}, u32[]{:S(2)}, u32[]{:S(2)}) collective-permute-start(bf16[64,256]{1,0:T(8,128)(2,1)S(1)} %get-tuple-element.23.a0), channel_id=1, source_target_pairs={{0,128},{128,0},{1,129},{129,1},{2,130},{130,2},{3,131},{131,3},{4... | collective-permute-start | bytes 98312 | tf_op jit(solution)/shard_map/ppermute | solution.py:26
  104.7 0.1 broadcast_select_fusion.light
  104.8 6.1 %prepare.1 = (bf16[768,256]{1,0:T(8,128)(2,1)S(1)}, f32[2,256,256]{2,1,0:T(8,128)S(1)}, f32[2,64,256]{2,1,0:T(8,128)S(1)}, f32[2,8,256]{2,1,0:T(8,128)S(1)}, f32[2,64,128]{2,1,0:T(8,128)S(1)}) custom-call(s32[5]{0:T(128)S(1)} %stack.7.ids.refs_0_, bf16[4,64,4096]{2,1,0:T(8,128)(2,1)S(1)} %copy-done.1, bf16[4,64,4096]{2,1,0:T(8,128)(2,1)S(1)} %copy-done.1, ...), custom_call_target="tpu_custom_call" | custom-call | tf_op jit(solution)/shard_map/prepare/pallas_call | solution.py:352
  111.0 1.5 %render.1 = (bf16[2,64,256]{2,1,0:T(8,128)(2,1)}, bf16[2,64,256]{2,1,0:T(8,128)(2,1)}) custom-call(s32[5]{0:T(128)S(1)} %stack.7.ids.refs_0_, bf16[64,256]{1,0:T(8,128)(2,1)S(1)} %get-tuple-element.23.a0, bf16[64,256]{1,0:T(8,128)(2,1)S(1)} %collective-permute-done.10.a1, bf16[64,256]{1,0:T(8,128)(2,1)S(1)} %collective-permute-done.11.a2, ...), custom_call_target="tpu_custom_call" | custom-call | tf_op jit(solution)/shard_map/render/pallas_call | solution.py:440
  (44 shorter events, 0.1 us)
Async XLA Ops:
  0.6 97.3 %copy-start = (bf16[4096,128]{1,0:T(8,128)(2,1)S(1)}, bf16[4096,128]{1,0:T(8,128)(2,1)}, u32[]{:S(2)}) copy-start(bf16[4096,128]{1,0:T(8,128)(2,1)} %param.18) | copy-start | bytes 3145732
  0.6 5.7 %copy-start.2 = (bf16[2,256,2048]{2,1,0:T(8,128)(2,1)S(1)}, bf16[2,256,2048]{2,1,0:T(8,128)(2,1)}, u32[]{:S(2)}) copy-start(bf16[2,256,2048]{2,1,0:T(8,128)(2,1)} %refs_3_.3) | copy-start | bytes 6291460
  0.7 6.8 %copy-start.6 = (bf16[2,256,2048]{2,1,0:T(8,128)(2,1)S(1)}, bf16[2,256,2048]{2,1,0:T(8,128)(2,1)}, u32[]{:S(2)}) copy-start(bf16[2,256,2048]{2,1,0:T(8,128)(2,1)} %v.1) | copy-start | bytes 6291460
  3.1 14.5 %collective-permute-start = (bf16[256,2048]{1,0:T(8,128)(2,1)}, bf16[256,2048]{1,0:T(8,128)(2,1)}, u32[]{:S(2)}, u32[]{:S(2)}) collective-permute-start(bf16[256,2048]{1,0:T(8,128)(2,1)} %dynamic-slice_bitcast_fusion.2), channel_id=1, source_target_pairs={{0,1},{1,0},{2,3},{3,2},{4,5},{5,4},{6,7},{7,6},{8,9},{9,8},{10,11... | collective-permute-start | bytes 3145736 | tf_op jit(solution)/shard_map/ppermute | solution.py:22
  7.4 10.3 %collective-permute-start.1 = (bf16[256,2048]{1,0:T(8,128)(2,1)}, bf16[256,2048]{1,0:T(8,128)(2,1)}, u32[]{:S(2)}, u32[]{:S(2)}) collective-permute-start(bf16[256,2048]{1,0:T(8,128)(2,1)} %dynamic-slice_bitcast_fusion.1), channel_id=1, source_target_pairs={{0,1},{1,0},{2,3},{3,2},{4,5},{5,4},{6,7},{7,6},{8,9},{9,8},{10,11... | collective-permute-start | bytes 3145736 | tf_op jit(solution)/shard_map/ppermute | solution.py:22
  8.5 4.8 %copy-start.13 = (s32[4]{0:T(128)S(1)}, s32[4]{0:T(128)}, u32[]{:S(2)}) copy-start(s32[4]{0:T(128)} %param.15) | copy-start | bytes 52
  8.5 9.2 %collective-permute-start.2 = (bf16[256,2048]{1,0:T(8,128)(2,1)}, bf16[256,2048]{1,0:T(8,128)(2,1)}, u32[]{:S(2)}, u32[]{:S(2)}) collective-permute-start(bf16[256,2048]{1,0:T(8,128)(2,1)} %dynamic-slice_bitcast_fusion), channel_id=1, source_target_pairs={{0,1},{1,0},{2,3},{3,2},{4,5},{5,4},{6,7},{7,6},{8,9},{9,8},{10,11... | collective-permute-start | bytes 3145736 | tf_op jit(solution)/shard_map/ppermute | solution.py:22
  11.7 40.1 %collective-permute-start.7 = (bf16[192,2048]{1,0:T(8,128)(2,1)}, bf16[192,2048]{1,0:T(8,128)(2,1)}, u32[]{:S(2)}, u32[]{:S(2)}) collective-permute-start(bf16[192,2048]{1,0:T(8,128)(2,1)} %get-tuple-element.33), channel_id=1, source_target_pairs={{0,2},{1,3},{2,0},{3,1},{4,6},{5,7},{6,4},{7,5},{8,10},{9,11},{10,... | collective-permute-start | bytes 2359304 | tf_op jit(solution)/shard_map/ppermute | solution.py:22
  11.7 40.2 %collective-permute-start.8 = (bf16[192,2048]{1,0:T(8,128)(2,1)}, bf16[192,2048]{1,0:T(8,128)(2,1)}, u32[]{:S(2)}, u32[]{:S(2)}) collective-permute-start(bf16[192,2048]{1,0:T(8,128)(2,1)} %get-tuple-element.32), channel_id=1, source_target_pairs={{0,3},{1,2},{2,1},{3,0},{4,7},{5,6},{6,5},{7,4},{8,11},{9,10},{10,... | collective-permute-start | bytes 2359304 | tf_op jit(solution)/shard_map/ppermute | solution.py:22
  17.7 1.6 %copy-start.3 = (bf16[2,256,2048]{2,1,0:T(8,128)(2,1)S(1)}, bf16[2,256,2048]{2,1,0:T(8,128)(2,1)}, u32[]{:S(2)}) copy-start(bf16[2,256,2048]{2,1,0:T(8,128)(2,1)} %q.1) | copy-start | bytes 6291460
  19.3 1.6 %copy-start.7 = (bf16[2,256,2048]{2,1,0:T(8,128)(2,1)S(1)}, bf16[2,256,2048]{2,1,0:T(8,128)(2,1)}, u32[]{:S(2)}) copy-start(bf16[2,256,2048]{2,1,0:T(8,128)(2,1)} %v.1) | copy-start | bytes 6291460
  20.9 1.2 %copy-start.9 = (bf16[4,2048,64]{1,2,0:T(8,128)(2,1)S(1)}, bf16[4,2048,64]{1,2,0:T(8,128)(2,1)}, u32[]{:S(2)}) copy-start(bf16[4,2048,64]{1,2,0:T(8,128)(2,1)} %param.16) | copy-start | bytes 3145732
  22.1 29.7 %copy-start.14 = (s32[2,256]{1,0:T(2,128)S(1)}, s32[2,256]{1,0:T(2,128)}, u32[]{:S(2)}) copy-start(s32[2,256]{1,0:T(2,128)} %param.17) | copy-start | bytes 6148
  48.6 1.4 %copy-start.4 = (f32[16,64,512]{2,1,0:T(8,128)}, f32[16,64,512]{2,1,0:T(8,128)S(1)}, u32[]{:S(2)}) copy-start(f32[16,64,512]{2,1,0:T(8,128)S(1)} %get-tuple-element.22.mean) | copy-start | bytes 6291460
  50.0 36.2 %collective-permute-start.3 = (bf16[64,2048]{1,0:T(8,128)(2,1)S(1)}, bf16[64,2048]{1,0:T(8,128)(2,1)S(1)}, u32[]{:S(2)}, u32[]{:S(2)}) collective-permute-start(bf16[64,2048]{1,0:T(8,128)(2,1)S(1)} %get-tuple-element.18), channel_id=1, source_target_pairs={{0,2},{1,3},{2,0},{3,1},{4,6},{5,7},{6,4},{7,5},{8,10},{9,11},{10,... | collective-permute-start | bytes 786440 | tf_op jit(solution)/shard_map/ppermute | solution.py:22
  50.0 36.2 %collective-permute-start.4 = (bf16[64,2048]{1,0:T(8,128)(2,1)S(1)}, bf16[64,2048]{1,0:T(8,128)(2,1)S(1)}, u32[]{:S(2)}, u32[]{:S(2)}) collective-permute-start(bf16[64,2048]{1,0:T(8,128)(2,1)S(1)} %get-tuple-element.19), channel_id=1, source_target_pairs={{0,3},{1,2},{2,1},{3,0},{4,7},{5,6},{6,5},{7,4},{8,11},{9,10},{10,... | collective-permute-start | bytes 786440 | tf_op jit(solution)/shard_map/ppermute | solution.py:22
  51.8 11.8 %collective-permute-start.5 = (f32[16,512]{1,0:T(8,128)S(1)}, f32[16,512]{1,0:T(8,128)S(1)}, u32[]{:S(2)}, u32[]{:S(2)}) collective-permute-start(f32[16,512]{1,0:T(8,128)S(1)} %get-tuple-element.21), channel_id=1, source_target_pairs={{0,2},{1,3},{2,0},{3,1},{4,6},{5,7},{6,4},{7,5},{8,10},{9,11},{10,... | collective-permute-start | bytes 98312 | tf_op jit(solution)/shard_map/ppermute | solution.py:22
  86.0 13.2 %collective-permute-start.9 = (bf16[80,384]{1,0:T(8,128)(2,1)S(1)}, bf16[80,384]{1,0:T(8,128)(2,1)S(1)}, u32[]{:S(2)}, u32[]{:S(2)}) collective-permute-start(bf16[80,384]{1,0:T(8,128)(2,1)S(1)} %remote.3), channel_id=1, source_target_pairs={{0,2},{1,3},{2,0},{3,1},{4,6},{5,7},{6,4},{7,5},{8,10},{9,11},{10,... | collective-permute-start | bytes 184328 | tf_op jit(solution)/shard_map/ppermute | solution.py:22
  96.4 4.7 %collective-permute-start.6 = (bf16[80,128]{1,0:T(8,128)(2,1)S(1)}, bf16[80,128]{1,0:T(8,128)(2,1)S(1)}, u32[]{:S(2)}, u32[]{:S(2)}) collective-permute-start(bf16[80,128]{1,0:T(8,128)(2,1)S(1)} %remote.2), channel_id=1, source_target_pairs={{0,2},{1,3},{2,0},{3,1},{4,6},{5,7},{6,4},{7,5},{8,10},{9,11},{10,... | collective-permute-start | bytes 61448 | tf_op jit(solution)/shard_map/ppermute | solution.py:22
  99.3 1.6 %copy-start.5 = (f32[16,64,512]{2,1,0:T(8,128)S(1)}, f32[16,64,512]{2,1,0:T(8,128)}, u32[]{:S(2)}) copy-start(f32[16,64,512]{2,1,0:T(8,128)} %copy-done.4) | copy-start | bytes 6291460
  100.9 3.9 %copy-start.1 = (bf16[4,64,4096]{2,1,0:T(8,128)(2,1)S(1)}, bf16[4,64,4096]{2,1,0:T(8,128)(2,1)}, u32[]{:S(2)}) copy-start(bf16[4,64,4096]{2,1,0:T(8,128)(2,1)} %w3.1) | copy-start | bytes 6291460
  100.9 3.9 %copy-start.8 = (bf16[128,4096]{1,0:T(8,128)(2,1)S(1)}, bf16[128,4096]{1,0:T(8,128)(2,1)}, u32[]{:S(2)}) copy-start(bf16[128,4096]{1,0:T(8,128)(2,1)} %w_env.1) | copy-start | bytes 3145732
  100.9 3.9 %copy-start.10 = (bf16[4096,64]{0,1:T(8,128)(2,1)S(1)}, bf16[4096,64]{0,1:T(8,128)(2,1)}, u32[]{:S(2)}) copy-start(bf16[4096,64]{0,1:T(8,128)(2,1)} %param.23) | copy-start | bytes 1572868
  100.9 3.9 %copy-start.11 = (bf16[2,4096]{1,0:T(2,128)(2,1)S(1)}, bf16[2,4096]{1,0:T(2,128)(2,1)}, u32[]{:S(2)}) copy-start(bf16[2,4096]{1,0:T(2,128)(2,1)} %scale.1) | copy-start | bytes 49156
  100.9 4.0 %copy-start.12 = (bf16[2,4096]{1,0:T(2,128)(2,1)S(1)}, bf16[2,4096]{1,0:T(2,128)(2,1)}, u32[]{:S(2)}) copy-start(bf16[2,4096]{1,0:T(2,128)(2,1)} %shift.1) | copy-start | bytes 49156
  101.2 9.7 %collective-permute-start.10 = (bf16[64,256]{1,0:T(8,128)(2,1)S(1)}, bf16[64,256]{1,0:T(8,128)(2,1)S(1)}, u32[]{:S(2)}, u32[]{:S(2)}) collective-permute-start(bf16[64,256]{1,0:T(8,128)(2,1)S(1)} %get-tuple-element.24), channel_id=1, source_target_pairs={{0,1},{1,0},{2,3},{3,2},{4,5},{5,4},{6,7},{7,6},{8,9},{9,8},{10,11... | collective-permute-start | bytes 98312 | tf_op jit(solution)/shard_map/ppermute | solution.py:22
  103.2 7.8 %collective-permute-start.12 = (bf16[64,256]{1,0:T(8,128)(2,1)S(1)}, bf16[64,256]{1,0:T(8,128)(2,1)S(1)}, u32[]{:S(2)}, u32[]{:S(2)}) collective-permute-start(bf16[64,256]{1,0:T(8,128)(2,1)S(1)} %get-tuple-element.24), channel_id=1, source_target_pairs={{0,129},{1,128},{2,131},{3,130},{4,133},{5,132},{6,135},{7,134},{8... | collective-permute-start | bytes 98312 | tf_op jit(solution)/shard_map/ppermute | solution.py:34
  103.3 7.6 %collective-permute-start.11 = (bf16[64,256]{1,0:T(8,128)(2,1)S(1)}, bf16[64,256]{1,0:T(8,128)(2,1)S(1)}, u32[]{:S(2)}, u32[]{:S(2)}) collective-permute-start(bf16[64,256]{1,0:T(8,128)(2,1)S(1)} %get-tuple-element.23.a0), channel_id=1, source_target_pairs={{0,128},{128,0},{1,129},{129,1},{2,130},{130,2},{3,131},{131,3},{4... | collective-permute-start | bytes 98312 | tf_op jit(solution)/shard_map/ppermute | solution.py:26

commit v3 on v2

--- a/solution.py
+++ b/solution.py
@@ -48,20 +48,38 @@
     return dot_lanes(high, right) + dot_lanes(low, right)
 
 
-def plain_softmax(keys, queries, values):
-    powers = jnp.exp2(dot_lanes(keys, queries) * SCALE).astype(jnp.bfloat16)
-    summed = jnp.dot(values, powers, preferred_element_type=jnp.float32)
-    total = summed[64:65]
-    return summed[:64], total, jnp.log2(total)
-
-
-def shifted_softmax(keys, queries, values):
-    scores = dot_lanes(keys, queries)
-    top = jnp.max(scores, axis=0, keepdims=True)
-    powers = jnp.exp2((scores - top) * SCALE).astype(jnp.bfloat16)
-    summed = jnp.dot(values, powers, preferred_element_type=jnp.float32)
-    total = summed[64:65]
-    return summed[:64], total, top * SCALE + jnp.log2(total)
+def scores_of(keys, queries):
+    half = keys.shape[0] // 2
+    return [dot_lanes(keys[:half], queries), dot_lanes(keys[half:], queries)]
+
+
+def plain_softmax(units):
+    found = []
+    ahead = scores_of(*units[0][:2])
+    for n, (_, _, values) in enumerate(units):
+        scores = ahead
+        if n + 1 < len(units):
+            ahead = scores_of(*units[n + 1][:2])
+        half = values.shape[1] // 2
+        powers = [jnp.exp2(s * SCALE).astype(jnp.bfloat16) for s in scores]
+        summed = jnp.dot(
+            values[:, :half], powers[0], preferred_element_type=jnp.float32
+        ) + jnp.dot(values[:, half:], powers[1], preferred_element_type=jnp.float32)
+        total = summed[64:65]
+        found.append((summed[:64], total, jnp.log2(total)))
+    return found
+
+
+def shifted_softmax(units):
+    found = []
+    for keys, queries, values in units:
+        scores = dot_lanes(keys, queries)
+        top = jnp.max(scores, axis=0, keepdims=True)
+        powers = jnp.exp2((scores - top) * SCALE).astype(jnp.bfloat16)
+        summed = jnp.dot(values, powers, preferred_element_type=jnp.float32)
+        total = summed[64:65]
+        found.append((summed[:64], total, top * SCALE + jnp.log2(total)))
+    return found
 
 
 def worst(levels):
@@ -71,32 +89,69 @@
     return jnp.max(largest)
 
 
-def local_kernel(ids, q, qx, k, kx, v, vx, w, vw, mean, level):
+def first_kernel(place, q, same, cross, sems):
+    me = place[0]
+    count = same.shape[0]
+    copies = [
+        pltpu.make_async_copy(q.at[me, pl.ds(0, count)], same, sems.at[0]),
+        pltpu.make_async_copy(q.at[1 - me, pl.ds(0, count)], cross, sems.at[1]),
+    ]
+    for copy in copies:
+        copy.start()
+    for copy in copies:
+        copy.wait()
+
+
+def second_kernel(place, q, k, v, same, cross, bundle, sems):
+    me = place[0]
+    count = same.shape[0]
+    rest = pl.ds(q.shape[1] - count, count)
+    copies = [
+        pltpu.make_async_copy(a.at[1 - me], bundle.at[n], sems.at[n])
+        for n, a in enumerate((q, k, v))
+    ]
+    copies += [
+        pltpu.make_async_copy(q.at[me, rest], same, sems.at[3]),
+        pltpu.make_async_copy(q.at[1 - me, rest], cross, sems.at[4]),
+    ]
+    for copy in copies:
+        copy.start()
+    for copy in copies:
+        copy.wait()
+
+
+def local_kernel(me, grp, kinds, q, qx, k, kx, v, vx, w, vw, mean, level):
     step = pl.program_id(0)
+    reads = []
 
     for i in range(STEP_HEADS):
         cols = slice(i * HD, (i + 1) * HD)
         values = jnp.concatenate((v[:, cols], vx[:, cols]), axis=0)
         read = dot_lanes(w[:, cols], values).astype(jnp.bfloat16)
-        vw[i, :64] = read
-        vw[i, 64:] = jnp.ones((16, read.shape[1]), jnp.bfloat16)
+        read = jnp.concatenate((read, jnp.ones((16, read.shape[1]), jnp.bfloat16)), axis=0)
+        vw[i] = read
+        reads.append(read)
 
     def attend(softmax):
-        levels = []
+        units = []
         for i in range(STEP_HEADS):
             cols = slice(i * HD, (i + 1) * HD)
             keys = jnp.concatenate((k[:, cols], kx[:, cols]), axis=0)
-            rows = []
-            for lanes, spans in ((0, ((0, 128),)), (256, ((128, 192), (192, 256)))):
+            for spans in (((0, 128),), ((128, 192), (192, 256))):
                 pieces = []
                 for a, b in spans:
                     pieces += [q[a:b, cols], qx[a:b, cols]]
-                summed, total, row = softmax(keys, jnp.concatenate(pieces, axis=0), vw[i])
-                mean[i, :, lanes : lanes + 256] = summed * (1.0 / total)
+                units.append((keys, jnp.concatenate(pieces, axis=0), reads[i]))
+        found = softmax(units)
+        levels = []
+        for i in range(STEP_HEADS):
+            rows = []
+            for n in range(2):
+                summed, total, row = found[2 * i + n]
+                mean[i, :, n * 256 : n * 256 + 256] = summed * (1.0 / total)
                 rows.append(row)
-            row = jnp.concatenate(rows, axis=1)
-            level[pl.ds(step * STEP_HEADS + i, 1), :] = row
-            levels.append(row)
+            levels.append(jnp.concatenate(rows, axis=1))
+            level[pl.ds(step * STEP_HEADS + i, 1), :] = levels[-1]
         return worst(levels)
 
     reach = attend(plain_softmax)
@@ -106,7 +161,7 @@
         attend(shifted_softmax)
 
 
-def remote_kernel(spans, ids, qs, qd, k, kx, vw, home, out, acc, share):
+def remote_kernel(spans, me, qs, qd, k, kx, vw, home, out, acc, share):
     step = pl.program_id(0)
 
     @pl.when(step == 0)
@@ -117,16 +172,21 @@
 
     def attend(softmax):
         gathered = [before[:, a * 2 : b * 2] for a, b in spans]
-        levels = []
+        units = []
         for i in range(STEP_HEADS):
             cols = slice(i * HD, (i + 1) * HD)
             keys = jnp.concatenate((k[:, cols], kx[:, cols]), axis=0)
+            for a, b in spans:
+                queries = jnp.concatenate((qs[a:b, cols], qd[a:b, cols]), axis=0)
+                units.append((keys, queries, vw[i]))
+        found = softmax(units)
+        levels = []
+        for i in range(STEP_HEADS):
             row = pl.ds(step * STEP_HEADS + i, 1)
             theirs = home[row, :]
             rows, mines = [], []
             for n, (a, b) in enumerate(spans):
-                queries = jnp.concatenate((qs[a:b, cols], qd[a:b, cols]), axis=0)
-                summed, total, level = softmax(keys, queries, vw[i])
+                summed, total, level = found[i * len(spans) + n]
                 mine = 1.0 / (1.0 + jnp.exp2(theirs[:, 2 * a : 2 * b] - level))
                 mine = mine.astype(jnp.bfloat16).astype(jnp.float32)
                 gathered[n] = gathered[n] + summed * (mine / total)
@@ -173,7 +233,7 @@
 
 
 def prepare_kernel(
-    ids, w0, w1, w2, w3, w_env, final, scale, shift, light,
+    me, grp, kinds, w0, w1, w2, w3, w_env, final, scale, shift, light,
     mixer, cross, direct, base, bias, reads, gram, column, sums, shifts,
 ):
     step = pl.program_id(0)
@@ -227,8 +287,8 @@
             base[l] = jnp.broadcast_to(own, base.shape[1:])
 
 
-def render_kernel(ids, a0, a1, a2, a3, mixer, cross, direct, base, bias, attrs, rendered):
-    me = ids[0]
+def render_kernel(place, a0, a1, a2, a3, mixer, cross, direct, base, bias, attrs, rendered):
+    me = place[0]
     attrs[pl.ds(me, 1)] = a0[...][None]
     attrs[pl.ds(1 - me, 1)] = a1[...][None]
     latents = jnp.concatenate((a0[...], a1[...], a2[...], a3[...]), axis=0)
@@ -250,6 +310,10 @@
 
 def resident(*arrays):
     return [pltpu.with_memory_space_constraint(a, pltpu.VMEM) for a in arrays]
+
+
+def stay(array):
+    return pltpu.with_memory_space_constraint(array, pltpu.HBM)
 
 
 def whole(shape):
@@ -279,41 +343,60 @@
     me = lax.axis_index("seq") % 2
     grp = lax.axis_index("grp")
 
-    def pick(array, group, start=0, count=rows):
-        return lax.dynamic_slice(array, (group, start, 0), (1, count, width))[0]
-
-    same0 = seq_swap(pick(q_inv, me, 0, first), 2)
-    cross0 = seq_swap(pick(q_inv, 1 - me, 0, first), 3)
-    kx = seq_swap(pick(k_inv, 1 - me), 1)
-    vx = seq_swap(pick(v_inv, 1 - me), 1)
-    qx = seq_swap(pick(q_inv, 1 - me), 1)
-
-    mine = 2 * grp + me
-    others = (mine, 2 * grp + 1 - me, 2 * (1 - grp) + me, 2 * (1 - grp) + 1 - me)
-    ids = jnp.stack([me] + [group_ids[n] for n in others]).astype(jnp.int32)
+    place = me.reshape(1).astype(jnp.int32)
+    side = grp.reshape(1).astype(jnp.int32)
+    scalar = pl.BlockSpec(memory_space=pltpu.SMEM)
+    remain = pl.BlockSpec(memory_space=pltpu.HBM)
+    ahead, behind = pl.pallas_call(
+        first_kernel,
+        in_specs=[scalar, remain],
+        out_specs=[remain] * 2,
+        out_shape=[pltpu.HBM((first, width), jnp.bfloat16)] * 2,
+        scratch_shapes=[pltpu.SemaphoreType.DMA((2,))],
+        compiler_params=LIMIT,
+        name="first",
+    )(place, stay(q_inv))
+    same0 = seq_swap(ahead, 2)
+    cross0 = seq_swap(behind, 3)
+    late_same, late_cross, bundle = pl.pallas_call(
+        second_kernel,
+        in_specs=[scalar, remain, remain, remain],
+        out_specs=[remain] * 3,
+        out_shape=[
+            pltpu.HBM((rows - first, width), jnp.bfloat16),
+            pltpu.HBM((rows - first, width), jnp.bfloat16),
+            pltpu.HBM((3, rows, width), jnp.bfloat16),
+        ],
+        scratch_shapes=[pltpu.SemaphoreType.DMA((5,))],
+        compiler_params=LIMIT,
+        name="second",
+    )(place, stay(q_inv), stay(k_inv), stay(v_inv))
+    bundle = seq_swap(bundle, 1)
 
     cols = STEP_HEADS * HD
     steps = heads // STEP_HEADS
-    picked = pl.BlockSpec((None, rows, cols), lambda g, s: (s[0], 0, g))
-    plain = pl.BlockSpec((rows, cols), lambda g, s: (0, g))
-    reads = pl.BlockSpec((STEP_HEADS, 80, 2 * rows), lambda g, s: (g, 0, 0))
+    picked = pl.BlockSpec((None, rows, cols), lambda g, m, *_: (m[0], 0, g))
+    given = [
+        pl.BlockSpec((None, rows, cols), lambda g, *_, n=n: (n, 0, g)) for n in range(3)
+    ]
+    reads = pl.BlockSpec((STEP_HEADS, 80, 2 * rows), lambda g, *_: (g, 0, 0))
     vw, mean, level = pl.pallas_call(
         local_kernel,
         grid_spec=pltpu.PrefetchScalarGridSpec(
-            num_scalar_prefetch=1,
+            num_scalar_prefetch=3,
             grid=(steps,),
             in_specs=[
                 picked,
-                plain,
+                given[0],
                 picked,
-                plain,
+                given[1],
                 picked,
-                plain,
-                pl.BlockSpec((None, patch, cols), lambda g, s: (s[1], 0, g)),
+                given[2],
+                pl.BlockSpec((None, patch, cols), lambda g, m, r, t: (t[2 * r[0] + m[0]], 0, g)),
             ],
             out_specs=[
                 reads,
-                pl.BlockSpec((STEP_HEADS, 64, 2 * rows), lambda g, s: (g, 0, 0)),
+                pl.BlockSpec((STEP_HEADS, 64, 2 * rows), lambda g, *_: (g, 0, 0)),
                 whole((heads, 2 * rows)),
             ],
         ),
@@ -324,10 +407,19 @@
         ],
         compiler_params=LIMIT,
         name="local",
-    )(ids, q_inv, qx, k_inv, kx, v_inv, vx, jnp.swapaxes(w_attr, 1, 2))
-
-    late_same = pick(q_inv, me, first, rows - first)
-    late_cross = pick(q_inv, 1 - me, first, rows - first)
+    )(
+        place,
+        side,
+        group_ids,
+        stay(q_inv),
+        bundle,
+        stay(k_inv),
+        bundle,
+        stay(v_inv),
+        bundle,
+        stay(jnp.swapaxes(w_attr, 1, 2)),
+    )
+
     level, late_same, late_cross = lax.optimization_barrier((level, late_same, late_cross))
     home = seq_swap(level, 2)
     same1 = seq_swap(late_same, 2)
@@ -336,10 +428,17 @@
     lighting = jnp.take(env_table, env_ids, axis=0)
     strips = model // CHUNK
     weights = [
-        pl.BlockSpec((None, patch, CHUNK), lambda g, s, n=n: (s[1 + n], 0, g))
+        pl.BlockSpec(
+            (None, patch, CHUNK),
+            lambda g, m, r, t, n=n: (
+                t[2 * (r[0] if n < 2 else 1 - r[0]) + (1 - m[0] if n % 2 else m[0])],
+                0,
+                g,
+            ),
+        )
         for n in range(4)
     ]
-    strip = lambda count: pl.BlockSpec((count, CHUNK), lambda g, s: (0, g))
+    strip = lambda count: pl.BlockSpec((count, CHUNK), lambda g, *_: (0, g))
     kinds = 4 * patch
     inputs = kinds + channels
     out_shapes = [
@@ -352,7 +451,7 @@
     prepared = pl.pallas_call(
         prepare_kernel,
         grid_spec=pltpu.PrefetchScalarGridSpec(
-            num_scalar_prefetch=1,
+            num_scalar_prefetch=3,
             grid=(strips,),
             in_specs=weights
             + [
@@ -375,7 +474,9 @@
         compiler_params=LIMIT,
         name="prepare",
     )(
-        ids,
+        place,
+        side,
+        group_ids,
         w_embed_attr,
         w_embed_attr,
         w_embed_attr,
@@ -390,7 +491,7 @@
     def remote(same, crossed, spans, lane):
         count = same.shape[0]
         wide = 2 * count
-        block = pl.BlockSpec((count, cols), lambda g, s: (0, g))
+        block = pl.BlockSpec((count, cols), lambda g, m: (0, g))
         sent = pl.pallas_call(
             lambda *refs: remote_kernel(spans, *refs),
             grid_spec=pltpu.PrefetchScalarGridSpec(
@@ -400,9 +501,9 @@
                     block,
                     block,
                     picked,
-                    plain,
+                    given[1],
                     reads,
-                    pl.BlockSpec((heads, wide), lambda g, s: (0, lane)),
+                    pl.BlockSpec((heads, wide), lambda g, m: (0, lane)),
                 ],
                 out_specs=whole((64 + heads, wide)),
                 scratch_shapes=[
@@ -413,7 +514,7 @@
             out_shape=jax.ShapeDtypeStruct((64 + heads, wide), jnp.bfloat16),
             compiler_params=LIMIT,
             name="remote",
-        )(ids, same, crossed, k_inv, kx, vw, home)
+        )(place, same, crossed, k_inv, bundle, vw, home)
         return seq_swap(sent, 2)
 
     back0 = remote(same0, cross0, ((0, 128), (128, 192)), 0)
@@ -447,7 +548,7 @@
         ],
         compiler_params=LIMIT,
         name="render",
-    )(ids, *resident(own, a1, a2, a3, *prepared))
+    )(place, *resident(own, a1, a2, a3, *prepared))
     return (jnp.swapaxes(attrs, 1, 2), jnp.swapaxes(rendered, 1, 2))
 
 

time: 113 us -> 255 us (2.26)
  Pallas kernels: 67 us -> 218 us
  local copies, waits for them, and re-layouts: 20.3 us -> 1.41 us
  waiting for transfers between devices: 11.8 us -> 22 us
    pallas_call x0 -> x2, Pallas kernels: none -> 161 us  [the longest x1 112 us: on_device(): pl.pallas_call(second_kernel, in_specs=[scalar, remain, remain, remain],...]
    ppermute x11 -> x9, waiting for transfers between devices: 11.8 us -> 22 us  [seq_swap(): return lax.ppermute(block, 'seq', [(i, i ^ flip) for i in range(count)])]
    squeeze x5 -> x0, local copies, waits for them, and re-layouts: 8.37 us -> none  [pick(): return lax.dynamic_slice(array, (group, start, 0), (1, count, width))[0]]
    unnamed x31 -> x23, local copies, waits for them, and re-layouts: 7.38 us -> 0.07 us
    pallas_call x2, Pallas kernels: 32.6 us -> 26.9 us  [remote(): pl.pallas_call(lambda *refs: remote_kernel(spans, *refs), grid_spec=pltpu...]
    pallas_call x1, Pallas kernels: 26.5 us -> 22 us  [on_device(): pl.pallas_call(local_kernel, grid_spec=pltpu.PrefetchScalarGridSpec(num_s...]
    another operation x1 -> x0, local copies, waits for them, and re-layouts: 2.59 us -> none  [on_device(): ids = jnp.stack([me] + [group_ids[n] for n in others]).astype(jnp.int32)]
    ppermute x11 -> x9, starting transfers between devices: 10.8 us -> 11.1 us  [seq_swap(): return lax.ppermute(block, 'seq', [(i, i ^ flip) for i in range(count)])]
  transfers between devices with their start and end apart: 13 -> 11, of which waited for: 1 -> 2; matrix products, arithmetic and copies ran while one was open for 9% -> 1% of each run, Pallas kernels for 58% -> 41%
where the time goes in v3:
time: 255 us
  Pallas kernels  218 us (85%)
  waiting for transfers between devices  22 us (9%)
  starting transfers between devices  12.6 us (5%)
    pallas_call x1, Pallas kernels, on_device(): pl.pallas_call(second_kernel, in_specs=[scalar, remain, remain, remain],...  112 us
    pallas_call x1, Pallas kernels, on_device(): pl.pallas_call(first_kernel, in_specs=[scalar, remain], out_specs=[remain...  48.8 us
    pallas_call x2, Pallas kernels, remote(): pl.pallas_call(lambda *refs: remote_kernel(spans, *refs), grid_spec=pltpu...  26.9 us
    pallas_call x1, Pallas kernels, on_device(): pl.pallas_call(local_kernel, grid_spec=pltpu.PrefetchScalarGridSpec(num_s...  22 us
    ppermute x9, waiting for transfers between devices, seq_swap(): return lax.ppermute(block, 'seq', [(i, i ^ flip) for i in range(count)])  22 us
    ppermute x9, starting transfers between devices, seq_swap(): return lax.ppermute(block, 'seq', [(i, i ^ flip) for i in range(count)])  11.1 us
    pallas_call x1, Pallas kernels, on_device(): pl.pallas_call(prepare_kernel, grid_spec=pltpu.PrefetchScalarGridSpec(num...  6.24 us
  transfers between devices with their start and end apart: 11, of which 2 were waited for; matrix products, arithmetic and copies ran while one was open for 1% of the time, Pallas kernels for 41%

profile of v3, /device:TPU:1, one launch (start us, length us, event | category | flops | bytes accessed | tf_op | source)
XLA Modules:
  0.0 254.6 jit_solution(9150391927644105727)
XLA Ops:
  0.6 0.0 copy-start
  0.7 112.3 %second.1 = (bf16[64,2048]{1,0:T(8,128)(2,1)}, bf16[64,2048]{1,0:T(8,128)(2,1)}, bf16[3,256,2048]{2,1,0:T(8,128)(2,1)}) custom-call(s32[1]{0:T(128)} %bitcast.place.me.refs_0_, bf16[2,256,2048]{2,1,0:T(8,128)(2,1)} %q.5, bf16[2,256,2048]{2,1,0:T(8,128)(2,1)} %refs_3_.3, bf16[2,256,2048]{2,1,0:T(8,128)(2,1)} %v.3), custom_call_target="tpu_custom_call" | custom-call | tf_op jit(solution)/shard_map/second/pallas_call | solution.py:361
  113.0 0.0 copy-start.7
  113.0 3.3 %collective-permute-start = (bf16[3,256,2048]{2,1,0:T(8,128)(2,1)}, bf16[3,256,2048]{2,1,0:T(8,128)(2,1)}, u32[]{:S(2)}, u32[]{:S(2)}) collective-permute-start(bf16[3,256,2048]{2,1,0:T(8,128)(2,1)} %get-tuple-element.22), channel_id=1, source_target_pairs={{0,1},{1,0},{2,3},{3,2},{4,5},{5,4},{6,7},{7,6},{8,9},{9,8},{10,11... | collective-permute-start | bytes 9437192 | tf_op jit(solution)/shard_map/ppermute | solution.py:22
  116.3 48.8 %first.1 = (bf16[192,2048]{1,0:T(8,128)(2,1)}, bf16[192,2048]{1,0:T(8,128)(2,1)}) custom-call(s32[1]{0:T(128)} %bitcast.place.me.refs_0_, bf16[2,256,2048]{2,1,0:T(8,128)(2,1)} %q.5), custom_call_target="tpu_custom_call" | custom-call | tf_op jit(solution)/shard_map/first/pallas_call | solution.py:350
  165.1 0.1 collective-permute-start.5
  165.2 1.6 collective-permute-start.6
  166.8 0.0 copy-start.8
  166.8 0.0 copy-start.1
  166.8 22.0 %local.1 = (bf16[16,80,512]{2,1,0:T(8,128)(2,1)S(1)}, f32[16,64,512]{2,1,0:T(8,128)S(1)}, f32[16,512]{1,0:T(8,128)S(1)}) custom-call(s32[1]{0:T(128)} %bitcast.place.me.refs_0_, s32[1]{0:T(128)} %bitcast.1.grp, s32[4]{0:T(128)S(1)} %copy-done.7, bf16[2,256,2048]{2,1,0:T(8,128)(2,1)} %q.5, bf16[3,256,2048]{2,1,0:T(8,128)(2,1)} %collective-permute-done.qx.kx.vx.refs_4_, ...), custom_call_target="tpu_custom_call" | custom-call | tf_op jit(solution)/shard_map/local/pallas_call | solution.py:383
  188.9 0.1 collective-permute-start.1
  189.0 1.8 collective-permute-start.2
  190.8 0.1 collective-permute-start.3
  190.9 11.1 %collective-permute-done.6.refs_2_ = bf16[192,2048]{1,0:T(8,128)(2,1)} collective-permute-done((bf16[192,2048]{1,0:T(8,128)(2,1)}, bf16[192,2048]{1,0:T(8,128)(2,1)}, u32[]{:S(2)}, u32[]{:S(2)}) %collective-permute-start.6) | collective-permute-done | bytes 786464 | tf_op jit(solution)/shard_map/ppermute | solution.py:22
  202.1 10.9 %collective-permute-done.3.refs_6_ = f32[16,512]{1,0:T(8,128)S(1)} collective-permute-done((f32[16,512]{1,0:T(8,128)S(1)}, f32[16,512]{1,0:T(8,128)S(1)}, u32[]{:S(2)}, u32[]{:S(2)}) %collective-permute-start.3) | collective-permute-done | bytes 32800 | tf_op jit(solution)/shard_map/ppermute | solution.py:22
  212.9 18.2 %remote.3 = bf16[80,384]{1,0:T(8,128)(2,1)S(1)} custom-call(s32[1]{0:T(128)} %bitcast.place.me.refs_0_, bf16[192,2048]{1,0:T(8,128)(2,1)} %collective-permute-done.5.refs_1_, bf16[192,2048]{1,0:T(8,128)(2,1)} %collective-permute-done.6.refs_2_, bf16[2,256,2048]{2,1,0:T(8,128)(2,1)S(1)} %copy-done.1, ...), custom_call_target="tpu_custom_call" | custom-call | tf_op jit(solution)/shard_map/remote/pallas_call | solution.py:495
  231.2 0.2 collective-permute-start.7
  231.4 8.7 %remote.2 = bf16[80,128]{1,0:T(8,128)(2,1)S(1)} custom-call(s32[1]{0:T(128)} %bitcast.place.me.refs_0_, bf16[64,2048]{1,0:T(8,128)(2,1)S(1)} %collective-permute-done.1.refs_1_, bf16[64,2048]{1,0:T(8,128)(2,1)S(1)} %collective-permute-done.2.refs_2_, bf16[2,256,2048]{2,1,0:T(8,128)(2,1)S(1)} %copy-done.1, ...), custom_call_target="tpu_custom_call" | custom-call | tf_op jit(solution)/shard_map/remote/pallas_call | solution.py:495
  240.0 1.6 collective-permute-start.4
  241.7 1.3 gather_fusion
  243.1 0.0 copy-start.2
  243.1 0.0 copy-start.3
  243.1 0.0 copy-start.5
  243.1 0.0 copy-start.6
  243.1 0.1 early.1
  243.3 0.2 merge.1
  243.4 2.3 collective-permute-start.8
  245.7 1.2 collective-permute-start.10
  246.9 0.2 collective-permute-start.9
  247.2 0.1 broadcast_select_fusion.light
  247.3 6.2 %prepare.1 = (bf16[768,256]{1,0:T(8,128)(2,1)S(1)}, f32[2,256,256]{2,1,0:T(8,128)S(1)}, f32[2,64,256]{2,1,0:T(8,128)S(1)}, f32[2,8,256]{2,1,0:T(8,128)S(1)}, f32[2,64,128]{2,1,0:T(8,128)S(1)}) custom-call(s32[1]{0:T(128)} %bitcast.place.me.refs_0_, s32[1]{0:T(128)} %bitcast.1.grp, s32[4]{0:T(128)S(1)} %copy-done.7, bf16[4,64,4096]{2,1,0:T(8,128)(2,1)S(1)} %copy-done.2, ...), custom_call_target="tpu_custom_call" | custom-call | tf_op jit(solution)/shard_map/prepare/pallas_call | solution.py:451
  253.6 1.0 render.1
  (27 shorter events, 0.1 us)
Async XLA Ops:
  0.6 241.1 %copy-start = (bf16[4096,128]{1,0:T(8,128)(2,1)S(1)}, bf16[4096,128]{1,0:T(8,128)(2,1)}, u32[]{:S(2)}) copy-start(bf16[4096,128]{1,0:T(8,128)(2,1)} %param.18) | copy-start | bytes 3145732
  113.0 53.8 %copy-start.7 = (s32[4]{0:T(128)S(1)}, s32[4]{0:T(128)}, u32[]{:S(2)}) copy-start(s32[4]{0:T(128)} %kinds.3) | copy-start | bytes 52
  113.0 53.8 %collective-permute-start = (bf16[3,256,2048]{2,1,0:T(8,128)(2,1)}, bf16[3,256,2048]{2,1,0:T(8,128)(2,1)}, u32[]{:S(2)}, u32[]{:S(2)}) collective-permute-start(bf16[3,256,2048]{2,1,0:T(8,128)(2,1)} %get-tuple-element.22), channel_id=1, source_target_pairs={{0,1},{1,0},{2,3},{3,2},{4,5},{5,4},{6,7},{7,6},{8,9},{9,8},{10,11... | collective-permute-start | bytes 9437192 | tf_op jit(solution)/shard_map/ppermute | solution.py:22
  165.1 25.9 %collective-permute-start.5 = (bf16[192,2048]{1,0:T(8,128)(2,1)}, bf16[192,2048]{1,0:T(8,128)(2,1)}, u32[]{:S(2)}, u32[]{:S(2)}) collective-permute-start(bf16[192,2048]{1,0:T(8,128)(2,1)} %get-tuple-element.31), channel_id=1, source_target_pairs={{0,2},{1,3},{2,0},{3,1},{4,6},{5,7},{6,4},{7,5},{8,10},{9,11},{10,... | collective-permute-start | bytes 2359304 | tf_op jit(solution)/shard_map/ppermute | solution.py:22
  165.2 36.9 %collective-permute-start.6 = (bf16[192,2048]{1,0:T(8,128)(2,1)}, bf16[192,2048]{1,0:T(8,128)(2,1)}, u32[]{:S(2)}, u32[]{:S(2)}) collective-permute-start(bf16[192,2048]{1,0:T(8,128)(2,1)} %get-tuple-element.32), channel_id=1, source_target_pairs={{0,3},{1,2},{2,1},{3,0},{4,7},{5,6},{6,5},{7,4},{8,11},{9,10},{10,... | collective-permute-start | bytes 2359304 | tf_op jit(solution)/shard_map/ppermute | solution.py:22
  166.8 22.1 %copy-start.10 = (bf16[64,2048]{1,0:T(8,128)(2,1)S(1)}, bf16[64,2048]{1,0:T(8,128)(2,1)}, u32[]{:S(2)}) copy-start(bf16[64,2048]{1,0:T(8,128)(2,1)} %get-tuple-element.26) | copy-start | bytes 786436
  166.8 22.2 %copy-start.9 = (bf16[64,2048]{1,0:T(8,128)(2,1)S(1)}, bf16[64,2048]{1,0:T(8,128)(2,1)}, u32[]{:S(2)}) copy-start(bf16[64,2048]{1,0:T(8,128)(2,1)} %get-tuple-element.27) | copy-start | bytes 786436
  166.8 24.0 %copy-start.8 = (s32[2,256]{1,0:T(2,128)S(1)}, s32[2,256]{1,0:T(2,128)}, u32[]{:S(2)}) copy-start(s32[2,256]{1,0:T(2,128)} %param.17) | copy-start | bytes 6148
  166.8 46.1 %copy-start.1 = (bf16[2,256,2048]{2,1,0:T(8,128)(2,1)S(1)}, bf16[2,256,2048]{2,1,0:T(8,128)(2,1)}, u32[]{:S(2)}) copy-start(bf16[2,256,2048]{2,1,0:T(8,128)(2,1)} %refs_3_.3) | copy-start | bytes 6291460
  188.9 42.5 %collective-permute-start.1 = (bf16[64,2048]{1,0:T(8,128)(2,1)S(1)}, bf16[64,2048]{1,0:T(8,128)(2,1)S(1)}, u32[]{:S(2)}, u32[]{:S(2)}) collective-permute-start(bf16[64,2048]{1,0:T(8,128)(2,1)S(1)} %copy-done.10), channel_id=1, source_target_pairs={{0,2},{1,3},{2,0},{3,1},{4,6},{5,7},{6,4},{7,5},{8,10},{9,11},{10,... | collective-permute-start | bytes 786440 | tf_op jit(solution)/shard_map/ppermute | solution.py:22
  189.0 42.4 %collective-permute-start.2 = (bf16[64,2048]{1,0:T(8,128)(2,1)S(1)}, bf16[64,2048]{1,0:T(8,128)(2,1)S(1)}, u32[]{:S(2)}, u32[]{:S(2)}) collective-permute-start(bf16[64,2048]{1,0:T(8,128)(2,1)S(1)} %copy-done.9), channel_id=1, source_target_pairs={{0,3},{1,2},{2,1},{3,0},{4,7},{5,6},{6,5},{7,4},{8,11},{9,10},{10,... | collective-permute-start | bytes 786440 | tf_op jit(solution)/shard_map/ppermute | solution.py:22
  190.8 22.1 %collective-permute-start.3 = (f32[16,512]{1,0:T(8,128)S(1)}, f32[16,512]{1,0:T(8,128)S(1)}, u32[]{:S(2)}, u32[]{:S(2)}) collective-permute-start(f32[16,512]{1,0:T(8,128)S(1)} %get-tuple-element.29), channel_id=1, source_target_pairs={{0,2},{1,3},{2,0},{3,1},{4,6},{5,7},{6,4},{7,5},{8,10},{9,11},{10,... | collective-permute-start | bytes 98312 | tf_op jit(solution)/shard_map/ppermute | solution.py:22
  231.2 11.9 %collective-permute-start.7 = (bf16[80,384]{1,0:T(8,128)(2,1)S(1)}, bf16[80,384]{1,0:T(8,128)(2,1)S(1)}, u32[]{:S(2)}, u32[]{:S(2)}) collective-permute-start(bf16[80,384]{1,0:T(8,128)(2,1)S(1)} %remote.3), channel_id=1, source_target_pairs={{0,2},{1,3},{2,0},{3,1},{4,6},{5,7},{6,4},{7,5},{8,10},{9,11},{10,... | collective-permute-start | bytes 184328 | tf_op jit(solution)/shard_map/ppermute | solution.py:22
  240.0 3.2 %collective-permute-start.4 = (bf16[80,128]{1,0:T(8,128)(2,1)S(1)}, bf16[80,128]{1,0:T(8,128)(2,1)S(1)}, u32[]{:S(2)}, u32[]{:S(2)}) collective-permute-start(bf16[80,128]{1,0:T(8,128)(2,1)S(1)} %remote.2), channel_id=1, source_target_pairs={{0,2},{1,3},{2,0},{3,1},{4,6},{5,7},{6,4},{7,5},{8,10},{9,11},{10,... | collective-permute-start | bytes 61448 | tf_op jit(solution)/shard_map/ppermute | solution.py:22
  243.1 4.2 %copy-start.2 = (bf16[4,64,4096]{2,1,0:T(8,128)(2,1)S(1)}, bf16[4,64,4096]{2,1,0:T(8,128)(2,1)}, u32[]{:S(2)}) copy-start(bf16[4,64,4096]{2,1,0:T(8,128)(2,1)} %w3.1) | copy-start | bytes 6291460
  243.1 4.2 %copy-start.3 = (bf16[128,4096]{1,0:T(8,128)(2,1)S(1)}, bf16[128,4096]{1,0:T(8,128)(2,1)}, u32[]{:S(2)}) copy-start(bf16[128,4096]{1,0:T(8,128)(2,1)} %w_env.1) | copy-start | bytes 3145732
  243.1 4.2 %copy-start.4 = (bf16[4096,64]{0,1:T(8,128)(2,1)S(1)}, bf16[4096,64]{0,1:T(8,128)(2,1)}, u32[]{:S(2)}) copy-start(bf16[4096,64]{0,1:T(8,128)(2,1)} %param.23) | copy-start | bytes 1572868
  243.1 4.2 %copy-start.5 = (bf16[2,4096]{1,0:T(2,128)(2,1)S(1)}, bf16[2,4096]{1,0:T(2,128)(2,1)}, u32[]{:S(2)}) copy-start(bf16[2,4096]{1,0:T(2,128)(2,1)} %scale.1) | copy-start | bytes 49156
  243.1 4.2 %copy-start.6 = (bf16[2,4096]{1,0:T(2,128)(2,1)S(1)}, bf16[2,4096]{1,0:T(2,128)(2,1)}, u32[]{:S(2)}) copy-start(bf16[2,4096]{1,0:T(2,128)(2,1)} %shift.1) | copy-start | bytes 49156
  243.4 10.2 %collective-permute-start.8 = (bf16[64,256]{1,0:T(8,128)(2,1)S(1)}, bf16[64,256]{1,0:T(8,128)(2,1)S(1)}, u32[]{:S(2)}, u32[]{:S(2)}) collective-permute-start(bf16[64,256]{1,0:T(8,128)(2,1)S(1)} %get-tuple-element.34), channel_id=1, source_target_pairs={{0,1},{1,0},{2,3},{3,2},{4,5},{5,4},{6,7},{7,6},{8,9},{9,8},{10,11... | collective-permute-start | bytes 98312 | tf_op jit(solution)/shard_map/ppermute | solution.py:22
  245.7 7.9 %collective-permute-start.10 = (bf16[64,256]{1,0:T(8,128)(2,1)S(1)}, bf16[64,256]{1,0:T(8,128)(2,1)S(1)}, u32[]{:S(2)}, u32[]{:S(2)}) collective-permute-start(bf16[64,256]{1,0:T(8,128)(2,1)S(1)} %get-tuple-element.34), channel_id=1, source_target_pairs={{0,129},{1,128},{2,131},{3,130},{4,133},{5,132},{6,135},{7,134},{8... | collective-permute-start | bytes 98312 | tf_op jit(solution)/shard_map/ppermute | solution.py:34
  246.9 6.7 %collective-permute-start.9 = (bf16[64,256]{1,0:T(8,128)(2,1)S(1)}, bf16[64,256]{1,0:T(8,128)(2,1)S(1)}, u32[]{:S(2)}, u32[]{:S(2)}) collective-permute-start(bf16[64,256]{1,0:T(8,128)(2,1)S(1)} %get-tuple-element.33.a0), channel_id=1, source_target_pairs={{0,128},{128,0},{1,129},{129,1},{2,130},{130,2},{3,131},{131,3},{4... | collective-permute-start | bytes 98312 | tf_op jit(solution)/shard_map/ppermute | solution.py:26

commit v4 on v3

--- a/solution.py
+++ b/solution.py
@@ -89,35 +89,43 @@
     return jnp.max(largest)
 
 
-def first_kernel(place, q, same, cross, sems):
+def shuttle(pieces, arrive, leave):
+    inward = [
+        pltpu.make_async_copy(source, held, arrive.at[n])
+        for n, (source, held, _) in enumerate(pieces)
+    ]
+    outward = [
+        pltpu.make_async_copy(held, target, leave.at[n])
+        for n, (_, held, target) in enumerate(pieces)
+    ]
+    for copy in inward:
+        copy.start()
+    for here, there in zip(inward, outward):
+        here.wait()
+        there.start()
+    for copy in outward:
+        copy.wait()
+
+
+def first_kernel(place, q, same, cross, held, arrive, leave):
+    me = place[0]
+    count = same.shape[0] // 2
+    pieces = []
+    for n, (group, target) in enumerate(((me, same), (1 - me, cross))):
+        for half in range(2):
+            span = pl.ds(half * count, count)
+            pieces.append((q.at[group, span], held.at[n, span], target.at[span]))
+    shuttle(pieces, arrive, leave)
+
+
+def second_kernel(place, q, k, v, same, cross, bundle, held, rest, arrive, leave):
     me = place[0]
     count = same.shape[0]
-    copies = [
-        pltpu.make_async_copy(q.at[me, pl.ds(0, count)], same, sems.at[0]),
-        pltpu.make_async_copy(q.at[1 - me, pl.ds(0, count)], cross, sems.at[1]),
-    ]
-    for copy in copies:
-        copy.start()
-    for copy in copies:
-        copy.wait()
-
-
-def second_kernel(place, q, k, v, same, cross, bundle, sems):
-    me = place[0]
-    count = same.shape[0]
-    rest = pl.ds(q.shape[1] - count, count)
-    copies = [
-        pltpu.make_async_copy(a.at[1 - me], bundle.at[n], sems.at[n])
-        for n, a in enumerate((q, k, v))
-    ]
-    copies += [
-        pltpu.make_async_copy(q.at[me, rest], same, sems.at[3]),
-        pltpu.make_async_copy(q.at[1 - me, rest], cross, sems.at[4]),
-    ]
-    for copy in copies:
-        copy.start()
-    for copy in copies:
-        copy.wait()
+    tail = pl.ds(q.shape[1] - count, count)
+    pieces = [(a.at[1 - me], held.at[n], bundle.at[n]) for n, a in enumerate((q, k, v))]
+    pieces.append((q.at[me, tail], rest.at[0], same))
+    pieces.append((q.at[1 - me, tail], rest.at[1], cross))
+    shuttle(pieces, arrive, leave)
 
 
 def local_kernel(me, grp, kinds, q, qx, k, kx, v, vx, w, vw, mean, level):
@@ -352,7 +360,8 @@
         in_specs=[scalar, remain],
         out_specs=[remain] * 2,
         out_shape=[pltpu.HBM((first, width), jnp.bfloat16)] * 2,
-        scratch_shapes=[pltpu.SemaphoreType.DMA((2,))],
+        scratch_shapes=[pltpu.VMEM((2, first, width), jnp.bfloat16)]
+        + [pltpu.SemaphoreType.DMA((4,))] * 2,
         compiler_params=LIMIT,
         name="first",
     )(place, stay(q_inv))
@@ -367,7 +376,11 @@
             pltpu.HBM((rows - first, width), jnp.bfloat16),
             pltpu.HBM((3, rows, width), jnp.bfloat16),
         ],
-        scratch_shapes=[pltpu.SemaphoreType.DMA((5,))],
+        scratch_shapes=[
+            pltpu.VMEM((3, rows, width), jnp.bfloat16),
+            pltpu.VMEM((2, rows - first, width), jnp.bfloat16),
+        ]
+        + [pltpu.SemaphoreType.DMA((5,))] * 2,
         compiler_params=LIMIT,
         name="second",
     )(place, stay(q_inv), stay(k_inv), stay(v_inv))

time: 255 us -> 99.2 us (0.39)
  Pallas kernels: 218 us -> 61.9 us
    pallas_call x1, Pallas kernels: 112 us -> 3.27 us  [on_device(): pl.pallas_call(second_kernel, in_specs=[scalar, remain, remain, remain],...]
    pallas_call x1, Pallas kernels: 48.8 us -> 2.21 us  [on_device(): pl.pallas_call(first_kernel, in_specs=[scalar, remain], out_specs=[remain...]
  transfers between devices with their start and end apart: 11 -> 11, of which waited for: 2 -> 3; matrix products, arithmetic and copies ran while one was open for 1% -> 2% of each run, Pallas kernels for 41% -> 58%
where the time goes in v4:
time: 99.2 us; the launch traced here: 99 us
  Pallas kernels  61.9 us (62%)
  waiting for transfers between devices  21.9 us (22%)
  starting transfers between devices  12.7 us (13%)
  local copies, waits for them, and re-layouts  1.41 us (1%)
    pallas_call x2, Pallas kernels, remote(): pl.pallas_call(lambda *refs: remote_kernel(spans, *refs), grid_spec=pltpu...  26.9 us
    pallas_call x1, Pallas kernels, on_device(): pl.pallas_call(local_kernel, grid_spec=pltpu.PrefetchScalarGridSpec(num_s...  22 us
    ppermute x9, waiting for transfers between devices, seq_swap(): return lax.ppermute(block, 'seq', [(i, i ^ flip) for i in range(count)])  21.9 us
    ppermute x9, starting transfers between devices, seq_swap(): return lax.ppermute(block, 'seq', [(i, i ^ flip) for i in range(count)])  11.2 us
    pallas_call x1, Pallas kernels, on_device(): pl.pallas_call(prepare_kernel, grid_spec=pltpu.PrefetchScalarGridSpec(num...  6.24 us
    pallas_call x1, Pallas kernels, on_device(): pl.pallas_call(second_kernel, in_specs=[scalar, remain, remain, remain],...  3.27 us
    pallas_call x1, Pallas kernels, on_device(): pl.pallas_call(first_kernel, in_specs=[scalar, remain], out_specs=[remain...  2.21 us
  transfers between devices with their start and end apart: 11, of which 3 were waited for; matrix products, arithmetic and copies ran while one was open for 2% of the time, Pallas kernels for 58%

profile of v4, /device:TPU:1, one launch (start us, length us, event | category | flops | bytes accessed | tf_op | source)
XLA Modules:
  0.0 99.0 jit_solution(10033718543730890796)
XLA Ops:
  0.6 0.0 copy-start
  0.7 3.3 %second.1 = (bf16[64,2048]{1,0:T(8,128)(2,1)}, bf16[64,2048]{1,0:T(8,128)(2,1)}, bf16[3,256,2048]{2,1,0:T(8,128)(2,1)}) custom-call(s32[1]{0:T(128)} %bitcast.place.me.refs_0_, bf16[2,256,2048]{2,1,0:T(8,128)(2,1)} %q.5, bf16[2,256,2048]{2,1,0:T(8,128)(2,1)} %refs_3_.3, bf16[2,256,2048]{2,1,0:T(8,128)(2,1)} %v.3), custom_call_target="tpu_custom_call" | custom-call | tf_op jit(solution)/shard_map/second/pallas_call | solution.py:370
  3.9 0.0 copy-start.7
  3.9 3.3 %collective-permute-start = (bf16[3,256,2048]{2,1,0:T(8,128)(2,1)}, bf16[3,256,2048]{2,1,0:T(8,128)(2,1)}, u32[]{:S(2)}, u32[]{:S(2)}) collective-permute-start(bf16[3,256,2048]{2,1,0:T(8,128)(2,1)} %get-tuple-element.22), channel_id=1, source_target_pairs={{0,1},{1,0},{2,3},{3,2},{4,5},{5,4},{6,7},{7,6},{8,9},{9,8},{10,11... | collective-permute-start | bytes 9437192 | tf_op jit(solution)/shard_map/ppermute | solution.py:22
  7.2 2.2 %first.1 = (bf16[192,2048]{1,0:T(8,128)(2,1)}, bf16[192,2048]{1,0:T(8,128)(2,1)}) custom-call(s32[1]{0:T(128)} %bitcast.place.me.refs_0_, bf16[2,256,2048]{2,1,0:T(8,128)(2,1)} %q.5), custom_call_target="tpu_custom_call" | custom-call | tf_op jit(solution)/shard_map/first/pallas_call | solution.py:358
  9.5 0.1 collective-permute-start.5
  9.6 1.6 %collective-permute-start.6 = (bf16[192,2048]{1,0:T(8,128)(2,1)}, bf16[192,2048]{1,0:T(8,128)(2,1)}, u32[]{:S(2)}, u32[]{:S(2)}) collective-permute-start(bf16[192,2048]{1,0:T(8,128)(2,1)} %get-tuple-element.32), channel_id=1, source_target_pairs={{0,3},{1,2},{2,1},{3,0},{4,7},{5,6},{6,5},{7,4},{8,11},{9,10},{10,... | collective-permute-start | bytes 2359304 | tf_op jit(solution)/shard_map/ppermute | solution.py:22
  11.2 1.7 %collective-permute-done.qx.kx.vx.refs_4_ = bf16[3,256,2048]{2,1,0:T(8,128)(2,1)} collective-permute-done((bf16[3,256,2048]{2,1,0:T(8,128)(2,1)}, bf16[3,256,2048]{2,1,0:T(8,128)(2,1)}, u32[]{:S(2)}, u32[]{:S(2)}) %collective-permute-start) | collective-permute-done | bytes 3145760 | tf_op jit(solution)/shard_map/ppermute | solution.py:22
  12.9 0.0 copy-start.1
  12.9 22.0 %local.1 = (bf16[16,80,512]{2,1,0:T(8,128)(2,1)S(1)}, f32[16,64,512]{2,1,0:T(8,128)S(1)}, f32[16,512]{1,0:T(8,128)S(1)}) custom-call(s32[1]{0:T(128)} %bitcast.place.me.refs_0_, s32[1]{0:T(128)} %bitcast.1.grp, s32[4]{0:T(128)S(1)} %copy-done.7, bf16[2,256,2048]{2,1,0:T(8,128)(2,1)} %q.5, bf16[3,256,2048]{2,1,0:T(8,128)(2,1)} %collective-permute-done.qx.kx.vx.refs_4_, ...), custom_call_target="tpu_custom_call" | custom-call | tf_op jit(solution)/shard_map/local/pallas_call | solution.py:396
  34.9 0.1 collective-permute-start.1
  35.0 2.0 %collective-permute-start.2 = (bf16[64,2048]{1,0:T(8,128)(2,1)S(1)}, bf16[64,2048]{1,0:T(8,128)(2,1)S(1)}, u32[]{:S(2)}, u32[]{:S(2)}) collective-permute-start(bf16[64,2048]{1,0:T(8,128)(2,1)S(1)} %copy-done.9), channel_id=1, source_target_pairs={{0,3},{1,2},{2,1},{3,0},{4,7},{5,6},{6,5},{7,4},{8,11},{9,10},{10,... | collective-permute-start | bytes 786440 | tf_op jit(solution)/shard_map/ppermute | solution.py:22
  37.1 9.4 %collective-permute-done.6.refs_2_ = bf16[192,2048]{1,0:T(8,128)(2,1)} collective-permute-done((bf16[192,2048]{1,0:T(8,128)(2,1)}, bf16[192,2048]{1,0:T(8,128)(2,1)}, u32[]{:S(2)}, u32[]{:S(2)}) %collective-permute-start.6) | collective-permute-done | bytes 786464 | tf_op jit(solution)/shard_map/ppermute | solution.py:22
  46.5 10.9 %collective-permute-done.3.refs_6_ = f32[16,512]{1,0:T(8,128)S(1)} collective-permute-done((f32[16,512]{1,0:T(8,128)S(1)}, f32[16,512]{1,0:T(8,128)S(1)}, u32[]{:S(2)}, u32[]{:S(2)}) %collective-permute-start.3) | collective-permute-done | bytes 32800 | tf_op jit(solution)/shard_map/ppermute | solution.py:22
  57.3 18.2 %remote.3 = bf16[80,384]{1,0:T(8,128)(2,1)S(1)} custom-call(s32[1]{0:T(128)} %bitcast.place.me.refs_0_, bf16[192,2048]{1,0:T(8,128)(2,1)} %collective-permute-done.5.refs_1_, bf16[192,2048]{1,0:T(8,128)(2,1)} %collective-permute-done.6.refs_2_, bf16[2,256,2048]{2,1,0:T(8,128)(2,1)S(1)} %copy-done.1, ...), custom_call_target="tpu_custom_call" | custom-call | tf_op jit(solution)/shard_map/remote/pallas_call | solution.py:508
  75.6 0.2 collective-permute-start.7
  75.7 8.7 %remote.2 = bf16[80,128]{1,0:T(8,128)(2,1)S(1)} custom-call(s32[1]{0:T(128)} %bitcast.place.me.refs_0_, bf16[64,2048]{1,0:T(8,128)(2,1)S(1)} %collective-permute-done.1.refs_1_, bf16[64,2048]{1,0:T(8,128)(2,1)S(1)} %collective-permute-done.2.refs_2_, bf16[2,256,2048]{2,1,0:T(8,128)(2,1)S(1)} %copy-done.1, ...), custom_call_target="tpu_custom_call" | custom-call | tf_op jit(solution)/shard_map/remote/pallas_call | solution.py:508
  84.4 1.6 %collective-permute-start.4 = (bf16[80,128]{1,0:T(8,128)(2,1)S(1)}, bf16[80,128]{1,0:T(8,128)(2,1)S(1)}, u32[]{:S(2)}, u32[]{:S(2)}) collective-permute-start(bf16[80,128]{1,0:T(8,128)(2,1)S(1)} %remote.2), channel_id=1, source_target_pairs={{0,2},{1,3},{2,0},{3,1},{4,6},{5,7},{6,4},{7,5},{8,10},{9,11},{10,... | collective-permute-start | bytes 61448 | tf_op jit(solution)/shard_map/ppermute | solution.py:22
  86.1 1.3 %gather_fusion = bf16[512,128]{1,0:T(8,128)(2,1)S(1)} fusion(bf16[4096,128]{1,0:T(8,128)(2,1)S(1)} %copy-done, s32[1024]{0:T(1024)S(1)} %pad_clamp_fusion), kind=kCustom, calls=%fused_computation | custom fusion | bytes 264192 | tf_op jit(solution)/shard_map/jit(_take)/gather | solution.py:441
  87.5 0.0 copy-start.2
  87.5 0.0 copy-start.3
  87.5 0.0 copy-start.4
  87.5 0.0 copy-start.5
  87.5 0.0 copy-start.6
  87.5 0.1 early.1
  87.7 0.2 merge.1
  87.8 2.3 %collective-permute-start.8 = (bf16[64,256]{1,0:T(8,128)(2,1)S(1)}, bf16[64,256]{1,0:T(8,128)(2,1)S(1)}, u32[]{:S(2)}, u32[]{:S(2)}) collective-permute-start(bf16[64,256]{1,0:T(8,128)(2,1)S(1)} %get-tuple-element.34), channel_id=1, source_target_pairs={{0,1},{1,0},{2,3},{3,2},{4,5},{5,4},{6,7},{7,6},{8,9},{9,8},{10,11... | collective-permute-start | bytes 98312 | tf_op jit(solution)/shard_map/ppermute | solution.py:22
  90.1 1.2 %collective-permute-start.10 = (bf16[64,256]{1,0:T(8,128)(2,1)S(1)}, bf16[64,256]{1,0:T(8,128)(2,1)S(1)}, u32[]{:S(2)}, u32[]{:S(2)}) collective-permute-start(bf16[64,256]{1,0:T(8,128)(2,1)S(1)} %get-tuple-element.34), channel_id=1, source_target_pairs={{0,129},{1,128},{2,131},{3,130},{4,133},{5,132},{6,135},{7,134},{8... | collective-permute-start | bytes 98312 | tf_op jit(solution)/shard_map/ppermute | solution.py:34
  91.3 0.2 collective-permute-start.9
  91.6 0.1 broadcast_select_fusion.light
  91.7 6.2 %prepare.1 = (bf16[768,256]{1,0:T(8,128)(2,1)S(1)}, f32[2,256,256]{2,1,0:T(8,128)S(1)}, f32[2,64,256]{2,1,0:T(8,128)S(1)}, f32[2,8,256]{2,1,0:T(8,128)S(1)}, f32[2,64,128]{2,1,0:T(8,128)S(1)}) custom-call(s32[1]{0:T(128)} %bitcast.place.me.refs_0_, s32[1]{0:T(128)} %bitcast.1.grp, s32[4]{0:T(128)S(1)} %copy-done.7, bf16[4,64,4096]{2,1,0:T(8,128)(2,1)S(1)} %copy-done.2, ...), custom_call_target="tpu_custom_call" | custom-call | tf_op jit(solution)/shard_map/prepare/pallas_call | solution.py:464
  98.0 1.0 render.1
  (27 shorter events, 0.1 us)
Async XLA Ops:
  0.6 85.5 %copy-start = (bf16[4096,128]{1,0:T(8,128)(2,1)S(1)}, bf16[4096,128]{1,0:T(8,128)(2,1)}, u32[]{:S(2)}) copy-start(bf16[4096,128]{1,0:T(8,128)(2,1)} %param.18) | copy-start | bytes 3145732
  3.9 8.9 %copy-start.7 = (s32[4]{0:T(128)S(1)}, s32[4]{0:T(128)}, u32[]{:S(2)}) copy-start(s32[4]{0:T(128)} %kinds.3) | copy-start | bytes 52
  3.9 8.9 %collective-permute-start = (bf16[3,256,2048]{2,1,0:T(8,128)(2,1)}, bf16[3,256,2048]{2,1,0:T(8,128)(2,1)}, u32[]{:S(2)}, u32[]{:S(2)}) collective-permute-start(bf16[3,256,2048]{2,1,0:T(8,128)(2,1)} %get-tuple-element.22), channel_id=1, source_target_pairs={{0,1},{1,0},{2,3},{3,2},{4,5},{5,4},{6,7},{7,6},{8,9},{9,8},{10,11... | collective-permute-start | bytes 9437192 | tf_op jit(solution)/shard_map/ppermute | solution.py:22
  9.5 27.6 %collective-permute-start.5 = (bf16[192,2048]{1,0:T(8,128)(2,1)}, bf16[192,2048]{1,0:T(8,128)(2,1)}, u32[]{:S(2)}, u32[]{:S(2)}) collective-permute-start(bf16[192,2048]{1,0:T(8,128)(2,1)} %get-tuple-element.31), channel_id=1, source_target_pairs={{0,2},{1,3},{2,0},{3,1},{4,6},{5,7},{6,4},{7,5},{8,10},{9,11},{10,... | collective-permute-start | bytes 2359304 | tf_op jit(solution)/shard_map/ppermute | solution.py:22
  9.6 36.9 %collective-permute-start.6 = (bf16[192,2048]{1,0:T(8,128)(2,1)}, bf16[192,2048]{1,0:T(8,128)(2,1)}, u32[]{:S(2)}, u32[]{:S(2)}) collective-permute-start(bf16[192,2048]{1,0:T(8,128)(2,1)} %get-tuple-element.32), channel_id=1, source_target_pairs={{0,3},{1,2},{2,1},{3,0},{4,7},{5,6},{6,5},{7,4},{8,11},{9,10},{10,... | collective-permute-start | bytes 2359304 | tf_op jit(solution)/shard_map/ppermute | solution.py:22
  12.9 22.1 %copy-start.10 = (bf16[64,2048]{1,0:T(8,128)(2,1)S(1)}, bf16[64,2048]{1,0:T(8,128)(2,1)}, u32[]{:S(2)}) copy-start(bf16[64,2048]{1,0:T(8,128)(2,1)} %get-tuple-element.26) | copy-start | bytes 786436
  12.9 22.2 %copy-start.9 = (bf16[64,2048]{1,0:T(8,128)(2,1)S(1)}, bf16[64,2048]{1,0:T(8,128)(2,1)}, u32[]{:S(2)}) copy-start(bf16[64,2048]{1,0:T(8,128)(2,1)} %get-tuple-element.27) | copy-start | bytes 786436
  12.9 24.2 %copy-start.8 = (s32[2,256]{1,0:T(2,128)S(1)}, s32[2,256]{1,0:T(2,128)}, u32[]{:S(2)}) copy-start(s32[2,256]{1,0:T(2,128)} %param.17) | copy-start | bytes 6148
  12.9 44.5 %copy-start.1 = (bf16[2,256,2048]{2,1,0:T(8,128)(2,1)S(1)}, bf16[2,256,2048]{2,1,0:T(8,128)(2,1)}, u32[]{:S(2)}) copy-start(bf16[2,256,2048]{2,1,0:T(8,128)(2,1)} %refs_3_.3) | copy-start | bytes 6291460
  34.9 40.8 %collective-permute-start.1 = (bf16[64,2048]{1,0:T(8,128)(2,1)S(1)}, bf16[64,2048]{1,0:T(8,128)(2,1)S(1)}, u32[]{:S(2)}, u32[]{:S(2)}) collective-permute-start(bf16[64,2048]{1,0:T(8,128)(2,1)S(1)} %copy-done.10), channel_id=1, source_target_pairs={{0,2},{1,3},{2,0},{3,1},{4,6},{5,7},{6,4},{7,5},{8,10},{9,11},{10,... | collective-permute-start | bytes 786440 | tf_op jit(solution)/shard_map/ppermute | solution.py:22
  35.0 40.7 %collective-permute-start.2 = (bf16[64,2048]{1,0:T(8,128)(2,1)S(1)}, bf16[64,2048]{1,0:T(8,128)(2,1)S(1)}, u32[]{:S(2)}, u32[]{:S(2)}) collective-permute-start(bf16[64,2048]{1,0:T(8,128)(2,1)S(1)} %copy-done.9), channel_id=1, source_target_pairs={{0,3},{1,2},{2,1},{3,0},{4,7},{5,6},{6,5},{7,4},{8,11},{9,10},{10,... | collective-permute-start | bytes 786440 | tf_op jit(solution)/shard_map/ppermute | solution.py:22
  37.0 20.3 %collective-permute-start.3 = (f32[16,512]{1,0:T(8,128)S(1)}, f32[16,512]{1,0:T(8,128)S(1)}, u32[]{:S(2)}, u32[]{:S(2)}) collective-permute-start(f32[16,512]{1,0:T(8,128)S(1)} %get-tuple-element.29), channel_id=1, source_target_pairs={{0,2},{1,3},{2,0},{3,1},{4,6},{5,7},{6,4},{7,5},{8,10},{9,11},{10,... | collective-permute-start | bytes 98312 | tf_op jit(solution)/shard_map/ppermute | solution.py:22
  75.6 11.9 %collective-permute-start.7 = (bf16[80,384]{1,0:T(8,128)(2,1)S(1)}, bf16[80,384]{1,0:T(8,128)(2,1)S(1)}, u32[]{:S(2)}, u32[]{:S(2)}) collective-permute-start(bf16[80,384]{1,0:T(8,128)(2,1)S(1)} %remote.3), channel_id=1, source_target_pairs={{0,2},{1,3},{2,0},{3,1},{4,6},{5,7},{6,4},{7,5},{8,10},{9,11},{10,... | collective-permute-start | bytes 184328 | tf_op jit(solution)/shard_map/ppermute | solution.py:22
  84.4 3.2 %collective-permute-start.4 = (bf16[80,128]{1,0:T(8,128)(2,1)S(1)}, bf16[80,128]{1,0:T(8,128)(2,1)S(1)}, u32[]{:S(2)}, u32[]{:S(2)}) collective-permute-start(bf16[80,128]{1,0:T(8,128)(2,1)S(1)} %remote.2), channel_id=1, source_target_pairs={{0,2},{1,3},{2,0},{3,1},{4,6},{5,7},{6,4},{7,5},{8,10},{9,11},{10,... | collective-permute-start | bytes 61448 | tf_op jit(solution)/shard_map/ppermute | solution.py:22
  87.5 4.2 %copy-start.2 = (bf16[4,64,4096]{2,1,0:T(8,128)(2,1)S(1)}, bf16[4,64,4096]{2,1,0:T(8,128)(2,1)}, u32[]{:S(2)}) copy-start(bf16[4,64,4096]{2,1,0:T(8,128)(2,1)} %w3.1) | copy-start | bytes 6291460
  87.5 4.2 %copy-start.3 = (bf16[128,4096]{1,0:T(8,128)(2,1)S(1)}, bf16[128,4096]{1,0:T(8,128)(2,1)}, u32[]{:S(2)}) copy-start(bf16[128,4096]{1,0:T(8,128)(2,1)} %w_env.1) | copy-start | bytes 3145732
  87.5 4.2 %copy-start.4 = (bf16[4096,64]{0,1:T(8,128)(2,1)S(1)}, bf16[4096,64]{0,1:T(8,128)(2,1)}, u32[]{:S(2)}) copy-start(bf16[4096,64]{0,1:T(8,128)(2,1)} %param.23) | copy-start | bytes 1572868
  87.5 4.2 %copy-start.5 = (bf16[2,4096]{1,0:T(2,128)(2,1)S(1)}, bf16[2,4096]{1,0:T(2,128)(2,1)}, u32[]{:S(2)}) copy-start(bf16[2,4096]{1,0:T(2,128)(2,1)} %scale.1) | copy-start | bytes 49156
  87.5 4.2 %copy-start.6 = (bf16[2,4096]{1,0:T(2,128)(2,1)S(1)}, bf16[2,4096]{1,0:T(2,128)(2,1)}, u32[]{:S(2)}) copy-start(bf16[2,4096]{1,0:T(2,128)(2,1)} %shift.1) | copy-start | bytes 49156
  87.8 10.2 %collective-permute-start.8 = (bf16[64,256]{1,0:T(8,128)(2,1)S(1)}, bf16[64,256]{1,0:T(8,128)(2,1)S(1)}, u32[]{:S(2)}, u32[]{:S(2)}) collective-permute-start(bf16[64,256]{1,0:T(8,128)(2,1)S(1)} %get-tuple-element.34), channel_id=1, source_target_pairs={{0,1},{1,0},{2,3},{3,2},{4,5},{5,4},{6,7},{7,6},{8,9},{9,8},{10,11... | collective-permute-start | bytes 98312 | tf_op jit(solution)/shard_map/ppermute | solution.py:22
  90.1 7.9 %collective-permute-start.10 = (bf16[64,256]{1,0:T(8,128)(2,1)S(1)}, bf16[64,256]{1,0:T(8,128)(2,1)S(1)}, u32[]{:S(2)}, u32[]{:S(2)}) collective-permute-start(bf16[64,256]{1,0:T(8,128)(2,1)S(1)} %get-tuple-element.34), channel_id=1, source_target_pairs={{0,129},{1,128},{2,131},{3,130},{4,133},{5,132},{6,135},{7,134},{8... | collective-permute-start | bytes 98312 | tf_op jit(solution)/shard_map/ppermute | solution.py:34
  91.3 6.7 %collective-permute-start.9 = (bf16[64,256]{1,0:T(8,128)(2,1)S(1)}, bf16[64,256]{1,0:T(8,128)(2,1)S(1)}, u32[]{:S(2)}, u32[]{:S(2)}) collective-permute-start(bf16[64,256]{1,0:T(8,128)(2,1)S(1)} %get-tuple-element.33.a0), channel_id=1, source_target_pairs={{0,128},{128,0},{1,129},{129,1},{2,130},{130,2},{3,131},{131,3},{4... | collective-permute-start | bytes 98312 | tf_op jit(solution)/shard_map/ppermute | solution.py:26

commit v5 on v4

--- a/solution.py
+++ b/solution.py
@@ -107,15 +107,17 @@
         copy.wait()
 
 
-def first_kernel(place, q, same, cross, held, arrive, leave):
+def first_kernel(place, q, same, cross, arrive):
     me = place[0]
-    count = same.shape[0] // 2
-    pieces = []
-    for n, (group, target) in enumerate(((me, same), (1 - me, cross))):
-        for half in range(2):
-            span = pl.ds(half * count, count)
-            pieces.append((q.at[group, span], held.at[n, span], target.at[span]))
-    shuttle(pieces, arrive, leave)
+    rows = pl.ds(0, same.shape[0])
+    copies = [
+        pltpu.make_async_copy(q.at[me, rows], same, arrive.at[0]),
+        pltpu.make_async_copy(q.at[1 - me, rows], cross, arrive.at[1]),
+    ]
+    for copy in copies:
+        copy.start()
+    for copy in copies:
+        copy.wait()
 
 
 def second_kernel(place, q, k, v, same, cross, bundle, held, rest, arrive, leave):
@@ -218,6 +220,79 @@
         out[64:] = share[...].astype(jnp.bfloat16)
 
 
+def last_kernel(place, qs, qd, k, kx, vw, home, out, acc, share):
+    me = place[0]
+    heads = vw.shape[0]
+    zero = jnp.zeros((2 * qs.shape[0], HD), jnp.bfloat16)
+
+    def scores_at(start):
+        cols = pl.ds(start, 2 * HD)
+        keys = jnp.concatenate((k[me, :, cols], kx[:, cols]), axis=0)
+        pair = jnp.concatenate((qs[:, cols], qd[:, cols]), axis=0)
+        queries = jnp.concatenate(
+            (
+                jnp.concatenate((pair[:, :HD], zero), axis=1),
+                jnp.concatenate((zero, pair[:, HD:]), axis=1),
+            ),
+            axis=0,
+        )
+        half = keys.shape[0] // 2
+        return [dot_lanes(keys[:half], queries), dot_lanes(keys[half:], queries)]
+
+    def finish(head, scores, top):
+        wide = scores[0].shape[1] // 2
+        powers = []
+        for block in scores:
+            shifted = block if top is None else block - top
+            powers.append(jnp.exp2(shifted * SCALE).astype(jnp.bfloat16))
+        found = []
+        for n in range(2):
+            read = vw[head + n]
+            half = read.shape[1] // 2
+            lanes = slice(n * wide, (n + 1) * wide)
+            summed = jnp.dot(
+                read[:, :half], powers[0][:, lanes], preferred_element_type=jnp.float32
+            ) + jnp.dot(read[:, half:], powers[1][:, lanes], preferred_element_type=jnp.float32)
+            total = summed[64:65]
+            level = jnp.log2(total)
+            if top is not None:
+                level = level + top[:, lanes] * SCALE
+            row = pl.ds(head + n, 1)
+            mine = 1.0 / (1.0 + jnp.exp2(home[row, :] - level))
+            mine = mine.astype(jnp.bfloat16).astype(jnp.float32)
+            share[row, :] = mine
+            found.append((summed[:64] * (mine / total), level))
+        return found
+
+    gathered = jnp.zeros(acc.shape, jnp.float32)
+    levels = []
+    ahead = scores_at(0)
+    for head in range(0, heads, 2):
+        scores = ahead
+        if head + 2 < heads:
+            ahead = scores_at((head + 2) * HD)
+        for piece, level in finish(head, scores, None):
+            gathered = gathered + piece
+            levels.append(level)
+    acc[...] = gathered
+
+    @pl.when(jnp.logical_not(worst(levels) < SAFE))
+    def _():
+        acc[...] = jnp.zeros_like(acc)
+
+        def body(n, carry):
+            scores = scores_at(pl.multiple_of(n * 2 * HD, 2 * HD))
+            top = jnp.maximum(*(jnp.max(s, axis=0, keepdims=True) for s in scores))
+            for piece, _ in finish(2 * n, scores, top):
+                acc[...] += piece
+            return carry
+
+        lax.fori_loop(0, heads // 2, body, 0)
+
+    out[:64] = acc[...].astype(jnp.bfloat16)
+    out[64:] = share[...].astype(jnp.bfloat16)
+
+
 def blend(remote, mean, start):
     acc = remote[:64].astype(jnp.float32)
     for h in range(mean.shape[0]):
@@ -358,10 +433,9 @@
     ahead, behind = pl.pallas_call(
         first_kernel,
         in_specs=[scalar, remain],
-        out_specs=[remain] * 2,
-        out_shape=[pltpu.HBM((first, width), jnp.bfloat16)] * 2,
-        scratch_shapes=[pltpu.VMEM((2, first, width), jnp.bfloat16)]
-        + [pltpu.SemaphoreType.DMA((4,))] * 2,
+        out_specs=[RESIDENT] * 2,
+        out_shape=[pltpu.VMEM((first, width), jnp.bfloat16)] * 2,
+        scratch_shapes=[pltpu.SemaphoreType.DMA((2,))],
         compiler_params=LIMIT,
         name="first",
     )(place, stay(q_inv))
@@ -405,7 +479,9 @@
                 given[1],
                 picked,
                 given[2],
-                pl.BlockSpec((None, patch, cols), lambda g, m, r, t: (t[2 * r[0] + m[0]], 0, g)),
+                pl.BlockSpec(
+                    (None, patch, cols), lambda g, m, r, t: (t[2 * r[0] + m[0]], 0, g)
+                ),
             ],
             out_specs=[
                 reads,
@@ -531,7 +607,22 @@
         return seq_swap(sent, 2)
 
     back0 = remote(same0, cross0, ((0, 128), (128, 192)), 0)
-    back1 = remote(same1, cross1, ((0, 64),), 3)
+    last = 2 * (rows - first)
+    back1 = seq_swap(
+        pl.pallas_call(
+            last_kernel,
+            in_specs=[scalar] + [RESIDENT] * 6,
+            out_specs=RESIDENT,
+            out_shape=pltpu.VMEM((64 + heads, last), jnp.bfloat16),
+            scratch_shapes=[
+                pltpu.VMEM((64, last), jnp.float32),
+                pltpu.VMEM((heads, last), jnp.float32),
+            ],
+            compiler_params=LIMIT,
+            name="last",
+        )(place, *resident(same1, cross1, k_inv, bundle[1], vw, home[:, 2 * first :])),
+        2,
+    )
     early = pl.pallas_call(
         early_kernel,
         in_specs=[RESIDENT] * 2,

time: 99.2 us -> 97 us (0.978)
  Pallas kernels: 61.9 us -> 59.5 us
  local copies, waits for them, and re-layouts: 1.41 us -> 2.74 us
  waiting for transfers between devices: 21.9 us -> 20.8 us
    pallas_call x2 -> x1, Pallas kernels: 26.9 us -> 18.2 us  [remote(): pl.pallas_call(lambda *refs: remote_kernel(spans, *refs), grid_spec=pltpu...]
    pallas_call x1 -> x2, Pallas kernels: 2.21 us -> 8.74 us  [the longest x1 6.09 us: on_device(): pl.pallas_call(last_kernel, in_specs=[scalar] + [RESIDENT] * 6, out_specs...]
    squeeze x0 -> x1, local copies, waits for them, and re-layouts: none -> 1.32 us  [on_device(): bundle[1]]
    ppermute x9, waiting for transfers between devices: 21.9 us -> 20.8 us  [seq_swap(): return lax.ppermute(block, 'seq', [(i, i ^ flip) for i in range(count)])]
  transfers between devices with their start and end apart: 11 -> 11, of which waited for: 3 -> 3; matrix products, arithmetic and copies ran while one was open for 2% -> 3% of each run, Pallas kernels for 58% -> 57%
where the time goes in v5:
time: 97 us; the launch traced here: 96.8 us
  Pallas kernels  59.5 us (61%)
  waiting for transfers between devices  20.8 us (21%)
  starting transfers between devices  12.7 us (13%)
  local copies, waits for them, and re-layouts  2.74 us (3%)
    pallas_call x1, Pallas kernels, on_device(): pl.pallas_call(local_kernel, grid_spec=pltpu.PrefetchScalarGridSpec(num_s...  21.8 us
    ppermute x9, waiting for transfers between devices, seq_swap(): return lax.ppermute(block, 'seq', [(i, i ^ flip) for i in range(count)])  20.8 us
    pallas_call x1, Pallas kernels, remote(): pl.pallas_call(lambda *refs: remote_kernel(spans, *refs), grid_spec=pltpu...  18.2 us
    ppermute x9, starting transfers between devices, seq_swap(): return lax.ppermute(block, 'seq', [(i, i ^ flip) for i in range(count)])  11.2 us
    pallas_call x1, Pallas kernels, on_device(): pl.pallas_call(prepare_kernel, grid_spec=pltpu.PrefetchScalarGridSpec(num...  6.23 us
    pallas_call x1, Pallas kernels, on_device(): pl.pallas_call(last_kernel, in_specs=[scalar] + [RESIDENT] * 6, out_specs...  6.09 us
    pallas_call x1, Pallas kernels, on_device(): pl.pallas_call(second_kernel, in_specs=[scalar, remain, remain, remain],...  3.27 us
    pallas_call x1, Pallas kernels, on_device(): pl.pallas_call(first_kernel, in_specs=[scalar, remain], out_specs=[RESIDE...  2.64 us
  transfers between devices with their start and end apart: 11, of which 3 were waited for; matrix products, arithmetic and copies ran while one was open for 3% of the time, Pallas kernels for 57%

profile of v5, /device:TPU:1, one launch (start us, length us, event | category | flops | bytes accessed | tf_op | source)
XLA Modules:
  0.0 96.8 jit_solution(6310777168920558255)
XLA Ops:
  0.6 0.0 copy-start
  0.7 3.3 %second.1 = (bf16[64,2048]{1,0:T(8,128)(2,1)}, bf16[64,2048]{1,0:T(8,128)(2,1)}, bf16[3,256,2048]{2,1,0:T(8,128)(2,1)}) custom-call(s32[1]{0:T(128)} %bitcast.place.me.refs_0_, bf16[2,256,2048]{2,1,0:T(8,128)(2,1)} %q.5, bf16[2,256,2048]{2,1,0:T(8,128)(2,1)} %refs_3_.1, bf16[2,256,2048]{2,1,0:T(8,128)(2,1)} %v.3), custom_call_target="tpu_custom_call" | custom-call | tf_op jit(solution)/shard_map/second/pallas_call | solution.py:444
  3.9 0.0 copy-start.8
  3.9 0.0 copy-start.7
  4.0 3.3 %collective-permute-start = (bf16[3,256,2048]{2,1,0:T(8,128)(2,1)}, bf16[3,256,2048]{2,1,0:T(8,128)(2,1)}, u32[]{:S(2)}, u32[]{:S(2)}) collective-permute-start(bf16[3,256,2048]{2,1,0:T(8,128)(2,1)} %get-tuple-element.22), channel_id=1, source_target_pairs={{0,1},{1,0},{2,3},{3,2},{4,5},{5,4},{6,7},{7,6},{8,9},{9,8},{10,11... | collective-permute-start | bytes 9437192 | tf_op jit(solution)/shard_map/ppermute | solution.py:22
  7.2 2.6 %first.1 = (bf16[192,2048]{1,0:T(8,128)(2,1)}, bf16[192,2048]{1,0:T(8,128)(2,1)}) custom-call(s32[1]{0:T(128)} %bitcast.place.me.refs_0_, bf16[2,256,2048]{2,1,0:T(8,128)(2,1)} %q.5), custom_call_target="tpu_custom_call" | custom-call | tf_op jit(solution)/shard_map/first/pallas_call | solution.py:433
  9.9 0.1 collective-permute-start.5
  10.0 1.6 %collective-permute-start.6 = (bf16[192,2048]{1,0:T(8,128)(2,1)}, bf16[192,2048]{1,0:T(8,128)(2,1)}, u32[]{:S(2)}, u32[]{:S(2)}) collective-permute-start(bf16[192,2048]{1,0:T(8,128)(2,1)} %get-tuple-element.32), channel_id=1, source_target_pairs={{0,3},{1,2},{2,1},{3,0},{4,7},{5,6},{6,5},{7,4},{8,11},{9,10},{10,... | collective-permute-start | bytes 2359304 | tf_op jit(solution)/shard_map/ppermute | solution.py:22
  11.7 1.2 %collective-permute-done.qx.kx.vx.refs_4_ = bf16[3,256,2048]{2,1,0:T(8,128)(2,1)} collective-permute-done((bf16[3,256,2048]{2,1,0:T(8,128)(2,1)}, bf16[3,256,2048]{2,1,0:T(8,128)(2,1)}, u32[]{:S(2)}, u32[]{:S(2)}) %collective-permute-start) | collective-permute-done | bytes 3145760 | tf_op jit(solution)/shard_map/ppermute | solution.py:22
  12.9 21.8 %local.1 = (bf16[16,80,512]{2,1,0:T(8,128)(2,1)S(1)}, f32[16,64,512]{2,1,0:T(8,128)S(1)}, f32[16,512]{1,0:T(8,128)S(1)}) custom-call(s32[1]{0:T(128)} %bitcast.place.me.refs_0_, s32[1]{0:T(128)} %bitcast.1.grp, s32[4]{0:T(128)S(1)} %copy-done.7, bf16[2,256,2048]{2,1,0:T(8,128)(2,1)} %q.5, bf16[3,256,2048]{2,1,0:T(8,128)(2,1)} %collective-permute-done.qx.kx.vx.refs_4_, ...), custom_call_target="tpu_custom_call" | custom-call | tf_op jit(solution)/shard_map/local/pallas_call | solution.py:470
  34.7 0.0 copy-start.1
  34.7 0.1 collective-permute-start.1
  34.8 2.0 %collective-permute-start.2 = (bf16[64,2048]{1,0:T(8,128)(2,1)S(1)}, bf16[64,2048]{1,0:T(8,128)(2,1)S(1)}, u32[]{:S(2)}, u32[]{:S(2)}) collective-permute-start(bf16[64,2048]{1,0:T(8,128)(2,1)S(1)} %copy-done.9), channel_id=1, source_target_pairs={{0,3},{1,2},{2,1},{3,0},{4,7},{5,6},{6,5},{7,4},{8,11},{9,10},{10,... | collective-permute-start | bytes 786440 | tf_op jit(solution)/shard_map/ppermute | solution.py:22
  36.8 1.3 %slice_bitcast_fusion.kx = bf16[256,2048]{1,0:T(8,128)(2,1)S(1)} fusion(bf16[3,256,2048]{2,1,0:T(8,128)(2,1)} %collective-permute-done.qx.kx.vx.refs_4_), kind=kLoop, calls=%fused_computation.1 | loop fusion | bytes 2097152 | tf_op jit(solution)/shard_map/squeeze | solution.py:623
  38.2 8.7 %collective-permute-done.6.refs_2_ = bf16[192,2048]{1,0:T(8,128)(2,1)} collective-permute-done((bf16[192,2048]{1,0:T(8,128)(2,1)}, bf16[192,2048]{1,0:T(8,128)(2,1)}, u32[]{:S(2)}, u32[]{:S(2)}) %collective-permute-start.6) | collective-permute-done | bytes 786464 | tf_op jit(solution)/shard_map/ppermute | solution.py:22
  46.9 10.9 %collective-permute-done.3.refs_6_ = f32[16,512]{1,0:T(8,128)S(1)} collective-permute-done((f32[16,512]{1,0:T(8,128)S(1)}, f32[16,512]{1,0:T(8,128)S(1)}, u32[]{:S(2)}, u32[]{:S(2)}) %collective-permute-start.3) | collective-permute-done | bytes 32800 | tf_op jit(solution)/shard_map/ppermute | solution.py:22
  57.8 18.2 %remote.1 = bf16[80,384]{1,0:T(8,128)(2,1)S(1)} custom-call(s32[1]{0:T(128)} %bitcast.place.me.refs_0_, bf16[192,2048]{1,0:T(8,128)(2,1)} %collective-permute-done.5.refs_1_, bf16[192,2048]{1,0:T(8,128)(2,1)} %collective-permute-done.6.refs_2_, bf16[2,256,2048]{2,1,0:T(8,128)(2,1)S(1)} %copy-done.1, ...), custom_call_target="tpu_custom_call" | custom-call | tf_op jit(solution)/shard_map/remote/pallas_call | solution.py:584
  76.0 0.2 collective-permute-start.7
  76.1 6.1 %last.1 = bf16[80,128]{1,0:T(8,128)(2,1)S(1)} custom-call(s32[1]{0:T(128)} %bitcast.place.me.refs_0_, bf16[64,2048]{1,0:T(8,128)(2,1)S(1)} %collective-permute-done.1.qs, bf16[64,2048]{1,0:T(8,128)(2,1)S(1)} %collective-permute-done.2.qd, bf16[2,256,2048]{2,1,0:T(8,128)(2,1)S(1)} %copy-done.1, bf16[256,2048]{1,0:T(8,128)(2,1)S(1)} %slice_bitcast_fusion.kx, ...), custom_call_target="tpu_custom_call" | custom-call | tf_op jit(solution)/shard_map/last/pallas_call | solution.py:612
  82.2 1.7 %collective-permute-start.4 = (bf16[80,128]{1,0:T(8,128)(2,1)S(1)}, bf16[80,128]{1,0:T(8,128)(2,1)S(1)}, u32[]{:S(2)}, u32[]{:S(2)}) collective-permute-start(bf16[80,128]{1,0:T(8,128)(2,1)S(1)} %last.1), channel_id=1, source_target_pairs={{0,2},{1,3},{2,0},{3,1},{4,6},{5,7},{6,4},{7,5},{8,10},{9,11},{10,... | collective-permute-start | bytes 61448 | tf_op jit(solution)/shard_map/ppermute | solution.py:22
  83.9 1.3 %gather_fusion = bf16[512,128]{1,0:T(8,128)(2,1)S(1)} fusion(bf16[4096,128]{1,0:T(8,128)(2,1)S(1)} %copy-done, s32[1024]{0:T(1024)S(1)} %pad_clamp_fusion), kind=kCustom, calls=%fused_computation | custom fusion | bytes 264192 | tf_op jit(solution)/shard_map/jit(_take)/gather | solution.py:517
  85.3 0.0 copy-start.2
  85.3 0.0 copy-start.3
  85.3 0.0 copy-start.6
  85.3 0.1 early.1
  85.5 0.2 merge.1
  85.6 2.3 %collective-permute-start.8 = (bf16[64,256]{1,0:T(8,128)(2,1)S(1)}, bf16[64,256]{1,0:T(8,128)(2,1)S(1)}, u32[]{:S(2)}, u32[]{:S(2)}) collective-permute-start(bf16[64,256]{1,0:T(8,128)(2,1)S(1)} %get-tuple-element.34), channel_id=1, source_target_pairs={{0,1},{1,0},{2,3},{3,2},{4,5},{5,4},{6,7},{7,6},{8,9},{9,8},{10,11... | collective-permute-start | bytes 98312 | tf_op jit(solution)/shard_map/ppermute | solution.py:22
  87.9 1.2 %collective-permute-start.10 = (bf16[64,256]{1,0:T(8,128)(2,1)S(1)}, bf16[64,256]{1,0:T(8,128)(2,1)S(1)}, u32[]{:S(2)}, u32[]{:S(2)}) collective-permute-start(bf16[64,256]{1,0:T(8,128)(2,1)S(1)} %get-tuple-element.34), channel_id=1, source_target_pairs={{0,129},{1,128},{2,131},{3,130},{4,133},{5,132},{6,135},{7,134},{8... | collective-permute-start | bytes 98312 | tf_op jit(solution)/shard_map/ppermute | solution.py:34
  89.1 0.3 collective-permute-start.9
  89.4 0.1 broadcast_select_fusion.light
  89.6 6.2 %prepare.1 = (bf16[768,256]{1,0:T(8,128)(2,1)S(1)}, f32[2,256,256]{2,1,0:T(8,128)S(1)}, f32[2,64,256]{2,1,0:T(8,128)S(1)}, f32[2,8,256]{2,1,0:T(8,128)S(1)}, f32[2,64,128]{2,1,0:T(8,128)S(1)}) custom-call(s32[1]{0:T(128)} %bitcast.place.me.refs_0_, s32[1]{0:T(128)} %bitcast.1.grp, s32[4]{0:T(128)S(1)} %copy-done.7, bf16[4,64,4096]{2,1,0:T(8,128)(2,1)S(1)} %copy-done.2, ...), custom_call_target="tpu_custom_call" | custom-call | tf_op jit(solution)/shard_map/prepare/pallas_call | solution.py:540
  95.8 1.0 %render.1 = (bf16[2,64,256]{2,1,0:T(8,128)(2,1)}, bf16[2,64,256]{2,1,0:T(8,128)(2,1)}) custom-call(s32[1]{0:T(128)} %bitcast.place.me.refs_0_, bf16[64,256]{1,0:T(8,128)(2,1)S(1)} %get-tuple-element.33.a0, bf16[64,256]{1,0:T(8,128)(2,1)S(1)} %collective-permute-done.8.a1, bf16[64,256]{1,0:T(8,128)(2,1)S(1)} %collective-permute-done.9.a2, ...), custom_call_target="tpu_custom_call" | custom-call | tf_op jit(solution)/shard_map/render/pallas_call | solution.py:645
  (29 shorter events, 0.1 us)
Async XLA Ops:
  0.6 83.3 %copy-start = (bf16[4096,128]{1,0:T(8,128)(2,1)S(1)}, bf16[4096,128]{1,0:T(8,128)(2,1)}, u32[]{:S(2)}) copy-start(bf16[4096,128]{1,0:T(8,128)(2,1)} %param.18) | copy-start | bytes 3145732
  3.9 7.7 %copy-start.8 = (s32[2,256]{1,0:T(2,128)S(1)}, s32[2,256]{1,0:T(2,128)}, u32[]{:S(2)}) copy-start(s32[2,256]{1,0:T(2,128)} %param.17) | copy-start | bytes 6148
  3.9 8.9 %copy-start.7 = (s32[4]{0:T(128)S(1)}, s32[4]{0:T(128)}, u32[]{:S(2)}) copy-start(s32[4]{0:T(128)} %kinds.3) | copy-start | bytes 52
  4.0 8.9 %collective-permute-start = (bf16[3,256,2048]{2,1,0:T(8,128)(2,1)}, bf16[3,256,2048]{2,1,0:T(8,128)(2,1)}, u32[]{:S(2)}, u32[]{:S(2)}) collective-permute-start(bf16[3,256,2048]{2,1,0:T(8,128)(2,1)} %get-tuple-element.22), channel_id=1, source_target_pairs={{0,1},{1,0},{2,3},{3,2},{4,5},{5,4},{6,7},{7,6},{8,9},{9,8},{10,11... | collective-permute-start | bytes 9437192 | tf_op jit(solution)/shard_map/ppermute | solution.py:22
  9.9 28.3 %collective-permute-start.5 = (bf16[192,2048]{1,0:T(8,128)(2,1)}, bf16[192,2048]{1,0:T(8,128)(2,1)}, u32[]{:S(2)}, u32[]{:S(2)}) collective-permute-start(bf16[192,2048]{1,0:T(8,128)(2,1)} %get-tuple-element.31), channel_id=1, source_target_pairs={{0,2},{1,3},{2,0},{3,1},{4,6},{5,7},{6,4},{7,5},{8,10},{9,11},{10,... | collective-permute-start | bytes 2359304 | tf_op jit(solution)/shard_map/ppermute | solution.py:22
  10.0 36.9 %collective-permute-start.6 = (bf16[192,2048]{1,0:T(8,128)(2,1)}, bf16[192,2048]{1,0:T(8,128)(2,1)}, u32[]{:S(2)}, u32[]{:S(2)}) collective-permute-start(bf16[192,2048]{1,0:T(8,128)(2,1)} %get-tuple-element.32), channel_id=1, source_target_pairs={{0,3},{1,2},{2,1},{3,0},{4,7},{5,6},{6,5},{7,4},{8,11},{9,10},{10,... | collective-permute-start | bytes 2359304 | tf_op jit(solution)/shard_map/ppermute | solution.py:22
  12.9 21.8 %copy-start.10 = (bf16[64,2048]{1,0:T(8,128)(2,1)S(1)}, bf16[64,2048]{1,0:T(8,128)(2,1)}, u32[]{:S(2)}) copy-start(bf16[64,2048]{1,0:T(8,128)(2,1)} %get-tuple-element.26) | copy-start | bytes 786436
  12.9 21.9 %copy-start.9 = (bf16[64,2048]{1,0:T(8,128)(2,1)S(1)}, bf16[64,2048]{1,0:T(8,128)(2,1)}, u32[]{:S(2)}) copy-start(bf16[64,2048]{1,0:T(8,128)(2,1)} %get-tuple-element.27) | copy-start | bytes 786436
  34.7 23.1 %copy-start.1 = (bf16[2,256,2048]{2,1,0:T(8,128)(2,1)S(1)}, bf16[2,256,2048]{2,1,0:T(8,128)(2,1)}, u32[]{:S(2)}) copy-start(bf16[2,256,2048]{2,1,0:T(8,128)(2,1)} %refs_3_.1) | copy-start | bytes 6291460
  34.7 41.4 %collective-permute-start.1 = (bf16[64,2048]{1,0:T(8,128)(2,1)S(1)}, bf16[64,2048]{1,0:T(8,128)(2,1)S(1)}, u32[]{:S(2)}, u32[]{:S(2)}) collective-permute-start(bf16[64,2048]{1,0:T(8,128)(2,1)S(1)} %copy-done.10), channel_id=1, source_target_pairs={{0,2},{1,3},{2,0},{3,1},{4,6},{5,7},{6,4},{7,5},{8,10},{9,11},{10,... | collective-permute-start | bytes 786440 | tf_op jit(solution)/shard_map/ppermute | solution.py:22
  34.8 41.3 %collective-permute-start.2 = (bf16[64,2048]{1,0:T(8,128)(2,1)S(1)}, bf16[64,2048]{1,0:T(8,128)(2,1)S(1)}, u32[]{:S(2)}, u32[]{:S(2)}) collective-permute-start(bf16[64,2048]{1,0:T(8,128)(2,1)S(1)} %copy-done.9), channel_id=1, source_target_pairs={{0,3},{1,2},{2,1},{3,0},{4,7},{5,6},{6,5},{7,4},{8,11},{9,10},{10,... | collective-permute-start | bytes 786440 | tf_op jit(solution)/shard_map/ppermute | solution.py:22
  36.8 20.9 %collective-permute-start.3 = (f32[16,512]{1,0:T(8,128)S(1)}, f32[16,512]{1,0:T(8,128)S(1)}, u32[]{:S(2)}, u32[]{:S(2)}) collective-permute-start(f32[16,512]{1,0:T(8,128)S(1)} %get-tuple-element.29), channel_id=1, source_target_pairs={{0,2},{1,3},{2,0},{3,1},{4,6},{5,7},{6,4},{7,5},{8,10},{9,11},{10,... | collective-permute-start | bytes 98312 | tf_op jit(solution)/shard_map/ppermute | solution.py:22
  76.0 9.3 %collective-permute-start.7 = (bf16[80,384]{1,0:T(8,128)(2,1)S(1)}, bf16[80,384]{1,0:T(8,128)(2,1)S(1)}, u32[]{:S(2)}, u32[]{:S(2)}) collective-permute-start(bf16[80,384]{1,0:T(8,128)(2,1)S(1)} %remote.1), channel_id=1, source_target_pairs={{0,2},{1,3},{2,0},{3,1},{4,6},{5,7},{6,4},{7,5},{8,10},{9,11},{10,... | collective-permute-start | bytes 184328 | tf_op jit(solution)/shard_map/ppermute | solution.py:22
  82.2 3.2 %collective-permute-start.4 = (bf16[80,128]{1,0:T(8,128)(2,1)S(1)}, bf16[80,128]{1,0:T(8,128)(2,1)S(1)}, u32[]{:S(2)}, u32[]{:S(2)}) collective-permute-start(bf16[80,128]{1,0:T(8,128)(2,1)S(1)} %last.1), channel_id=1, source_target_pairs={{0,2},{1,3},{2,0},{3,1},{4,6},{5,7},{6,4},{7,5},{8,10},{9,11},{10,... | collective-permute-start | bytes 61448 | tf_op jit(solution)/shard_map/ppermute | solution.py:22
  85.3 4.2 %copy-start.2 = (bf16[4,64,4096]{2,1,0:T(8,128)(2,1)S(1)}, bf16[4,64,4096]{2,1,0:T(8,128)(2,1)}, u32[]{:S(2)}) copy-start(bf16[4,64,4096]{2,1,0:T(8,128)(2,1)} %w3.1) | copy-start | bytes 6291460
  85.3 4.2 %copy-start.3 = (bf16[128,4096]{1,0:T(8,128)(2,1)S(1)}, bf16[128,4096]{1,0:T(8,128)(2,1)}, u32[]{:S(2)}) copy-start(bf16[128,4096]{1,0:T(8,128)(2,1)} %w_env.1) | copy-start | bytes 3145732
  85.3 4.2 %copy-start.4 = (bf16[4096,64]{0,1:T(8,128)(2,1)S(1)}, bf16[4096,64]{0,1:T(8,128)(2,1)}, u32[]{:S(2)}) copy-start(bf16[4096,64]{0,1:T(8,128)(2,1)} %param.23) | copy-start | bytes 1572868
  85.3 4.2 %copy-start.5 = (bf16[2,4096]{1,0:T(2,128)(2,1)S(1)}, bf16[2,4096]{1,0:T(2,128)(2,1)}, u32[]{:S(2)}) copy-start(bf16[2,4096]{1,0:T(2,128)(2,1)} %scale.1) | copy-start | bytes 49156
  85.3 4.2 %copy-start.6 = (bf16[2,4096]{1,0:T(2,128)(2,1)S(1)}, bf16[2,4096]{1,0:T(2,128)(2,1)}, u32[]{:S(2)}) copy-start(bf16[2,4096]{1,0:T(2,128)(2,1)} %shift.1) | copy-start | bytes 49156
  85.6 10.2 %collective-permute-start.8 = (bf16[64,256]{1,0:T(8,128)(2,1)S(1)}, bf16[64,256]{1,0:T(8,128)(2,1)S(1)}, u32[]{:S(2)}, u32[]{:S(2)}) collective-permute-start(bf16[64,256]{1,0:T(8,128)(2,1)S(1)} %get-tuple-element.34), channel_id=1, source_target_pairs={{0,1},{1,0},{2,3},{3,2},{4,5},{5,4},{6,7},{7,6},{8,9},{9,8},{10,11... | collective-permute-start | bytes 98312 | tf_op jit(solution)/shard_map/ppermute | solution.py:22
  87.9 7.9 %collective-permute-start.10 = (bf16[64,256]{1,0:T(8,128)(2,1)S(1)}, bf16[64,256]{1,0:T(8,128)(2,1)S(1)}, u32[]{:S(2)}, u32[]{:S(2)}) collective-permute-start(bf16[64,256]{1,0:T(8,128)(2,1)S(1)} %get-tuple-element.34), channel_id=1, source_target_pairs={{0,129},{1,128},{2,131},{3,130},{4,133},{5,132},{6,135},{7,134},{8... | collective-permute-start | bytes 98312 | tf_op jit(solution)/shard_map/ppermute | solution.py:34
  89.1 6.7 %collective-permute-start.9 = (bf16[64,256]{1,0:T(8,128)(2,1)S(1)}, bf16[64,256]{1,0:T(8,128)(2,1)S(1)}, u32[]{:S(2)}, u32[]{:S(2)}) collective-permute-start(bf16[64,256]{1,0:T(8,128)(2,1)S(1)} %get-tuple-element.33.a0), channel_id=1, source_target_pairs={{0,128},{128,0},{1,129},{129,1},{2,130},{130,2},{3,131},{131,3},{4... | collective-permute-start | bytes 98312 | tf_op jit(solution)/shard_map/ppermute | solution.py:26

commit v6 on v5

--- a/solution.py
+++ b/solution.py
@@ -26,10 +26,10 @@
     return lax.ppermute(block, "grp", [(0, 1), (1, 0)])
 
 
-def both_swap(block):
+def both_swap(block, flip):
     count = lax.axis_size("seq")
     route = [
-        (g * count + i, (1 - g) * count + (i ^ 1)) for g in range(2) for i in range(count)
+        (g * count + i, (1 - g) * count + (i ^ flip)) for g in range(2) for i in range(count)
     ]
     return lax.ppermute(block, ("grp", "seq"), route)
 
@@ -120,17 +120,19 @@
         copy.wait()
 
 
-def second_kernel(place, q, k, v, same, cross, bundle, held, rest, arrive, leave):
+def second_kernel(place, q, k, v, bundle, sb, cb, sc, cc, held, rest, arrive, leave):
     me = place[0]
-    count = same.shape[0]
-    tail = pl.ds(q.shape[1] - count, count)
+    count = sb.shape[0]
+    start = q.shape[1] - 2 * count
     pieces = [(a.at[1 - me], held.at[n], bundle.at[n]) for n, a in enumerate((q, k, v))]
-    pieces.append((q.at[me, tail], rest.at[0], same))
-    pieces.append((q.at[1 - me, tail], rest.at[1], cross))
+    for n, (same, cross) in enumerate(((sb, cb), (sc, cc))):
+        span = pl.ds(start + n * count, count)
+        pieces.append((q.at[me, span], rest.at[2 * n], same))
+        pieces.append((q.at[1 - me, span], rest.at[2 * n + 1], cross))
     shuttle(pieces, arrive, leave)
 
 
-def local_kernel(me, grp, kinds, q, qx, k, kx, v, vx, w, vw, mean, level):
+def local_kernel(me, grp, kinds, q, qx, k, kx, v, vx, w, vw, mean, own, part, level):
     step = pl.program_id(0)
     reads = []
 
@@ -147,18 +149,21 @@
         for i in range(STEP_HEADS):
             cols = slice(i * HD, (i + 1) * HD)
             keys = jnp.concatenate((k[:, cols], kx[:, cols]), axis=0)
-            for spans in (((0, 128),), ((128, 192), (192, 256))):
-                pieces = []
-                for a, b in spans:
-                    pieces += [q[a:b, cols], qx[a:b, cols]]
-                units.append((keys, jnp.concatenate(pieces, axis=0), reads[i]))
+            for a, b in ((0, 128), (128, 256)):
+                queries = jnp.concatenate((q[a:b, cols], qx[a:b, cols]), axis=0)
+                units.append((keys, queries, reads[i]))
         found = softmax(units)
         levels = []
         for i in range(STEP_HEADS):
             rows = []
             for n in range(2):
                 summed, total, row = found[2 * i + n]
-                mean[i, :, n * 256 : n * 256 + 256] = summed * (1.0 / total)
+                scaled = summed * (1.0 / total)
+                if n == 0:
+                    mean[i] = scaled
+                else:
+                    own[i] = scaled[:, :128].astype(jnp.bfloat16)
+                    part[i] = scaled[:, 128:].astype(jnp.bfloat16)
                 rows.append(row)
             levels.append(jnp.concatenate(rows, axis=1))
             level[pl.ds(step * STEP_HEADS + i, 1), :] = levels[-1]
@@ -220,9 +225,19 @@
         out[64:] = share[...].astype(jnp.bfloat16)
 
 
-def last_kernel(place, qs, qd, k, kx, vw, home, out, acc, share):
+def halves(left, right):
+    first = lax.broadcasted_iota(jnp.int32, left.shape, 1) < 64
+    return (
+        jnp.where(first, left, pltpu.roll(right, 64, 1)),
+        jnp.where(first, pltpu.roll(left, 64, 1), right),
+    )
+
+
+def last_kernel(phase, place, qs, qd, k, kx, vw, home, *refs):
+    prior, outs, (acc, share, near) = refs[:phase], refs[phase:-3], refs[-3:]
     me = place[0]
     heads = vw.shape[0]
+    near[...] = halves(home[:, 256:384], home[:, 384:512])[phase]
     zero = jnp.zeros((2 * qs.shape[0], HD), jnp.bfloat16)
 
     def scores_at(start):
@@ -258,7 +273,7 @@
             if top is not None:
                 level = level + top[:, lanes] * SCALE
             row = pl.ds(head + n, 1)
-            mine = 1.0 / (1.0 + jnp.exp2(home[row, :] - level))
+            mine = 1.0 / (1.0 + jnp.exp2(near[row, :] - level))
             mine = mine.astype(jnp.bfloat16).astype(jnp.float32)
             share[row, :] = mine
             found.append((summed[:64] * (mine / total), level))
@@ -289,30 +304,29 @@
 
         lax.fori_loop(0, heads // 2, body, 0)
 
-    out[:64] = acc[...].astype(jnp.bfloat16)
-    out[64:] = share[...].astype(jnp.bfloat16)
-
-
-def blend(remote, mean, start):
+    if phase == 0:
+        outs[0][:64] = acc[...]
+        outs[0][64:] = share[...]
+    else:
+        for a, b, now in ((0, 64, acc), (64, 64 + heads, share)):
+            own, part = halves(prior[0][a:b], now[...])
+            outs[0][a:b] = own.astype(jnp.bfloat16)
+            outs[1][a:b] = part.astype(jnp.bfloat16)
+
+
+def blend(remote, mean):
     acc = remote[:64].astype(jnp.float32)
     for h in range(mean.shape[0]):
         keep = 1.0 - remote[64 + h : 65 + h].astype(jnp.float32)
-        acc = acc + mean[h, :, start : start + acc.shape[1]] * keep
-    return acc
-
-
-def early_kernel(remote, mean, out):
-    out[...] = blend(remote, mean, 0)
-
-
-def merge_kernel(remote, mean, early, own, other):
-    late = blend(remote, mean, early.shape[1])
-    mixed = early[:, 256:]
-    first = lax.broadcasted_iota(jnp.int32, late.shape, 1) < 64
-    own[:, :128] = early[:, :128].astype(jnp.bfloat16)
-    other[:, :128] = early[:, 128:256].astype(jnp.bfloat16)
-    own[:, 128:] = jnp.where(first, mixed, pltpu.roll(late, 64, 1)).astype(jnp.bfloat16)
-    other[:, 128:] = jnp.where(first, pltpu.roll(mixed, 64, 1), late).astype(jnp.bfloat16)
+        acc = acc + mean[h].astype(jnp.float32) * keep
+    return acc.astype(jnp.bfloat16)
+
+
+def join_kernel(remote, mean, own, other):
+    found = blend(remote, mean)
+    half = found.shape[1] // 2
+    own[...] = found[:, :half]
+    other[...] = found[:, half:]
 
 
 def prepare_kernel(
@@ -370,11 +384,16 @@
             base[l] = jnp.broadcast_to(own, base.shape[1:])
 
 
-def render_kernel(place, a0, a1, a2, a3, mixer, cross, direct, base, bias, attrs, rendered):
+def render_kernel(place, *refs):
+    ready, remote, mean = refs[:4], refs[4:8], refs[8:12]
+    mixer, cross, direct, base, bias, attrs, rendered = refs[12:]
     me = place[0]
-    attrs[pl.ds(me, 1)] = a0[...][None]
-    attrs[pl.ds(1 - me, 1)] = a1[...][None]
-    latents = jnp.concatenate((a0[...], a1[...], a2[...], a3[...]), axis=0)
+    found = [
+        jnp.concatenate((a[...], blend(r, m)), axis=1) for a, r, m in zip(ready, remote, mean)
+    ]
+    attrs[pl.ds(me, 1)] = found[0][None]
+    attrs[pl.ds(1 - me, 1)] = found[1][None]
+    latents = jnp.concatenate(found, axis=0)
     mixed = jnp.dot(mixer[...], latents, preferred_element_type=jnp.float32)
     square = mixed[:256] + mixed[256:512]
     wide = latents.astype(jnp.float32)
@@ -387,7 +406,7 @@
         rendered[l] = (read * invert + shift).astype(jnp.bfloat16)
 
 
-LIMIT = pltpu.CompilerParams(vmem_limit_bytes=24 << 20)
+LIMIT = pltpu.CompilerParams(vmem_limit_bytes=14 << 20)
 RESIDENT = pl.BlockSpec(memory_space=pltpu.VMEM)
 
 
@@ -419,7 +438,8 @@
 ):
     groups, rows, width = q_inv.shape
     heads = width // HD
-    first = 3 * rows // 4
+    first = rows // 2
+    piece = rows // 4
     patch = w_attr.shape[2]
     lights, model = mod_scale.shape
     channels = w_embed_env.shape[0]
@@ -441,20 +461,17 @@
     )(place, stay(q_inv))
     same0 = seq_swap(ahead, 2)
     cross0 = seq_swap(behind, 3)
-    late_same, late_cross, bundle = pl.pallas_call(
+    bundle, same1, cross1, same2, cross2 = pl.pallas_call(
         second_kernel,
         in_specs=[scalar, remain, remain, remain],
-        out_specs=[remain] * 3,
-        out_shape=[
-            pltpu.HBM((rows - first, width), jnp.bfloat16),
-            pltpu.HBM((rows - first, width), jnp.bfloat16),
-            pltpu.HBM((3, rows, width), jnp.bfloat16),
-        ],
+        out_specs=[remain] * 5,
+        out_shape=[pltpu.HBM((3, rows, width), jnp.bfloat16)]
+        + [pltpu.HBM((piece, width), jnp.bfloat16)] * 4,
         scratch_shapes=[
             pltpu.VMEM((3, rows, width), jnp.bfloat16),
-            pltpu.VMEM((2, rows - first, width), jnp.bfloat16),
+            pltpu.VMEM((4, piece, width), jnp.bfloat16),
         ]
-        + [pltpu.SemaphoreType.DMA((5,))] * 2,
+        + [pltpu.SemaphoreType.DMA((7,))] * 2,
         compiler_params=LIMIT,
         name="second",
     )(place, stay(q_inv), stay(k_inv), stay(v_inv))
@@ -467,7 +484,7 @@
         pl.BlockSpec((None, rows, cols), lambda g, *_, n=n: (n, 0, g)) for n in range(3)
     ]
     reads = pl.BlockSpec((STEP_HEADS, 80, 2 * rows), lambda g, *_: (g, 0, 0))
-    vw, mean, level = pl.pallas_call(
+    vw, mean, mean_own, mean_part, level = pl.pallas_call(
         local_kernel,
         grid_spec=pltpu.PrefetchScalarGridSpec(
             num_scalar_prefetch=3,
@@ -485,13 +502,17 @@
             ],
             out_specs=[
                 reads,
-                pl.BlockSpec((STEP_HEADS, 64, 2 * rows), lambda g, *_: (g, 0, 0)),
+                pl.BlockSpec((STEP_HEADS, 64, rows), lambda g, *_: (g, 0, 0)),
+                pl.BlockSpec((STEP_HEADS, 64, first), lambda g, *_: (g, 0, 0)),
+                pl.BlockSpec((STEP_HEADS, 64, first), lambda g, *_: (g, 0, 0)),
                 whole((heads, 2 * rows)),
             ],
         ),
         out_shape=[
             jax.ShapeDtypeStruct((heads, 80, 2 * rows), jnp.bfloat16),
-            jax.ShapeDtypeStruct((heads, 64, 2 * rows), jnp.float32),
+            jax.ShapeDtypeStruct((heads, 64, rows), jnp.float32),
+            jax.ShapeDtypeStruct((heads, 64, first), jnp.bfloat16),
+            jax.ShapeDtypeStruct((heads, 64, first), jnp.bfloat16),
             jax.ShapeDtypeStruct((heads, 2 * rows), jnp.float32),
         ],
         compiler_params=LIMIT,
@@ -509,10 +530,17 @@
         stay(jnp.swapaxes(w_attr, 1, 2)),
     )
 
-    level, late_same, late_cross = lax.optimization_barrier((level, late_same, late_cross))
+    level, same1, cross1 = lax.optimization_barrier((level, same1, cross1))
     home = seq_swap(level, 2)
-    same1 = seq_swap(late_same, 2)
-    cross1 = seq_swap(late_cross, 3)
+    same1 = seq_swap(same1, 2)
+    cross1 = seq_swap(cross1, 3)
+    means = [
+        mean_own,
+        seq_swap(mean_part, 1),
+        grp_swap(mean_own),
+        both_swap(mean_part, 1),
+    ]
+    kx = bundle[1]
 
     lighting = jnp.take(env_table, env_ids, axis=0)
     strips = model // CHUNK
@@ -604,47 +632,50 @@
             compiler_params=LIMIT,
             name="remote",
         )(place, same, crossed, k_inv, bundle, vw, home)
-        return seq_swap(sent, 2)
-
-    back0 = remote(same0, cross0, ((0, 128), (128, 192)), 0)
-    last = 2 * (rows - first)
-    back1 = seq_swap(
-        pl.pallas_call(
-            last_kernel,
-            in_specs=[scalar] + [RESIDENT] * 6,
-            out_specs=RESIDENT,
-            out_shape=pltpu.VMEM((64 + heads, last), jnp.bfloat16),
+        return sent
+
+    back0 = remote(same0, cross0, ((0, first),), 0)
+    back0, same2, cross2 = lax.optimization_barrier((back0, same2, cross2))
+    back0 = seq_swap(back0, 2)
+    same2 = seq_swap(same2, 2)
+    cross2 = seq_swap(cross2, 3)
+
+    def attend(phase, same, crossed, *prior):
+        shapes = [((64 + heads, first), jnp.bfloat16 if phase else jnp.float32)] * (1 + phase)
+        return pl.pallas_call(
+            lambda *refs: last_kernel(phase, *refs),
+            in_specs=[scalar] + [RESIDENT] * (6 + phase),
+            out_specs=[RESIDENT] * (1 + phase),
+            out_shape=[pltpu.VMEM(*shape) for shape in shapes],
             scratch_shapes=[
-                pltpu.VMEM((64, last), jnp.float32),
-                pltpu.VMEM((heads, last), jnp.float32),
+                pltpu.VMEM((64, first), jnp.float32),
+                pltpu.VMEM((heads, first), jnp.float32),
+                pltpu.VMEM((heads, first), jnp.float32),
             ],
             compiler_params=LIMIT,
             name="last",
-        )(place, *resident(same1, cross1, k_inv, bundle[1], vw, home[:, 2 * first :])),
-        2,
-    )
-    early = pl.pallas_call(
-        early_kernel,
+        )(place, *resident(same, crossed, k_inv, kx, vw, home, *prior))
+
+    (prior,) = attend(0, same1, cross1)
+    own, other = pl.pallas_call(
+        join_kernel,
         in_specs=[RESIDENT] * 2,
-        out_specs=RESIDENT,
-        out_shape=pltpu.VMEM((64, 2 * first), jnp.float32),
+        out_specs=[RESIDENT] * 2,
+        out_shape=[pltpu.VMEM((64, first), jnp.bfloat16)] * 2,
         compiler_params=LIMIT,
-        name="early",
+        name="join",
     )(*resident(back0, mean))
-    own, other = pl.pallas_call(
-        merge_kernel,
-        in_specs=[RESIDENT] * 3,
-        out_specs=[RESIDENT] * 2,
-        out_shape=[pltpu.VMEM((64, rows), jnp.bfloat16)] * 2,
-        compiler_params=LIMIT,
-        name="merge",
-    )(*resident(back1, mean, early))
-    a1 = seq_swap(other, 1)
-    a2 = grp_swap(own)
-    a3 = both_swap(other)
+    ready = [own, seq_swap(other, 1), grp_swap(own), both_swap(other, 1)]
+    sent, passed = attend(1, same2, cross2, prior)
+    parts = [
+        seq_swap(sent, 2),
+        seq_swap(passed, 3),
+        both_swap(sent, 2),
+        both_swap(passed, 3),
+    ]
     attrs, rendered = pl.pallas_call(
         render_kernel,
-        in_specs=[pl.BlockSpec(memory_space=pltpu.SMEM)] + [RESIDENT] * 9,
+        in_specs=[scalar] + [RESIDENT] * 17,
         out_specs=[RESIDENT] * 2,
         out_shape=[
             jax.ShapeDtypeStruct((groups, patch, rows), jnp.bfloat16),
@@ -652,7 +683,7 @@
         ],
         compiler_params=LIMIT,
         name="render",
-    )(place, *resident(own, a1, a2, a3, *prepared))
+    )(place, *resident(*ready, *parts, *means, *prepared))
     return (jnp.swapaxes(attrs, 1, 2), jnp.swapaxes(rendered, 1, 2))
 
 

time: 97 us -> 94.1 us (0.970)
  waiting for transfers between devices: 20.8 us -> 5.17 us
  starting transfers between devices: 12.7 us -> 22.4 us
  Pallas kernels: 59.5 us -> 61.3 us
  local copies, waits for them, and re-layouts: 2.74 us -> 3.99 us
    ppermute x9 -> x13, waiting for transfers between devices: 20.8 us -> 5.15 us  [seq_swap(): return lax.ppermute(block, 'seq', [(i, i ^ flip) for i in range(count)])]
    pallas_call x4, Pallas kernels: 7.35 us -> 15.7 us  [the longest x2 14.5 us: attend(): pl.pallas_call(lambda *refs: last_kernel(phase, *refs), in_specs=[scalar]...]
    pallas_call x1, Pallas kernels: 18.2 us -> 11.8 us  [remote(): pl.pallas_call(lambda *refs: remote_kernel(spans, *refs), grid_spec=pltpu...]
    ppermute x1 -> x4, starting transfers between devices: 1.2 us -> 5.32 us  [both_swap(): return lax.ppermute(block, ('grp', 'seq'), route)]
    ppermute x9 -> x13, starting transfers between devices: 11.2 us -> 15.3 us  [seq_swap(): return lax.ppermute(block, 'seq', [(i, i ^ flip) for i in range(count)])]
    ppermute x1 -> x2, starting transfers between devices: 0.25 us -> 1.75 us  [grp_swap(): return lax.ppermute(block, 'grp', [(0, 1), (1, 0)])]
  transfers between devices with their start and end apart: 11 -> 19, of which waited for: 3 -> 3; matrix products, arithmetic and copies ran while one was open for 3% -> 4% of each run, Pallas kernels for 57% -> 60%
where the time goes in v6:
time: 94.1 us; the launch traced here: 93.9 us
  Pallas kernels  61.3 us (65%)
  starting transfers between devices  22.4 us (24%)
  waiting for transfers between devices  5.17 us (5%)
  local copies, waits for them, and re-layouts  3.99 us (4%)
  between operations  0.95 us (1%)
    pallas_call x1, Pallas kernels, on_device(): pl.pallas_call(local_kernel, grid_spec=pltpu.PrefetchScalarGridSpec(num_s...  21.9 us
    ppermute x13, starting transfers between devices, seq_swap(): return lax.ppermute(block, 'seq', [(i, i ^ flip) for i in range(count)])  15.3 us
    pallas_call x2, Pallas kernels, attend(): pl.pallas_call(lambda *refs: last_kernel(phase, *refs), in_specs=[scalar]...  14.5 us
    pallas_call x1, Pallas kernels, remote(): pl.pallas_call(lambda *refs: remote_kernel(spans, *refs), grid_spec=pltpu...  11.8 us
    pallas_call x1, Pallas kernels, on_device(): pl.pallas_call(prepare_kernel, grid_spec=pltpu.PrefetchScalarGridSpec(num...  6.23 us
    ppermute x4, starting transfers between devices, both_swap(): return lax.ppermute(block, ('grp', 'seq'), route)  5.32 us
    ppermute x13, waiting for transfers between devices, seq_swap(): return lax.ppermute(block, 'seq', [(i, i ^ flip) for i in range(count)])  5.15 us
    pallas_call x1, Pallas kernels, on_device(): pl.pallas_call(second_kernel, in_specs=[scalar, remain, remain, remain],...  3.5 us
  transfers between devices with their start and end apart: 19, of which 3 were waited for; matrix products, arithmetic and copies ran while one was open for 4% of the time, Pallas kernels for 60%

profile of v6, /device:TPU:1, one launch (start us, length us, event | category | flops | bytes accessed | tf_op | source)
XLA Modules:
  0.0 93.9 jit_solution(6952465174964962516)
XLA Ops:
  0.7 3.5 %second.1 = (bf16[3,256,2048]{2,1,0:T(8,128)(2,1)}, bf16[64,2048]{1,0:T(8,128)(2,1)}, bf16[64,2048]{1,0:T(8,128)(2,1)}, bf16[64,2048]{1,0:T(8,128)(2,1)}, bf16[64,2048]{1,0:T(8,128)(2,1)}) custom-call(s32[1]{0:T(128)} %bitcast.place.me.refs_0_, bf16[2,256,2048]{2,1,0:T(8,128)(2,1)} %q.5, bf16[2,256,2048]{2,1,0:T(8,128)(2,1)} %refs_3_.5, bf16[2,256,2048]{2,1,0:T(8,128)(2,1)} %v.3), custom_call_target="tpu_custom_call" | custom-call | tf_op jit(solution)/shard_map/second/pallas_call | solution.py:464
  4.2 3.3 %collective-permute-start.2 = (bf16[3,256,2048]{2,1,0:T(8,128)(2,1)}, bf16[3,256,2048]{2,1,0:T(8,128)(2,1)}, u32[]{:S(2)}, u32[]{:S(2)}) collective-permute-start(bf16[3,256,2048]{2,1,0:T(8,128)(2,1)} %get-tuple-element.33), channel_id=1, source_target_pairs={{0,1},{1,0},{2,3},{3,2},{4,5},{5,4},{6,7},{7,6},{8,9},{9,8},{10,11... | collective-permute-start | bytes 9437192 | tf_op jit(solution)/shard_map/ppermute | solution.py:22
  7.5 2.2 %first.1 = (bf16[128,2048]{1,0:T(8,128)(2,1)}, bf16[128,2048]{1,0:T(8,128)(2,1)}) custom-call(s32[1]{0:T(128)} %bitcast.place.me.refs_0_, bf16[2,256,2048]{2,1,0:T(8,128)(2,1)} %q.5), custom_call_target="tpu_custom_call" | custom-call | tf_op jit(solution)/shard_map/first/pallas_call | solution.py:453
  9.7 0.1 collective-permute-start
  9.8 1.6 %collective-permute-start.1 = (bf16[128,2048]{1,0:T(8,128)(2,1)}, bf16[128,2048]{1,0:T(8,128)(2,1)}, u32[]{:S(2)}, u32[]{:S(2)}) collective-permute-start(bf16[128,2048]{1,0:T(8,128)(2,1)} %get-tuple-element.32), channel_id=1, source_target_pairs={{0,3},{1,2},{2,1},{3,0},{4,7},{5,6},{6,5},{7,4},{8,11},{9,10},{10,... | collective-permute-start | bytes 1572872 | tf_op jit(solution)/shard_map/ppermute | solution.py:22
  11.4 1.7 %collective-permute-done.2.qx.kx.vx.refs_4_ = bf16[3,256,2048]{2,1,0:T(8,128)(2,1)} collective-permute-done((bf16[3,256,2048]{2,1,0:T(8,128)(2,1)}, bf16[3,256,2048]{2,1,0:T(8,128)(2,1)}, u32[]{:S(2)}, u32[]{:S(2)}) %collective-permute-start.2) | collective-permute-done | bytes 3145760 | tf_op jit(solution)/shard_map/ppermute | solution.py:22
  13.1 21.9 %local.1 = (bf16[16,80,512]{2,1,0:T(8,128)(2,1)S(1)}, f32[16,64,256]{2,1,0:T(8,128)S(1)}, bf16[16,64,128]{2,1,0:T(8,128)(2,1)S(1)}, bf16[16,64,128]{2,1,0:T(8,128)(2,1)S(1)}, f32[16,512]{1,0:T(8,128)S(1)}) custom-call(s32[1]{0:T(128)} %bitcast.place.me.refs_0_, s32[1]{0:T(128)} %bitcast.1.grp, s32[4]{0:T(128)S(1)} %copy-done.9, bf16[2,256,2048]{2,1,0:T(8,128)(2,1)} %q.5, ...), custom_call_target="tpu_custom_call" | custom-call | tf_op jit(solution)/shard_map/local/pallas_call | solution.py:487
  35.0 0.7 copy-done.10
  35.8 1.5 %collective-permute-start.10 = (bf16[64,2048]{1,0:T(8,128)(2,1)}, bf16[64,2048]{1,0:T(8,128)(2,1)}, u32[]{:S(2)}, u32[]{:S(2)}) collective-permute-start(bf16[64,2048]{1,0:T(8,128)(2,1)} %get-tuple-element.47), channel_id=1, source_target_pairs={{0,2},{1,3},{2,0},{3,1},{4,6},{5,7},{6,4},{7,5},{8,10},{9,11},{10,... | collective-permute-start | bytes 786440 | tf_op jit(solution)/shard_map/ppermute | solution.py:22
  37.2 0.7 collective-permute-start.11
  38.0 0.5 collective-permute-done.3.refs_6_
  38.5 11.8 %remote.1 = bf16[80,256]{1,0:T(8,128)(2,1)S(1)} custom-call(s32[1]{0:T(128)} %bitcast.place.me.refs_0_, bf16[128,2048]{1,0:T(8,128)(2,1)} %collective-permute-done.refs_1_, bf16[128,2048]{1,0:T(8,128)(2,1)} %collective-permute-done.1.refs_2_, bf16[2,256,2048]{2,1,0:T(8,128)(2,1)S(1)} %copy-done.1, ...), custom_call_target="tpu_custom_call" | custom-call | tf_op jit(solution)/shard_map/remote/pallas_call | solution.py:612
  50.3 1.1 %collective-permute-start.4 = (bf16[80,256]{1,0:T(8,128)(2,1)S(1)}, bf16[80,256]{1,0:T(8,128)(2,1)S(1)}, u32[]{:S(2)}, u32[]{:S(2)}) collective-permute-start(bf16[80,256]{1,0:T(8,128)(2,1)S(1)} %remote.1), channel_id=1, source_target_pairs={{0,2},{1,3},{2,0},{3,1},{4,6},{5,7},{6,4},{7,5},{8,10},{9,11},{10,... | collective-permute-start | bytes 122888 | tf_op jit(solution)/shard_map/ppermute | solution.py:22
  51.4 0.4 collective-permute-start.8
  51.9 2.1 %collective-permute-start.9 = (bf16[64,2048]{1,0:T(8,128)(2,1)}, bf16[64,2048]{1,0:T(8,128)(2,1)}, u32[]{:S(2)}, u32[]{:S(2)}) collective-permute-start(bf16[64,2048]{1,0:T(8,128)(2,1)} %get-tuple-element.46), channel_id=1, source_target_pairs={{0,3},{1,2},{2,1},{3,0},{4,7},{5,6},{6,5},{7,4},{8,11},{9,10},{10,... | collective-permute-start | bytes 786440 | tf_op jit(solution)/shard_map/ppermute | solution.py:22
  54.1 2.8 %collective-permute-start.5 = (bf16[64,128]{1,0:T(8,128)(2,1)S(1)}, bf16[64,128]{1,0:T(8,128)(2,1)S(1)}, u32[]{:S(2)}, u32[]{:S(2)}) collective-permute-start(bf16[64,128]{1,0:T(8,128)(2,1)S(1)} %get-tuple-element.44), channel_id=1, source_target_pairs={{0,1},{1,0},{2,3},{3,2},{4,5},{5,4},{6,7},{7,6},{8,9},{9,8},{10,11... | collective-permute-start | bytes 49160 | tf_op jit(solution)/shard_map/ppermute | solution.py:22
  56.9 1.9 %gather_fusion = bf16[512,128]{1,0:T(8,128)(2,1)} fusion(bf16[4096,128]{1,0:T(8,128)(2,1)S(1)} %copy-done, s32[1024]{0:T(1024)S(1)} %pad_clamp_fusion), kind=kCustom, calls=%fused_computation | custom fusion | bytes 264192 | tf_op jit(solution)/shard_map/jit(_take)/gather | solution.py:545
  58.8 0.3 collective-permute-start.18
  59.1 1.6 %collective-permute-start.17 = (bf16[16,64,128]{2,1,0:T(8,128)(2,1)S(1)}, bf16[16,64,128]{2,1,0:T(8,128)(2,1)S(1)}, u32[]{:S(2)}, u32[]{:S(2)}) collective-permute-start(bf16[16,64,128]{2,1,0:T(8,128)(2,1)S(1)} %get-tuple-element.51.refs_8_), channel_id=1, source_target_pairs={{0,128},{128,0},{1,129},{129,1},{2,130},{130,2},{3,131},{131,3},{4... | collective-permute-start | bytes 786440 | tf_op jit(solution)/shard_map/ppermute | solution.py:26
  60.7 2.4 %collective-permute-start.7 = (bf16[64,128]{1,0:T(8,128)(2,1)S(1)}, bf16[64,128]{1,0:T(8,128)(2,1)S(1)}, u32[]{:S(2)}, u32[]{:S(2)}) collective-permute-start(bf16[64,128]{1,0:T(8,128)(2,1)S(1)} %get-tuple-element.44), channel_id=1, source_target_pairs={{0,129},{1,128},{2,131},{3,130},{4,133},{5,132},{6,135},{7,134},{8... | collective-permute-start | bytes 49160 | tf_op jit(solution)/shard_map/ppermute | solution.py:34
  63.1 2.9 %collective-permute-done.9.refs_2_ = bf16[64,2048]{1,0:T(8,128)(2,1)} collective-permute-done((bf16[64,2048]{1,0:T(8,128)(2,1)}, bf16[64,2048]{1,0:T(8,128)(2,1)}, u32[]{:S(2)}, u32[]{:S(2)}) %collective-permute-start.9) | collective-permute-done | bytes 262176 | tf_op jit(solution)/shard_map/ppermute | solution.py:22
  66.0 0.2 collective-permute-start.6
  66.2 1.3 %slice_bitcast_fusion.refs_4_ = bf16[256,2048]{1,0:T(8,128)(2,1)S(1)} fusion(bf16[3,256,2048]{2,1,0:T(8,128)(2,1)} %collective-permute-done.2.qx.kx.vx.refs_4_), kind=kLoop, calls=%fused_computation.1 | loop fusion | bytes 2097152 | tf_op jit(solution)/shard_map/squeeze | solution.py:543
  67.5 7.1 %last.2.refs_7_ = f32[80,128]{1,0:T(8,128)S(1)} custom-call(s32[1]{0:T(128)} %bitcast.place.me.refs_0_, bf16[64,2048]{1,0:T(8,128)(2,1)} %collective-permute-done.10.refs_1_, bf16[64,2048]{1,0:T(8,128)(2,1)} %collective-permute-done.11.refs_2_, bf16[2,256,2048]{2,1,0:T(8,128)(2,1)S(1)} %copy-done.1, bf16[256,2048]{1,0:T(8,128)(2,1)S(1)} %slice_bitcast_fusion.refs_4_, ...), custom_call_target="tpu_custom_call" | custom-call | tf_op jit(solution)/shard_map/last/pallas_call | solution.py:645
  74.7 7.3 %last.3 = (bf16[80,128]{1,0:T(8,128)(2,1)S(1)}, bf16[80,128]{1,0:T(8,128)(2,1)S(1)}) custom-call(s32[1]{0:T(128)} %bitcast.place.me.refs_0_, bf16[64,2048]{1,0:T(8,128)(2,1)} %collective-permute-done.8.refs_1_, bf16[64,2048]{1,0:T(8,128)(2,1)} %collective-permute-done.9.refs_2_, bf16[2,256,2048]{2,1,0:T(8,128)(2,1)S(1)} %copy-done.1, ...), custom_call_target="tpu_custom_call" | custom-call | tf_op jit(solution)/shard_map/last/pallas_call | solution.py:645
  82.1 1.1 %collective-permute-start.12 = (bf16[80,128]{1,0:T(8,128)(2,1)S(1)}, bf16[80,128]{1,0:T(8,128)(2,1)S(1)}, u32[]{:S(2)}, u32[]{:S(2)}) collective-permute-start(bf16[80,128]{1,0:T(8,128)(2,1)S(1)} %get-tuple-element.49), channel_id=1, source_target_pairs={{0,2},{1,3},{2,0},{3,1},{4,6},{5,7},{6,4},{7,5},{8,10},{9,11},{10,... | collective-permute-start | bytes 61448 | tf_op jit(solution)/shard_map/ppermute | solution.py:22
  83.2 1.4 %collective-permute-start.14 = (bf16[80,128]{1,0:T(8,128)(2,1)S(1)}, bf16[80,128]{1,0:T(8,128)(2,1)S(1)}, u32[]{:S(2)}, u32[]{:S(2)}) collective-permute-start(bf16[80,128]{1,0:T(8,128)(2,1)S(1)} %get-tuple-element.49), channel_id=1, source_target_pairs={{0,130},{1,131},{2,128},{3,129},{4,134},{5,135},{6,132},{7,133},{8... | collective-permute-start | bytes 61448 | tf_op jit(solution)/shard_map/ppermute | solution.py:34
  84.6 0.5 collective-permute-start.13
  85.1 1.2 %collective-permute-start.15 = (bf16[80,128]{1,0:T(8,128)(2,1)S(1)}, bf16[80,128]{1,0:T(8,128)(2,1)S(1)}, u32[]{:S(2)}, u32[]{:S(2)}) collective-permute-start(bf16[80,128]{1,0:T(8,128)(2,1)S(1)} %get-tuple-element.50), channel_id=1, source_target_pairs={{0,131},{1,130},{2,129},{3,128},{4,135},{5,134},{6,133},{7,132},{8... | collective-permute-start | bytes 61448 | tf_op jit(solution)/shard_map/ppermute | solution.py:34
  86.3 0.1 broadcast_select_fusion.light
  86.5 6.2 %prepare.1 = (bf16[768,256]{1,0:T(8,128)(2,1)S(1)}, f32[2,256,256]{2,1,0:T(8,128)S(1)}, f32[2,64,256]{2,1,0:T(8,128)S(1)}, f32[2,8,256]{2,1,0:T(8,128)S(1)}, f32[2,64,128]{2,1,0:T(8,128)S(1)}) custom-call(s32[1]{0:T(128)} %bitcast.place.me.refs_0_, s32[1]{0:T(128)} %bitcast.1.grp, s32[4]{0:T(128)S(1)} %copy-done.9, bf16[4,64,4096]{2,1,0:T(8,128)(2,1)S(1)} %copy-done.2, ...), custom_call_target="tpu_custom_call" | custom-call | tf_op jit(solution)/shard_map/prepare/pallas_call | solution.py:568
  92.8 1.2 %render.1 = (bf16[2,64,256]{2,1,0:T(8,128)(2,1)}, bf16[2,64,256]{2,1,0:T(8,128)(2,1)}) custom-call(s32[1]{0:T(128)} %bitcast.place.me.refs_0_, bf16[64,128]{1,0:T(8,128)(2,1)S(1)} %get-tuple-element.43.refs_0_, bf16[64,128]{1,0:T(8,128)(2,1)S(1)} %collective-permute-done.5.refs_1_, bf16[64,128]{1,0:T(8,128)(2,1)S(1)} %collective-permute-done.6.refs_2_, ...), custom_call_target="tpu_custom_call" | custom-call | tf_op jit(solution)/shard_map/render/pallas_call | solution.py:676
  (48 shorter events, 0.2 us)
Async XLA Ops:
  0.6 56.2 %copy-start = (bf16[4096,128]{1,0:T(8,128)(2,1)S(1)}, bf16[4096,128]{1,0:T(8,128)(2,1)}, u32[]{:S(2)}) copy-start(bf16[4096,128]{1,0:T(8,128)(2,1)} %param.18) | copy-start | bytes 3145732
  4.2 8.9 %copy-start.9 = (s32[4]{0:T(128)S(1)}, s32[4]{0:T(128)}, u32[]{:S(2)}) copy-start(s32[4]{0:T(128)} %kinds.3) | copy-start | bytes 52
  4.2 8.9 %collective-permute-start.2 = (bf16[3,256,2048]{2,1,0:T(8,128)(2,1)}, bf16[3,256,2048]{2,1,0:T(8,128)(2,1)}, u32[]{:S(2)}, u32[]{:S(2)}) collective-permute-start(bf16[3,256,2048]{2,1,0:T(8,128)(2,1)} %get-tuple-element.33), channel_id=1, source_target_pairs={{0,1},{1,0},{2,3},{3,2},{4,5},{5,4},{6,7},{7,6},{8,9},{9,8},{10,11... | collective-permute-start | bytes 9437192 | tf_op jit(solution)/shard_map/ppermute | solution.py:22
  9.7 28.3 %collective-permute-start = (bf16[128,2048]{1,0:T(8,128)(2,1)}, bf16[128,2048]{1,0:T(8,128)(2,1)}, u32[]{:S(2)}, u32[]{:S(2)}) collective-permute-start(bf16[128,2048]{1,0:T(8,128)(2,1)} %get-tuple-element.31), channel_id=1, source_target_pairs={{0,2},{1,3},{2,0},{3,1},{4,6},{5,7},{6,4},{7,5},{8,10},{9,11},{10,... | collective-permute-start | bytes 1572872 | tf_op jit(solution)/shard_map/ppermute | solution.py:22
  9.8 28.2 %collective-permute-start.1 = (bf16[128,2048]{1,0:T(8,128)(2,1)}, bf16[128,2048]{1,0:T(8,128)(2,1)}, u32[]{:S(2)}, u32[]{:S(2)}) collective-permute-start(bf16[128,2048]{1,0:T(8,128)(2,1)} %get-tuple-element.32), channel_id=1, source_target_pairs={{0,3},{1,2},{2,1},{3,0},{4,7},{5,6},{6,5},{7,4},{8,11},{9,10},{10,... | collective-permute-start | bytes 1572872 | tf_op jit(solution)/shard_map/ppermute | solution.py:22
  13.1 22.7 %copy-start.12 = (s32[2,256]{1,0:T(2,128)S(1)}, s32[2,256]{1,0:T(2,128)}, u32[]{:S(2)}) copy-start(s32[2,256]{1,0:T(2,128)} %param.17) | copy-start | bytes 6148
  13.1 25.4 %copy-start.1 = (bf16[2,256,2048]{2,1,0:T(8,128)(2,1)S(1)}, bf16[2,256,2048]{2,1,0:T(8,128)(2,1)}, u32[]{:S(2)}) copy-start(bf16[2,256,2048]{2,1,0:T(8,128)(2,1)} %refs_3_.5) | copy-start | bytes 6291460
  35.0 0.7 copy-start.10
  35.7 14.5 %copy-start.3 = (bf16[16,80,512]{2,1,0:T(8,128)(2,1)}, bf16[16,80,512]{2,1,0:T(8,128)(2,1)S(1)}, u32[]{:S(2)}) copy-start(bf16[16,80,512]{2,1,0:T(8,128)(2,1)S(1)} %get-tuple-element.34.refs_5_) | copy-start | bytes 3932164
  35.8 2.8 %collective-permute-start.3 = (f32[16,512]{1,0:T(8,128)S(1)}, f32[16,512]{1,0:T(8,128)S(1)}, u32[]{:S(2)}, u32[]{:S(2)}) collective-permute-start(f32[16,512]{1,0:T(8,128)S(1)} %get-tuple-element.38), channel_id=1, source_target_pairs={{0,2},{1,3},{2,0},{3,1},{4,6},{5,7},{6,4},{7,5},{8,10},{9,11},{10,... | collective-permute-start | bytes 98312 | tf_op jit(solution)/shard_map/ppermute | solution.py:22
  35.8 23.1 %collective-permute-start.10 = (bf16[64,2048]{1,0:T(8,128)(2,1)}, bf16[64,2048]{1,0:T(8,128)(2,1)}, u32[]{:S(2)}, u32[]{:S(2)}) collective-permute-start(bf16[64,2048]{1,0:T(8,128)(2,1)} %get-tuple-element.47), channel_id=1, source_target_pairs={{0,2},{1,3},{2,0},{3,1},{4,6},{5,7},{6,4},{7,5},{8,10},{9,11},{10,... | collective-permute-start | bytes 786440 | tf_op jit(solution)/shard_map/ppermute | solution.py:22
  37.2 21.9 %collective-permute-start.11 = (bf16[64,2048]{1,0:T(8,128)(2,1)}, bf16[64,2048]{1,0:T(8,128)(2,1)}, u32[]{:S(2)}, u32[]{:S(2)}) collective-permute-start(bf16[64,2048]{1,0:T(8,128)(2,1)} %get-tuple-element.48), channel_id=1, source_target_pairs={{0,3},{1,2},{2,1},{3,0},{4,7},{5,6},{6,5},{7,4},{8,11},{9,10},{10,... | collective-permute-start | bytes 786440 | tf_op jit(solution)/shard_map/ppermute | solution.py:22
  50.3 3.7 %collective-permute-start.4 = (bf16[80,256]{1,0:T(8,128)(2,1)S(1)}, bf16[80,256]{1,0:T(8,128)(2,1)S(1)}, u32[]{:S(2)}, u32[]{:S(2)}) collective-permute-start(bf16[80,256]{1,0:T(8,128)(2,1)S(1)} %remote.1), channel_id=1, source_target_pairs={{0,2},{1,3},{2,0},{3,1},{4,6},{5,7},{6,4},{7,5},{8,10},{9,11},{10,... | collective-permute-start | bytes 122888 | tf_op jit(solution)/shard_map/ppermute | solution.py:22
  51.4 9.3 %collective-permute-start.8 = (bf16[64,2048]{1,0:T(8,128)(2,1)}, bf16[64,2048]{1,0:T(8,128)(2,1)}, u32[]{:S(2)}, u32[]{:S(2)}) collective-permute-start(bf16[64,2048]{1,0:T(8,128)(2,1)} %get-tuple-element.45), channel_id=1, source_target_pairs={{0,2},{1,3},{2,0},{3,1},{4,6},{5,7},{6,4},{7,5},{8,10},{9,11},{10,... | collective-permute-start | bytes 786440 | tf_op jit(solution)/shard_map/ppermute | solution.py:22
  51.9 14.2 %collective-permute-start.9 = (bf16[64,2048]{1,0:T(8,128)(2,1)}, bf16[64,2048]{1,0:T(8,128)(2,1)}, u32[]{:S(2)}, u32[]{:S(2)}) collective-permute-start(bf16[64,2048]{1,0:T(8,128)(2,1)} %get-tuple-element.46), channel_id=1, source_target_pairs={{0,3},{1,2},{2,1},{3,0},{4,7},{5,6},{6,5},{7,4},{8,11},{9,10},{10,... | collective-permute-start | bytes 786440 | tf_op jit(solution)/shard_map/ppermute | solution.py:22
  54.1 4.7 %collective-permute-start.5 = (bf16[64,128]{1,0:T(8,128)(2,1)S(1)}, bf16[64,128]{1,0:T(8,128)(2,1)S(1)}, u32[]{:S(2)}, u32[]{:S(2)}) collective-permute-start(bf16[64,128]{1,0:T(8,128)(2,1)S(1)} %get-tuple-element.44), channel_id=1, source_target_pairs={{0,1},{1,0},{2,3},{3,2},{4,5},{5,4},{6,7},{7,6},{8,9},{9,8},{10,11... | collective-permute-start | bytes 49160 | tf_op jit(solution)/shard_map/ppermute | solution.py:22
  58.8 8.7 %copy-start.4 = (bf16[16,80,512]{2,1,0:T(8,128)(2,1)S(1)}, bf16[16,80,512]{2,1,0:T(8,128)(2,1)}, u32[]{:S(2)}) copy-start(bf16[16,80,512]{2,1,0:T(8,128)(2,1)} %copy-done.3) | copy-start | bytes 3932164
  58.8 25.8 %collective-permute-start.16 = (bf16[16,64,128]{2,1,0:T(8,128)(2,1)}, bf16[16,64,128]{2,1,0:T(8,128)(2,1)S(1)}, u32[]{:S(2)}, u32[]{:S(2)}) collective-permute-start(bf16[16,64,128]{2,1,0:T(8,128)(2,1)} %copy-done.10), channel_id=1, source_target_pairs={{0,1},{1,0},{2,3},{3,2},{4,5},{5,4},{6,7},{7,6},{8,9},{9,8},{10,11... | collective-permute-start | bytes 786440 | tf_op jit(solution)/shard_map/ppermute | solution.py:22
  58.8 33.9 %collective-permute-start.18 = (bf16[16,64,128]{2,1,0:T(8,128)(2,1)}, bf16[16,64,128]{2,1,0:T(8,128)(2,1)S(1)}, u32[]{:S(2)}, u32[]{:S(2)}) collective-permute-start(bf16[16,64,128]{2,1,0:T(8,128)(2,1)} %copy-done.10), channel_id=1, source_target_pairs={{0,129},{1,128},{2,131},{3,130},{4,133},{5,132},{6,135},{7,134},{8... | collective-permute-start | bytes 786440 | tf_op jit(solution)/shard_map/ppermute | solution.py:34
  59.1 26.0 %collective-permute-start.17 = (bf16[16,64,128]{2,1,0:T(8,128)(2,1)S(1)}, bf16[16,64,128]{2,1,0:T(8,128)(2,1)S(1)}, u32[]{:S(2)}, u32[]{:S(2)}) collective-permute-start(bf16[16,64,128]{2,1,0:T(8,128)(2,1)S(1)} %get-tuple-element.51.refs_8_), channel_id=1, source_target_pairs={{0,128},{128,0},{1,129},{129,1},{2,130},{130,2},{3,131},{131,3},{4... | collective-permute-start | bytes 786440 | tf_op jit(solution)/shard_map/ppermute | solution.py:26
  60.7 22.5 %collective-permute-start.7 = (bf16[64,128]{1,0:T(8,128)(2,1)S(1)}, bf16[64,128]{1,0:T(8,128)(2,1)S(1)}, u32[]{:S(2)}, u32[]{:S(2)}) collective-permute-start(bf16[64,128]{1,0:T(8,128)(2,1)S(1)} %get-tuple-element.44), channel_id=1, source_target_pairs={{0,129},{1,128},{2,131},{3,130},{4,133},{5,132},{6,135},{7,134},{8... | collective-permute-start | bytes 49160 | tf_op jit(solution)/shard_map/ppermute | solution.py:34
  66.0 16.0 %collective-permute-start.6 = (bf16[64,128]{1,0:T(8,128)(2,1)S(1)}, bf16[64,128]{1,0:T(8,128)(2,1)S(1)}, u32[]{:S(2)}, u32[]{:S(2)}) collective-permute-start(bf16[64,128]{1,0:T(8,128)(2,1)S(1)} %get-tuple-element.43.refs_0_), channel_id=1, source_target_pairs={{0,128},{128,0},{1,129},{129,1},{2,130},{130,2},{3,131},{131,3},{4... | collective-permute-start | bytes 49160 | tf_op jit(solution)/shard_map/ppermute | solution.py:26
  74.6 11.6 %copy-start.11 = (bf16[512,128]{1,0:T(8,128)(2,1)S(1)}, bf16[512,128]{1,0:T(8,128)(2,1)}, u32[]{:S(2)}) copy-start(bf16[512,128]{1,0:T(8,128)(2,1)} %gather_fusion) | copy-start | bytes 393220
  74.6 11.8 %copy-start.2 = (bf16[4,64,4096]{2,1,0:T(8,128)(2,1)S(1)}, bf16[4,64,4096]{2,1,0:T(8,128)(2,1)}, u32[]{:S(2)}) copy-start(bf16[4,64,4096]{2,1,0:T(8,128)(2,1)} %w3.1) | copy-start | bytes 6291460
  74.7 11.8 %copy-start.5 = (bf16[128,4096]{1,0:T(8,128)(2,1)S(1)}, bf16[128,4096]{1,0:T(8,128)(2,1)}, u32[]{:S(2)}) copy-start(bf16[128,4096]{1,0:T(8,128)(2,1)} %w_env.1) | copy-start | bytes 3145732
  74.7 11.8 %copy-start.6 = (bf16[4096,64]{0,1:T(8,128)(2,1)S(1)}, bf16[4096,64]{0,1:T(8,128)(2,1)}, u32[]{:S(2)}) copy-start(bf16[4096,64]{0,1:T(8,128)(2,1)} %param.23) | copy-start | bytes 1572868
  74.7 11.8 %copy-start.7 = (bf16[2,4096]{1,0:T(2,128)(2,1)S(1)}, bf16[2,4096]{1,0:T(2,128)(2,1)}, u32[]{:S(2)}) copy-start(bf16[2,4096]{1,0:T(2,128)(2,1)} %scale.1) | copy-start | bytes 49156
  74.7 11.8 %copy-start.8 = (bf16[2,4096]{1,0:T(2,128)(2,1)S(1)}, bf16[2,4096]{1,0:T(2,128)(2,1)}, u32[]{:S(2)}) copy-start(bf16[2,4096]{1,0:T(2,128)(2,1)} %shift.1) | copy-start | bytes 49156
  82.1 10.7 %collective-permute-start.12 = (bf16[80,128]{1,0:T(8,128)(2,1)S(1)}, bf16[80,128]{1,0:T(8,128)(2,1)S(1)}, u32[]{:S(2)}, u32[]{:S(2)}) collective-permute-start(bf16[80,128]{1,0:T(8,128)(2,1)S(1)} %get-tuple-element.49), channel_id=1, source_target_pairs={{0,2},{1,3},{2,0},{3,1},{4,6},{5,7},{6,4},{7,5},{8,10},{9,11},{10,... | collective-permute-start | bytes 61448 | tf_op jit(solution)/shard_map/ppermute | solution.py:22
  83.2 9.6 %collective-permute-start.14 = (bf16[80,128]{1,0:T(8,128)(2,1)S(1)}, bf16[80,128]{1,0:T(8,128)(2,1)S(1)}, u32[]{:S(2)}, u32[]{:S(2)}) collective-permute-start(bf16[80,128]{1,0:T(8,128)(2,1)S(1)} %get-tuple-element.49), channel_id=1, source_target_pairs={{0,130},{1,131},{2,128},{3,129},{4,134},{5,135},{6,132},{7,133},{8... | collective-permute-start | bytes 61448 | tf_op jit(solution)/shard_map/ppermute | solution.py:34
  84.6 8.1 %collective-permute-start.13 = (bf16[80,128]{1,0:T(8,128)(2,1)S(1)}, bf16[80,128]{1,0:T(8,128)(2,1)S(1)}, u32[]{:S(2)}, u32[]{:S(2)}) collective-permute-start(bf16[80,128]{1,0:T(8,128)(2,1)S(1)} %get-tuple-element.50), channel_id=1, source_target_pairs={{0,3},{1,2},{2,1},{3,0},{4,7},{5,6},{6,5},{7,4},{8,11},{9,10},{10,... | collective-permute-start | bytes 61448 | tf_op jit(solution)/shard_map/ppermute | solution.py:22
  85.1 7.7 %collective-permute-start.15 = (bf16[80,128]{1,0:T(8,128)(2,1)S(1)}, bf16[80,128]{1,0:T(8,128)(2,1)S(1)}, u32[]{:S(2)}, u32[]{:S(2)}) collective-permute-start(bf16[80,128]{1,0:T(8,128)(2,1)S(1)} %get-tuple-element.50), channel_id=1, source_target_pairs={{0,131},{1,130},{2,129},{3,128},{4,135},{5,134},{6,133},{7,132},{8... | collective-permute-start | bytes 61448 | tf_op jit(solution)/shard_map/ppermute | solution.py:34

commit v7 on v6

--- a/solution.py
+++ b/solution.py
@@ -120,15 +120,18 @@
         copy.wait()
 
 
-def second_kernel(place, q, k, v, bundle, sb, cb, sc, cc, held, rest, arrive, leave):
+def second_kernel(place, q, k, v, bundle, sb, cb, s1, c1, s2, c2, held, rest, arrive, leave):
     me = place[0]
-    count = sb.shape[0]
+    count, width = sb.shape
     start = q.shape[1] - 2 * count
+    left, right = pl.ds(0, width // 2), pl.ds(width // 2, width // 2)
     pieces = [(a.at[1 - me], held.at[n], bundle.at[n]) for n, a in enumerate((q, k, v))]
-    for n, (same, cross) in enumerate(((sb, cb), (sc, cc))):
-        span = pl.ds(start + n * count, count)
-        pieces.append((q.at[me, span], rest.at[2 * n], same))
-        pieces.append((q.at[1 - me, span], rest.at[2 * n + 1], cross))
+    for n, group, same, first, later in ((0, me, sb, s1, s2), (1, 1 - me, cb, c1, c2)):
+        span = pl.ds(start, count)
+        pieces.append((q.at[group, span], rest.at[n], same))
+        span = pl.ds(start + count, count)
+        for cols, target in ((left, first), (right, later)):
+            pieces.append((q.at[group, span, cols], rest.at[2 + n, :, cols], target))
     shuttle(pieces, arrive, leave)
 
 
@@ -233,17 +236,27 @@
     )
 
 
-def last_kernel(phase, place, qs, qd, k, kx, vw, home, *refs):
-    prior, outs, (acc, share, near) = refs[:phase], refs[phase:-3], refs[-3:]
+def last_kernel(stage, place, qs, qd, k, kx, vw, home, *refs):
+    prior, outs, (acc, share, near) = refs[:stage], refs[stage:-3], refs[-3:]
     me = place[0]
-    heads = vw.shape[0]
-    near[...] = halves(home[:, 256:384], home[:, 384:512])[phase]
+    base = vw.shape[0] // 2 if stage == 2 else 0
+    heads = base + qs.shape[1] // HD
+    near[...] = halves(home[:, 256:384], home[:, 384:512])[1 if stage else 0]
     zero = jnp.zeros((2 * qs.shape[0], HD), jnp.bfloat16)
-
-    def scores_at(start):
-        cols = pl.ds(start, 2 * HD)
+    if stage == 2:
+        seed = prior[1][:64]
+        share[:base] = prior[1][64 : 64 + base]
+    else:
+        seed = jnp.zeros(acc.shape, jnp.float32)
+
+    def scores_at(head):
+        cols = pl.ds(head * HD, 2 * HD)
+        near_cols = pl.ds((head - base) * HD, 2 * HD)
+        if not isinstance(head, int):
+            cols = pl.ds(pl.multiple_of(head * HD, 2 * HD), 2 * HD)
+            near_cols = pl.ds(pl.multiple_of((head - base) * HD, 2 * HD), 2 * HD)
         keys = jnp.concatenate((k[me, :, cols], kx[:, cols]), axis=0)
-        pair = jnp.concatenate((qs[:, cols], qd[:, cols]), axis=0)
+        pair = jnp.concatenate((qs[:, near_cols], qd[:, near_cols]), axis=0)
         queries = jnp.concatenate(
             (
                 jnp.concatenate((pair[:, :HD], zero), axis=1),
@@ -279,13 +292,13 @@
             found.append((summed[:64] * (mine / total), level))
         return found
 
-    gathered = jnp.zeros(acc.shape, jnp.float32)
+    gathered = seed
     levels = []
-    ahead = scores_at(0)
-    for head in range(0, heads, 2):
+    ahead = scores_at(base)
+    for head in range(base, heads, 2):
         scores = ahead
         if head + 2 < heads:
-            ahead = scores_at((head + 2) * HD)
+            ahead = scores_at(head + 2)
         for piece, level in finish(head, scores, None):
             gathered = gathered + piece
             levels.append(level)
@@ -293,20 +306,20 @@
 
     @pl.when(jnp.logical_not(worst(levels) < SAFE))
     def _():
-        acc[...] = jnp.zeros_like(acc)
+        acc[...] = seed
 
         def body(n, carry):
-            scores = scores_at(pl.multiple_of(n * 2 * HD, 2 * HD))
+            scores = scores_at(base + 2 * n)
             top = jnp.maximum(*(jnp.max(s, axis=0, keepdims=True) for s in scores))
-            for piece, _ in finish(2 * n, scores, top):
+            for piece, _ in finish(base + 2 * n, scores, top):
                 acc[...] += piece
             return carry
 
-        lax.fori_loop(0, heads // 2, body, 0)
-
-    if phase == 0:
+        lax.fori_loop(0, (heads - base) // 2, body, 0)
+
+    if stage < 2:
         outs[0][:64] = acc[...]
-        outs[0][64:] = share[...]
+        outs[0][64 : 64 + heads] = share[:heads]
     else:
         for a, b, now in ((0, 64, acc), (64, 64 + heads, share)):
             own, part = halves(prior[0][a:b], now[...])
@@ -329,19 +342,17 @@
     other[...] = found[:, half:]
 
 
-def prepare_kernel(
-    me, grp, kinds, w0, w1, w2, w3, w_env, final, scale, shift, light,
-    mixer, cross, direct, base, bias, reads, gram, column, sums, shifts,
-):
-    step = pl.program_id(0)
+def begin_kernel(me, grp, kinds, w0, w1, w2, w3, w_env, final, scale, shift, *sums):
+    @pl.when(pl.program_id(0) == 0)
+    def _():
+        for ref in sums:
+            ref[...] = jnp.zeros_like(ref)
+
+    gather_weights(w0, w1, w2, w3, w_env, final, scale, shift, *sums)
+
+
+def gather_weights(w0, w1, w2, w3, w_env, final, scale, shift, reads, gram, column, sums, shifts):
     lights = scale.shape[0]
-    width = pl.num_programs(0) * w0.shape[1]
-
-    @pl.when(step == 0)
-    def _():
-        for ref in (reads, gram, column, sums, shifts):
-            ref[...] = jnp.zeros_like(ref)
-
     rows = jnp.concatenate((w0[...], w1[...], w2[...], w3[...], w_env[...]), axis=0)
     weight = final[...].astype(jnp.float32)
 
@@ -361,6 +372,21 @@
     reads[...] += dot_lanes(jnp.concatenate(gains + [ones], axis=0), rows)
     gram[...] += dot_lanes(rows, rows)
     column[...] += dot_lanes(rows, jnp.ones((128, rows.shape[1]), jnp.bfloat16))
+
+
+def prepare_kernel(me, grp, kinds, w0, w1, w2, w3, w_env, final, scale, shift, light, *refs):
+    partial, (mixer, cross, direct, base, bias), sums = refs[:5], refs[5:10], refs[10:]
+    step = pl.program_id(0)
+    lights = scale.shape[0]
+    width = 2 * pl.num_programs(0) * w0.shape[1]
+
+    @pl.when(step == 0)
+    def _():
+        for ref, start in zip(sums, partial):
+            ref[...] = start[...]
+
+    gather_weights(w0, w1, w2, w3, w_env, final, scale, shift, *sums)
+    reads, gram, column, sums, shifts = sums
 
     @pl.when(step == pl.num_programs(0) - 1)
     def _():
@@ -461,21 +487,64 @@
     )(place, stay(q_inv))
     same0 = seq_swap(ahead, 2)
     cross0 = seq_swap(behind, 3)
-    bundle, same1, cross1, same2, cross2 = pl.pallas_call(
+    bundle, same1, cross1, *late = pl.pallas_call(
         second_kernel,
         in_specs=[scalar, remain, remain, remain],
-        out_specs=[remain] * 5,
+        out_specs=[remain] * 7,
         out_shape=[pltpu.HBM((3, rows, width), jnp.bfloat16)]
-        + [pltpu.HBM((piece, width), jnp.bfloat16)] * 4,
+        + [pltpu.HBM((piece, width), jnp.bfloat16)] * 2
+        + [pltpu.HBM((piece, width // 2), jnp.bfloat16)] * 4,
         scratch_shapes=[
             pltpu.VMEM((3, rows, width), jnp.bfloat16),
             pltpu.VMEM((4, piece, width), jnp.bfloat16),
         ]
-        + [pltpu.SemaphoreType.DMA((7,))] * 2,
+        + [pltpu.SemaphoreType.DMA((9,))] * 2,
         compiler_params=LIMIT,
         name="second",
     )(place, stay(q_inv), stay(k_inv), stay(v_inv))
     bundle = seq_swap(bundle, 1)
+
+    kinds = 4 * patch
+    inputs = kinds + channels
+    strips = model // CHUNK // 2
+
+    def sweep(start):
+        chosen = [
+            pl.BlockSpec(
+                (None, patch, CHUNK),
+                lambda g, m, r, t, n=n: (
+                    t[2 * (r[0] if n < 2 else 1 - r[0]) + (1 - m[0] if n % 2 else m[0])],
+                    0,
+                    g + start,
+                ),
+            )
+            for n in range(4)
+        ]
+        return chosen + [
+            pl.BlockSpec((count, CHUNK), lambda g, *_: (0, g + start))
+            for count in (channels, patch, lights, lights)
+        ]
+
+    sums = [
+        (2 * lights * patch + 16, inputs),
+        (inputs, inputs),
+        (inputs, 128),
+        (lights, patch, 128),
+        (lights, patch, 128),
+    ]
+    weights = (w_embed_attr,) * 4 + (w_embed_env, w_final.T, mod_scale, mod_shift)
+    partial = pl.pallas_call(
+        begin_kernel,
+        grid_spec=pltpu.PrefetchScalarGridSpec(
+            num_scalar_prefetch=3,
+            grid=(strips,),
+            in_specs=sweep(0),
+            out_specs=[whole(shape) for shape in sums],
+        ),
+        out_shape=[jax.ShapeDtypeStruct(shape, jnp.float32) for shape in sums],
+        compiler_params=LIMIT,
+        name="begin",
+    )(place, side, group_ids, *(stay(w) for w in weights))
 
     cols = STEP_HEADS * HD
     steps = heads // STEP_HEADS
@@ -496,9 +565,7 @@
                 given[1],
                 picked,
                 given[2],
-                pl.BlockSpec(
-                    (None, patch, cols), lambda g, m, r, t: (t[2 * r[0] + m[0]], 0, g)
-                ),
+                pl.BlockSpec((None, patch, cols), lambda g, m, r, t: (t[2 * r[0] + m[0]], 0, g)),
             ],
             out_specs=[
                 reads,
@@ -543,21 +610,6 @@
     kx = bundle[1]
 
     lighting = jnp.take(env_table, env_ids, axis=0)
-    strips = model // CHUNK
-    weights = [
-        pl.BlockSpec(
-            (None, patch, CHUNK),
-            lambda g, m, r, t, n=n: (
-                t[2 * (r[0] if n < 2 else 1 - r[0]) + (1 - m[0] if n % 2 else m[0])],
-                0,
-                g,
-            ),
-        )
-        for n in range(4)
-    ]
-    strip = lambda count: pl.BlockSpec((count, CHUNK), lambda g, *_: (0, g))
-    kinds = 4 * patch
-    inputs = kinds + channels
     out_shapes = [
         pltpu.VMEM((2 * kinds + 2 * lights * patch, kinds), jnp.bfloat16),
         pltpu.VMEM((lights, kinds, rows), jnp.float32),
@@ -570,40 +622,16 @@
         grid_spec=pltpu.PrefetchScalarGridSpec(
             num_scalar_prefetch=3,
             grid=(strips,),
-            in_specs=weights
-            + [
-                strip(channels),
-                strip(patch),
-                strip(lights),
-                strip(lights),
-                whole((lights, rows, channels)),
-            ],
+            in_specs=sweep(strips)
+            + [whole((lights, rows, channels))]
+            + [whole(shape) for shape in sums],
             out_specs=[whole(s.shape) for s in out_shapes],
-            scratch_shapes=[
-                pltpu.VMEM((2 * lights * patch + 16, inputs), jnp.float32),
-                pltpu.VMEM((inputs, inputs), jnp.float32),
-                pltpu.VMEM((inputs, 128), jnp.float32),
-                pltpu.VMEM((lights, patch, 128), jnp.float32),
-                pltpu.VMEM((lights, patch, 128), jnp.float32),
-            ],
+            scratch_shapes=[pltpu.VMEM(shape, jnp.float32) for shape in sums],
         ),
         out_shape=out_shapes,
         compiler_params=LIMIT,
         name="prepare",
-    )(
-        place,
-        side,
-        group_ids,
-        w_embed_attr,
-        w_embed_attr,
-        w_embed_attr,
-        w_embed_attr,
-        w_embed_env,
-        w_final.T,
-        mod_scale,
-        mod_shift,
-        lighting,
-    )
+    )(place, side, group_ids, *weights, lighting, *partial)
 
     def remote(same, crossed, spans, lane):
         count = same.shape[0]
@@ -635,17 +663,18 @@
         return sent
 
     back0 = remote(same0, cross0, ((0, first),), 0)
-    back0, same2, cross2 = lax.optimization_barrier((back0, same2, cross2))
+    back0, *late = lax.optimization_barrier((back0, *late))
     back0 = seq_swap(back0, 2)
-    same2 = seq_swap(same2, 2)
-    cross2 = seq_swap(cross2, 3)
-
-    def attend(phase, same, crossed, *prior):
-        shapes = [((64 + heads, first), jnp.bfloat16 if phase else jnp.float32)] * (1 + phase)
+    same2, cross2 = seq_swap(late[0], 2), seq_swap(late[1], 3)
+    same3, cross3 = seq_swap(late[2], 2), seq_swap(late[3], 3)
+
+    def attend(stage, same, crossed, *prior):
+        last = stage == 2
+        shapes = [((64 + heads, first), jnp.bfloat16 if last else jnp.float32)] * (1 + last)
         return pl.pallas_call(
-            lambda *refs: last_kernel(phase, *refs),
-            in_specs=[scalar] + [RESIDENT] * (6 + phase),
-            out_specs=[RESIDENT] * (1 + phase),
+            lambda *refs: last_kernel(stage, *refs),
+            in_specs=[scalar] + [RESIDENT] * (6 + stage),
+            out_specs=[RESIDENT] * (1 + last),
             out_shape=[pltpu.VMEM(*shape) for shape in shapes],
             scratch_shapes=[
                 pltpu.VMEM((64, first), jnp.float32),
@@ -666,13 +695,10 @@
         name="join",
     )(*resident(back0, mean))
     ready = [own, seq_swap(other, 1), grp_swap(own), both_swap(other, 1)]
-    sent, passed = attend(1, same2, cross2, prior)
-    parts = [
-        seq_swap(sent, 2),
-        seq_swap(passed, 3),
-        both_swap(sent, 2),
-        both_swap(passed, 3),
-    ]
+    (half,) = attend(1, same2, cross2, prior)
+    sent, passed = attend(2, same3, cross3, prior, half)
+    far = [both_swap(sent, 2), both_swap(passed, 3)]
+    parts = [seq_swap(sent, 2), seq_swap(passed, 3)] + far
     attrs, rendered = pl.pallas_call(
         render_kernel,
         in_specs=[scalar] + [RESIDENT] * 17,

time: 94.1 us -> 109 us (1.16)
  waiting for transfers between devices: 5.17 us -> 16.8 us
  Pallas kernels: 61.3 us -> 63.6 us
  starting transfers between devices: 22.4 us -> 23.7 us
    ppermute x13 -> x15, waiting for transfers between devices: 5.15 us -> 16.8 us  [seq_swap(): return lax.ppermute(block, 'seq', [(i, i ^ flip) for i in range(count)])]
    pallas_call x2 -> x4, Pallas kernels: 14.5 us -> 19.2 us  [the longest x3 14.6 us: attend(): pl.pallas_call(lambda *refs: last_kernel(stage, *refs), in_specs=[scalar]...]
    pallas_call x1, Pallas kernels: 6.23 us -> 3.77 us  [on_device(): pl.pallas_call(prepare_kernel, grid_spec=pltpu.PrefetchScalarGridSpec(num...]
    ppermute x13 -> x15, starting transfers between devices: 15.3 us -> 16.5 us  [seq_swap(): return lax.ppermute(block, 'seq', [(i, i ^ flip) for i in range(count)])]
  transfers between devices with their start and end apart: 19 -> 21, of which waited for: 3 -> 3; matrix products, arithmetic and copies ran while one was open for 4% -> 3% of each run, Pallas kernels for 60% -> 43%
where the time goes in v7:
time: 109 us
  Pallas kernels  63.6 us (58%)
  starting transfers between devices  23.7 us (22%)
  waiting for transfers between devices  16.8 us (15%)
  local copies, waits for them, and re-layouts  3.95 us (4%)
    pallas_call x1, Pallas kernels, on_device(): pl.pallas_call(local_kernel, grid_spec=pltpu.PrefetchScalarGridSpec(num_s...  21.9 us
    ppermute x15, waiting for transfers between devices, seq_swap(): return lax.ppermute(block, 'seq', [(i, i ^ flip) for i in range(count)])  16.8 us
    ppermute x15, starting transfers between devices, seq_swap(): return lax.ppermute(block, 'seq', [(i, i ^ flip) for i in range(count)])  16.5 us
    pallas_call x3, Pallas kernels, attend(): pl.pallas_call(lambda *refs: last_kernel(stage, *refs), in_specs=[scalar]...  14.6 us
    pallas_call x1, Pallas kernels, remote(): pl.pallas_call(lambda *refs: remote_kernel(spans, *refs), grid_spec=pltpu...  11.7 us
    ppermute x4, starting transfers between devices, both_swap(): return lax.ppermute(block, ('grp', 'seq'), route)  5.95 us
    pallas_call x1, Pallas kernels, on_device(): pl.pallas_call(begin_kernel, grid_spec=pltpu.PrefetchScalarGridSpec(num_s...  4.62 us
    pallas_call x1, Pallas kernels, on_device(): pl.pallas_call(prepare_kernel, grid_spec=pltpu.PrefetchScalarGridSpec(num...  3.77 us
  transfers between devices with their start and end apart: 21, of which 3 were waited for; matrix products, arithmetic and copies ran while one was open for 3% of the time, Pallas kernels for 43%

profile of v7, /device:TPU:1, one launch (start us, length us, event | category | flops | bytes accessed | tf_op | source)
XLA Modules:
  0.0 109.2 jit_solution(2226362730093336933)
XLA Ops:
  0.7 3.5 %second.1 = (bf16[3,256,2048]{2,1,0:T(8,128)(2,1)}, bf16[64,2048]{1,0:T(8,128)(2,1)}, bf16[64,2048]{1,0:T(8,128)(2,1)}, bf16[64,1024]{1,0:T(8,128)(2,1)}, bf16[6...) custom-call(s32[1]{0:T(128)} %bitcast.place.me.refs_0_, bf16[2,256,2048]{2,1,0:T(8,128)(2,1)} %q.5, ...), custom_call_target="tpu_custom_call" | custom-call | tf_op jit(solution)/shard_map/second/pallas_call | solution.py:490
  4.2 3.3 %collective-permute-start.2 = (bf16[3,256,2048]{2,1,0:T(8,128)(2,1)}, bf16[3,256,2048]{2,1,0:T(8,128)(2,1)}, u32[]{:S(2)}, u32[]{:S(2)}) collective-permute-start(bf16[3,256,2048]{2,1,0:T(8,128)(2,1)} %get-tuple-element.42), channel_id=1, source_target_pairs={{0,1},{1,0},{2,3},{3,2},{4,5},{5,4},{6,7},{7,6},{8,9},{9,8},{10,11... | collective-permute-start | bytes 9437192 | tf_op jit(solution)/shard_map/ppermute | solution.py:22
  7.5 2.2 %first.1 = (bf16[128,2048]{1,0:T(8,128)(2,1)}, bf16[128,2048]{1,0:T(8,128)(2,1)}) custom-call(s32[1]{0:T(128)} %bitcast.place.me.refs_0_, bf16[2,256,2048]{2,1,0:T(8,128)(2,1)} %q.5), custom_call_target="tpu_custom_call" | custom-call | tf_op jit(solution)/shard_map/first/pallas_call | solution.py:479
  9.8 1.6 %collective-permute-start.1 = (bf16[128,2048]{1,0:T(8,128)(2,1)}, bf16[128,2048]{1,0:T(8,128)(2,1)}, u32[]{:S(2)}, u32[]{:S(2)}) collective-permute-start(bf16[128,2048]{1,0:T(8,128)(2,1)} %get-tuple-element.41), channel_id=1, source_target_pairs={{0,3},{1,2},{2,1},{3,0},{4,7},{5,6},{6,5},{7,4},{8,11},{9,10},{10,... | collective-permute-start | bytes 1572872 | tf_op jit(solution)/shard_map/ppermute | solution.py:22
  11.4 1.7 %collective-permute-done.2.qx.kx.vx.refs_4_ = bf16[3,256,2048]{2,1,0:T(8,128)(2,1)} collective-permute-done((bf16[3,256,2048]{2,1,0:T(8,128)(2,1)}, bf16[3,256,2048]{2,1,0:T(8,128)(2,1)}, u32[]{:S(2)}, u32[]{:S(2)}) %collective-permute-start.2) | collective-permute-done | bytes 3145760 | tf_op jit(solution)/shard_map/ppermute | solution.py:22
  13.1 21.9 %local.1 = (bf16[16,80,512]{2,1,0:T(8,128)(2,1)S(1)}, f32[16,64,256]{2,1,0:T(8,128)S(1)}, bf16[16,64,128]{2,1,0:T(8,128)(2,1)S(1)}, bf16[16,64,128]{2,1,0:T(8,128)(2,1)S(1)}, f32[16,512]{1,0:T(8,128)S(1)}) custom-call(s32[1]{0:T(128)} %bitcast.place.me.refs_0_, s32[1]{0:T(128)} %bitcast.1.grp, s32[4]{0:T(128)S(1)} %copy-done.9, bf16[2,256,2048]{2,1,0:T(8,128)(2,1)} %q.5, ...), custom_call_target="tpu_custom_call" | custom-call | tf_op jit(solution)/shard_map/local/pallas_call | solution.py:556
  35.0 0.7 copy-done.10
  35.7 2.7 %collective-permute-done.3.refs_6_ = f32[16,512]{1,0:T(8,128)S(1)} collective-permute-done((f32[16,512]{1,0:T(8,128)S(1)}, f32[16,512]{1,0:T(8,128)S(1)}, u32[]{:S(2)}, u32[]{:S(2)}) %collective-permute-start.3) | collective-permute-done | bytes 32800 | tf_op jit(solution)/shard_map/ppermute | solution.py:22
  38.5 11.7 %remote.1 = bf16[80,256]{1,0:T(8,128)(2,1)S(1)} custom-call(s32[1]{0:T(128)} %bitcast.place.me.refs_0_, bf16[128,2048]{1,0:T(8,128)(2,1)} %collective-permute-done.refs_1_, bf16[128,2048]{1,0:T(8,128)(2,1)} %collective-permute-done.1.refs_2_, bf16[2,256,2048]{2,1,0:T(8,128)(2,1)S(1)} %copy-done.2, ...), custom_call_target="tpu_custom_call" | custom-call | tf_op jit(solution)/shard_map/remote/pallas_call | solution.py:640
  50.3 1.5 %collective-permute-start.8 = (bf16[64,1024]{1,0:T(8,128)(2,1)}, bf16[64,1024]{1,0:T(8,128)(2,1)}, u32[]{:S(2)}, u32[]{:S(2)}) collective-permute-start(bf16[64,1024]{1,0:T(8,128)(2,1)} %get-tuple-element.56), channel_id=1, source_target_pairs={{0,2},{1,3},{2,0},{3,1},{4,6},{5,7},{6,4},{7,5},{8,10},{9,11},{10,... | collective-permute-start | bytes 393224 | tf_op jit(solution)/shard_map/ppermute | solution.py:22
  51.8 0.2 collective-permute-start.10
  52.0 3.6 %collective-permute-start.11 = (bf16[64,2048]{1,0:T(8,128)(2,1)}, bf16[64,2048]{1,0:T(8,128)(2,1)}, u32[]{:S(2)}, u32[]{:S(2)}) collective-permute-start(bf16[64,2048]{1,0:T(8,128)(2,1)} %get-tuple-element.59), channel_id=1, source_target_pairs={{0,3},{1,2},{2,1},{3,0},{4,7},{5,6},{6,5},{7,4},{8,11},{9,10},{10,... | collective-permute-start | bytes 786440 | tf_op jit(solution)/shard_map/ppermute | solution.py:22
  55.7 0.8 collective-permute-start.5
  56.5 1.9 %gather_fusion = bf16[512,128]{1,0:T(8,128)(2,1)} fusion(bf16[4096,128]{1,0:T(8,128)(2,1)S(1)} %copy-done, s32[1024]{0:T(1024)S(1)} %pad_clamp_fusion), kind=kCustom, calls=%fused_computation | custom fusion | bytes 264192 | tf_op jit(solution)/shard_map/jit(_take)/gather | solution.py:612
  58.4 1.4 %collective-permute-start.12 = (bf16[64,1024]{1,0:T(8,128)(2,1)}, bf16[64,1024]{1,0:T(8,128)(2,1)S(1)}, u32[]{:S(2)}, u32[]{:S(2)}) collective-permute-start(bf16[64,1024]{1,0:T(8,128)(2,1)} %get-tuple-element.60), channel_id=1, source_target_pairs={{0,2},{1,3},{2,0},{3,1},{4,6},{5,7},{6,4},{7,5},{8,10},{9,11},{10,... | collective-permute-start | bytes 393224 | tf_op jit(solution)/shard_map/ppermute | solution.py:22
  59.8 0.6 collective-permute-start.13
  60.4 12.3 %collective-permute-done.9.refs_2_ = bf16[64,1024]{1,0:T(8,128)(2,1)S(1)} collective-permute-done((bf16[64,1024]{1,0:T(8,128)(2,1)}, bf16[64,1024]{1,0:T(8,128)(2,1)S(1)}, u32[]{:S(2)}, u32[]{:S(2)}) %collective-permute-start.9) | collective-permute-done | bytes 131104 | tf_op jit(solution)/shard_map/ppermute | solution.py:22
  72.8 3.5 %collective-permute-start.20 = (bf16[16,64,128]{2,1,0:T(8,128)(2,1)}, bf16[16,64,128]{2,1,0:T(8,128)(2,1)S(1)}, u32[]{:S(2)}, u32[]{:S(2)}) collective-permute-start(bf16[16,64,128]{2,1,0:T(8,128)(2,1)} %copy-done.10), channel_id=1, source_target_pairs={{0,129},{1,128},{2,131},{3,130},{4,133},{5,132},{6,135},{7,134},{8... | collective-permute-start | bytes 786440 | tf_op jit(solution)/shard_map/ppermute | solution.py:34
  76.3 0.8 collective-permute-start.19
  77.1 0.5 collective-permute-start.7
  77.6 0.5 collective-permute-start.6
  78.0 1.3 %slice_bitcast_fusion.refs_4_ = bf16[256,2048]{1,0:T(8,128)(2,1)S(1)} fusion(bf16[3,256,2048]{2,1,0:T(8,128)(2,1)} %collective-permute-done.2.qx.kx.vx.refs_4_), kind=kLoop, calls=%fused_computation.1 | loop fusion | bytes 2097152 | tf_op jit(solution)/shard_map/squeeze | solution.py:610
  79.3 7.1 %last.3.refs_7_ = f32[80,128]{1,0:T(8,128)S(1)} custom-call(s32[1]{0:T(128)} %bitcast.place.me.refs_0_, bf16[64,2048]{1,0:T(8,128)(2,1)} %collective-permute-done.10.refs_1_, bf16[64,2048]{1,0:T(8,128)(2,1)} %collective-permute-done.11.refs_2_, bf16[2,256,2048]{2,1,0:T(8,128)(2,1)S(1)} %copy-done.2, bf16[256,2048]{1,0:T(8,128)(2,1)S(1)} %slice_bitcast_fusion.refs_4_, ...), custom_call_target="tpu_custom_call" | custom-call | tf_op jit(solution)/shard_map/last/pallas_call | solution.py:674
  86.5 3.2 %last.4.refs_8_ = f32[80,128]{1,0:T(8,128)S(1)} custom-call(s32[1]{0:T(128)} %bitcast.place.me.refs_0_, bf16[64,1024]{1,0:T(8,128)(2,1)S(1)} %collective-permute-done.12.refs_1_, bf16[64,1024]{1,0:T(8,128)(2,1)S(1)} %collective-permute-done.13.refs_2_, bf16[2,256,2048]{2,1,0:T(8,128)(2,1)S(1)} %copy-done.2, bf16[256,2048]{1,0:T(8,128)(2,1)S(1)} %slice_bitcast_fusion.refs_4_, ...), custom_call_target="tpu_custom_call" | custom-call | tf_op jit(solution)/shard_map/last/pallas_call | solution.py:674
  89.7 4.3 %last.5 = (bf16[80,128]{1,0:T(8,128)(2,1)S(1)}, bf16[80,128]{1,0:T(8,128)(2,1)S(1)}) custom-call(s32[1]{0:T(128)} %bitcast.place.me.refs_0_, bf16[64,1024]{1,0:T(8,128)(2,1)} %collective-permute-done.8.refs_1_, bf16[64,1024]{1,0:T(8,128)(2,1)S(1)} %collective-permute-done.9.refs_2_, bf16[2,256,2048]{2,1,0:T(8,128)(2,1)S(1)} %copy-done.2, ...), custom_call_target="tpu_custom_call" | custom-call | tf_op jit(solution)/shard_map/last/pallas_call | solution.py:674
  94.0 1.0 collective-permute-start.14
  95.0 1.3 %collective-permute-start.16 = (bf16[80,128]{1,0:T(8,128)(2,1)S(1)}, bf16[80,128]{1,0:T(8,128)(2,1)S(1)}, u32[]{:S(2)}, u32[]{:S(2)}) collective-permute-start(bf16[80,128]{1,0:T(8,128)(2,1)S(1)} %get-tuple-element.62), channel_id=1, source_target_pairs={{0,130},{1,131},{2,128},{3,129},{4,134},{5,135},{6,132},{7,133},{8... | collective-permute-start | bytes 61448 | tf_op jit(solution)/shard_map/ppermute | solution.py:34
  96.3 2.4 %collective-permute-start.15 = (bf16[80,128]{1,0:T(8,128)(2,1)S(1)}, bf16[80,128]{1,0:T(8,128)(2,1)S(1)}, u32[]{:S(2)}, u32[]{:S(2)}) collective-permute-start(bf16[80,128]{1,0:T(8,128)(2,1)S(1)} %get-tuple-element.63), channel_id=1, source_target_pairs={{0,3},{1,2},{2,1},{3,0},{4,7},{5,6},{6,5},{7,4},{8,11},{9,10},{10,... | collective-permute-start | bytes 61448 | tf_op jit(solution)/shard_map/ppermute | solution.py:22
  98.6 0.7 collective-permute-start.17
  99.5 4.6 %begin.1 = (f32[272,384]{1,0:T(8,128)S(1)}, f32[384,384]{1,0:T(8,128)S(1)}, f32[384,128]{1,0:T(8,128)S(1)}, f32[2,64,128]{2,1,0:T(8,128)S(1)}, f32[2,64,128]{2,1,0:T(8,128)S(1)}) custom-call(s32[1]{0:T(128)} %bitcast.place.me.refs_0_, s32[1]{0:T(128)} %bitcast.1.grp, s32[4]{0:T(128)S(1)} %copy-done.9, bf16[4,64,4096]{2,1,0:T(8,128)(2,1)} %w3.3, ...), custom_call_target="tpu_custom_call" | custom-call | tf_op jit(solution)/shard_map/begin/pallas_call | solution.py:536
  104.2 3.8 %prepare.1 = (bf16[768,256]{1,0:T(8,128)(2,1)S(1)}, f32[2,256,256]{2,1,0:T(8,128)S(1)}, f32[2,64,256]{2,1,0:T(8,128)S(1)}, f32[2,8,256]{2,1,0:T(8,128)S(1)}, f32[2,64,128]{2,1,0:T(8,128)S(1)}) custom-call(s32[1]{0:T(128)} %bitcast.place.me.refs_0_, s32[1]{0:T(128)} %bitcast.1.grp, s32[4]{0:T(128)S(1)} %copy-done.9, bf16[4,64,4096]{2,1,0:T(8,128)(2,1)S(1)} %copy-done.1, ...), custom_call_target="tpu_custom_call" | custom-call | tf_op jit(solution)/shard_map/prepare/pallas_call | solution.py:620
  108.0 1.2 %render.1 = (bf16[2,64,256]{2,1,0:T(8,128)(2,1)}, bf16[2,64,256]{2,1,0:T(8,128)(2,1)}) custom-call(s32[1]{0:T(128)} %bitcast.place.me.refs_0_, bf16[64,128]{1,0:T(8,128)(2,1)S(1)} %get-tuple-element.54.refs_0_, bf16[64,128]{1,0:T(8,128)(2,1)S(1)} %collective-permute-done.5.refs_1_, bf16[64,128]{1,0:T(8,128)(2,1)S(1)} %collective-permute-done.6.refs_2_, ...), custom_call_target="tpu_custom_call" | custom-call | tf_op jit(solution)/shard_map/render/pallas_call | solution.py:702
  (54 shorter events, 0.6 us)
Async XLA Ops:
  0.6 55.9 %copy-start = (bf16[4096,128]{1,0:T(8,128)(2,1)S(1)}, bf16[4096,128]{1,0:T(8,128)(2,1)}, u32[]{:S(2)}) copy-start(bf16[4096,128]{1,0:T(8,128)(2,1)} %param.18) | copy-start | bytes 3145732
  4.2 8.9 %copy-start.9 = (s32[4]{0:T(128)S(1)}, s32[4]{0:T(128)}, u32[]{:S(2)}) copy-start(s32[4]{0:T(128)} %kinds.5) | copy-start | bytes 52
  4.2 8.9 %collective-permute-start.2 = (bf16[3,256,2048]{2,1,0:T(8,128)(2,1)}, bf16[3,256,2048]{2,1,0:T(8,128)(2,1)}, u32[]{:S(2)}, u32[]{:S(2)}) collective-permute-start(bf16[3,256,2048]{2,1,0:T(8,128)(2,1)} %get-tuple-element.42), channel_id=1, source_target_pairs={{0,1},{1,0},{2,3},{3,2},{4,5},{5,4},{6,7},{7,6},{8,9},{9,8},{10,11... | collective-permute-start | bytes 9437192 | tf_op jit(solution)/shard_map/ppermute | solution.py:22
  9.7 26.1 %collective-permute-start = (bf16[128,2048]{1,0:T(8,128)(2,1)}, bf16[128,2048]{1,0:T(8,128)(2,1)}, u32[]{:S(2)}, u32[]{:S(2)}) collective-permute-start(bf16[128,2048]{1,0:T(8,128)(2,1)} %get-tuple-element.40), channel_id=1, source_target_pairs={{0,2},{1,3},{2,0},{3,1},{4,6},{5,7},{6,4},{7,5},{8,10},{9,11},{10,... | collective-permute-start | bytes 1572872 | tf_op jit(solution)/shard_map/ppermute | solution.py:22
  9.8 26.0 %collective-permute-start.1 = (bf16[128,2048]{1,0:T(8,128)(2,1)}, bf16[128,2048]{1,0:T(8,128)(2,1)}, u32[]{:S(2)}, u32[]{:S(2)}) collective-permute-start(bf16[128,2048]{1,0:T(8,128)(2,1)} %get-tuple-element.41), channel_id=1, source_target_pairs={{0,3},{1,2},{2,1},{3,0},{4,7},{5,6},{6,5},{7,4},{8,11},{9,10},{10,... | collective-permute-start | bytes 1572872 | tf_op jit(solution)/shard_map/ppermute | solution.py:22
  13.1 25.4 %copy-start.2 = (bf16[2,256,2048]{2,1,0:T(8,128)(2,1)S(1)}, bf16[2,256,2048]{2,1,0:T(8,128)(2,1)}, u32[]{:S(2)}) copy-start(bf16[2,256,2048]{2,1,0:T(8,128)(2,1)} %refs_3_.7) | copy-start | bytes 6291460
  35.7 14.5 %copy-start.3 = (bf16[16,80,512]{2,1,0:T(8,128)(2,1)}, bf16[16,80,512]{2,1,0:T(8,128)(2,1)S(1)}, u32[]{:S(2)}) copy-start(bf16[16,80,512]{2,1,0:T(8,128)(2,1)S(1)} %get-tuple-element.43.refs_5_) | copy-start | bytes 3932164
  35.7 2.8 %collective-permute-start.3 = (f32[16,512]{1,0:T(8,128)S(1)}, f32[16,512]{1,0:T(8,128)S(1)}, u32[]{:S(2)}, u32[]{:S(2)}) collective-permute-start(f32[16,512]{1,0:T(8,128)S(1)} %get-tuple-element.47), channel_id=1, source_target_pairs={{0,2},{1,3},{2,0},{3,1},{4,6},{5,7},{6,4},{7,5},{8,10},{9,11},{10,... | collective-permute-start | bytes 98312 | tf_op jit(solution)/shard_map/ppermute | solution.py:22
  38.5 13.3 %copy-start.12 = (s32[2,256]{1,0:T(2,128)S(1)}, s32[2,256]{1,0:T(2,128)}, u32[]{:S(2)}) copy-start(s32[2,256]{1,0:T(2,128)} %param.17) | copy-start | bytes 6148
  50.2 5.4 %collective-permute-start.4 = (bf16[80,256]{1,0:T(8,128)(2,1)S(1)}, bf16[80,256]{1,0:T(8,128)(2,1)S(1)}, u32[]{:S(2)}, u32[]{:S(2)}) collective-permute-start(bf16[80,256]{1,0:T(8,128)(2,1)S(1)} %remote.1), channel_id=1, source_target_pairs={{0,2},{1,3},{2,0},{3,1},{4,6},{5,7},{6,4},{7,5},{8,10},{9,11},{10,... | collective-permute-start | bytes 122888 | tf_op jit(solution)/shard_map/ppermute | solution.py:22
  50.3 9.4 %collective-permute-start.8 = (bf16[64,1024]{1,0:T(8,128)(2,1)}, bf16[64,1024]{1,0:T(8,128)(2,1)}, u32[]{:S(2)}, u32[]{:S(2)}) collective-permute-start(bf16[64,1024]{1,0:T(8,128)(2,1)} %get-tuple-element.56), channel_id=1, source_target_pairs={{0,2},{1,3},{2,0},{3,1},{4,6},{5,7},{6,4},{7,5},{8,10},{9,11},{10,... | collective-permute-start | bytes 393224 | tf_op jit(solution)/shard_map/ppermute | solution.py:22
  51.8 25.3 %collective-permute-start.10 = (bf16[64,2048]{1,0:T(8,128)(2,1)}, bf16[64,2048]{1,0:T(8,128)(2,1)}, u32[]{:S(2)}, u32[]{:S(2)}) collective-permute-start(bf16[64,2048]{1,0:T(8,128)(2,1)} %get-tuple-element.58), channel_id=1, source_target_pairs={{0,2},{1,3},{2,0},{3,1},{4,6},{5,7},{6,4},{7,5},{8,10},{9,11},{10,... | collective-permute-start | bytes 786440 | tf_op jit(solution)/shard_map/ppermute | solution.py:22
  52.0 25.6 %collective-permute-start.11 = (bf16[64,2048]{1,0:T(8,128)(2,1)}, bf16[64,2048]{1,0:T(8,128)(2,1)}, u32[]{:S(2)}, u32[]{:S(2)}) collective-permute-start(bf16[64,2048]{1,0:T(8,128)(2,1)} %get-tuple-element.59), channel_id=1, source_target_pairs={{0,3},{1,2},{2,1},{3,0},{4,7},{5,6},{6,5},{7,4},{8,11},{9,10},{10,... | collective-permute-start | bytes 786440 | tf_op jit(solution)/shard_map/ppermute | solution.py:22
  55.7 2.7 %collective-permute-start.5 = (bf16[64,128]{1,0:T(8,128)(2,1)S(1)}, bf16[64,128]{1,0:T(8,128)(2,1)S(1)}, u32[]{:S(2)}, u32[]{:S(2)}) collective-permute-start(bf16[64,128]{1,0:T(8,128)(2,1)S(1)} %get-tuple-element.55), channel_id=1, source_target_pairs={{0,1},{1,0},{2,3},{3,2},{4,5},{5,4},{6,7},{7,6},{8,9},{9,8},{10,11... | collective-permute-start | bytes 49160 | tf_op jit(solution)/shard_map/ppermute | solution.py:22
  58.4 20.9 %copy-start.4 = (bf16[16,80,512]{2,1,0:T(8,128)(2,1)S(1)}, bf16[16,80,512]{2,1,0:T(8,128)(2,1)}, u32[]{:S(2)}) copy-start(bf16[16,80,512]{2,1,0:T(8,128)(2,1)} %copy-done.3) | copy-start | bytes 3932164
  58.4 14.4 %collective-permute-start.9 = (bf16[64,1024]{1,0:T(8,128)(2,1)}, bf16[64,1024]{1,0:T(8,128)(2,1)S(1)}, u32[]{:S(2)}, u32[]{:S(2)}) collective-permute-start(bf16[64,1024]{1,0:T(8,128)(2,1)} %get-tuple-element.57), channel_id=1, source_target_pairs={{0,3},{1,2},{2,1},{3,0},{4,7},{5,6},{6,5},{7,4},{8,11},{9,10},{10,... | collective-permute-start | bytes 393224 | tf_op jit(solution)/shard_map/ppermute | solution.py:22
  58.4 14.4 %collective-permute-start.12 = (bf16[64,1024]{1,0:T(8,128)(2,1)}, bf16[64,1024]{1,0:T(8,128)(2,1)S(1)}, u32[]{:S(2)}, u32[]{:S(2)}) collective-permute-start(bf16[64,1024]{1,0:T(8,128)(2,1)} %get-tuple-element.60), channel_id=1, source_target_pairs={{0,2},{1,3},{2,0},{3,1},{4,6},{5,7},{6,4},{7,5},{8,10},{9,11},{10,... | collective-permute-start | bytes 393224 | tf_op jit(solution)/shard_map/ppermute | solution.py:22
  59.8 16.5 %collective-permute-start.13 = (bf16[64,1024]{1,0:T(8,128)(2,1)}, bf16[64,1024]{1,0:T(8,128)(2,1)S(1)}, u32[]{:S(2)}, u32[]{:S(2)}) collective-permute-start(bf16[64,1024]{1,0:T(8,128)(2,1)} %get-tuple-element.61), channel_id=1, source_target_pairs={{0,3},{1,2},{2,1},{3,0},{4,7},{5,6},{6,5},{7,4},{8,11},{9,10},{10,... | collective-permute-start | bytes 393224 | tf_op jit(solution)/shard_map/ppermute | solution.py:22
  72.7 23.5 %collective-permute-start.18 = (bf16[16,64,128]{2,1,0:T(8,128)(2,1)}, bf16[16,64,128]{2,1,0:T(8,128)(2,1)S(1)}, u32[]{:S(2)}, u32[]{:S(2)}) collective-permute-start(bf16[16,64,128]{2,1,0:T(8,128)(2,1)} %copy-done.10), channel_id=1, source_target_pairs={{0,1},{1,0},{2,3},{3,2},{4,5},{5,4},{6,7},{7,6},{8,9},{9,8},{10,11... | collective-permute-start | bytes 786440 | tf_op jit(solution)/shard_map/ppermute | solution.py:22
  72.8 35.2 %collective-permute-start.20 = (bf16[16,64,128]{2,1,0:T(8,128)(2,1)}, bf16[16,64,128]{2,1,0:T(8,128)(2,1)S(1)}, u32[]{:S(2)}, u32[]{:S(2)}) collective-permute-start(bf16[16,64,128]{2,1,0:T(8,128)(2,1)} %copy-done.10), channel_id=1, source_target_pairs={{0,129},{1,128},{2,131},{3,130},{4,133},{5,132},{6,135},{7,134},{8... | collective-permute-start | bytes 786440 | tf_op jit(solution)/shard_map/ppermute | solution.py:34
  76.3 22.4 %collective-permute-start.19 = (bf16[16,64,128]{2,1,0:T(8,128)(2,1)S(1)}, bf16[16,64,128]{2,1,0:T(8,128)(2,1)S(1)}, u32[]{:S(2)}, u32[]{:S(2)}) collective-permute-start(bf16[16,64,128]{2,1,0:T(8,128)(2,1)S(1)} %get-tuple-element.64.refs_8_), channel_id=1, source_target_pairs={{0,128},{128,0},{1,129},{129,1},{2,130},{130,2},{3,131},{131,3},{4... | collective-permute-start | bytes 786440 | tf_op jit(solution)/shard_map/ppermute | solution.py:26
  77.1 17.9 %collective-permute-start.7 = (bf16[64,128]{1,0:T(8,128)(2,1)S(1)}, bf16[64,128]{1,0:T(8,128)(2,1)S(1)}, u32[]{:S(2)}, u32[]{:S(2)}) collective-permute-start(bf16[64,128]{1,0:T(8,128)(2,1)S(1)} %get-tuple-element.55), channel_id=1, source_target_pairs={{0,129},{1,128},{2,131},{3,130},{4,133},{5,132},{6,135},{7,134},{8... | collective-permute-start | bytes 49160 | tf_op jit(solution)/shard_map/ppermute | solution.py:34
  77.6 16.4 %collective-permute-start.6 = (bf16[64,128]{1,0:T(8,128)(2,1)S(1)}, bf16[64,128]{1,0:T(8,128)(2,1)S(1)}, u32[]{:S(2)}, u32[]{:S(2)}) collective-permute-start(bf16[64,128]{1,0:T(8,128)(2,1)S(1)} %get-tuple-element.54.refs_0_), channel_id=1, source_target_pairs={{0,128},{128,0},{1,129},{129,1},{2,130},{130,2},{3,131},{131,3},{4... | collective-permute-start | bytes 49160 | tf_op jit(solution)/shard_map/ppermute | solution.py:26
  89.7 9.6 %copy-start.11 = (bf16[512,128]{1,0:T(8,128)(2,1)S(1)}, bf16[512,128]{1,0:T(8,128)(2,1)}, u32[]{:S(2)}) copy-start(bf16[512,128]{1,0:T(8,128)(2,1)} %gather_fusion) | copy-start | bytes 393220
  94.0 14.0 %collective-permute-start.14 = (bf16[80,128]{1,0:T(8,128)(2,1)S(1)}, bf16[80,128]{1,0:T(8,128)(2,1)S(1)}, u32[]{:S(2)}, u32[]{:S(2)}) collective-permute-start(bf16[80,128]{1,0:T(8,128)(2,1)S(1)} %get-tuple-element.62), channel_id=1, source_target_pairs={{0,2},{1,3},{2,0},{3,1},{4,6},{5,7},{6,4},{7,5},{8,10},{9,11},{10,... | collective-permute-start | bytes 61448 | tf_op jit(solution)/shard_map/ppermute | solution.py:22
  95.0 13.0 %collective-permute-start.16 = (bf16[80,128]{1,0:T(8,128)(2,1)S(1)}, bf16[80,128]{1,0:T(8,128)(2,1)S(1)}, u32[]{:S(2)}, u32[]{:S(2)}) collective-permute-start(bf16[80,128]{1,0:T(8,128)(2,1)S(1)} %get-tuple-element.62), channel_id=1, source_target_pairs={{0,130},{1,131},{2,128},{3,129},{4,134},{5,135},{6,132},{7,133},{8... | collective-permute-start | bytes 61448 | tf_op jit(solution)/shard_map/ppermute | solution.py:34
  96.3 11.7 %collective-permute-start.15 = (bf16[80,128]{1,0:T(8,128)(2,1)S(1)}, bf16[80,128]{1,0:T(8,128)(2,1)S(1)}, u32[]{:S(2)}, u32[]{:S(2)}) collective-permute-start(bf16[80,128]{1,0:T(8,128)(2,1)S(1)} %get-tuple-element.63), channel_id=1, source_target_pairs={{0,3},{1,2},{2,1},{3,0},{4,7},{5,6},{6,5},{7,4},{8,11},{9,10},{10,... | collective-permute-start | bytes 61448 | tf_op jit(solution)/shard_map/ppermute | solution.py:22
  98.6 9.4 %collective-permute-start.17 = (bf16[80,128]{1,0:T(8,128)(2,1)S(1)}, bf16[80,128]{1,0:T(8,128)(2,1)S(1)}, u32[]{:S(2)}, u32[]{:S(2)}) collective-permute-start(bf16[80,128]{1,0:T(8,128)(2,1)S(1)} %get-tuple-element.63), channel_id=1, source_target_pairs={{0,131},{1,130},{2,129},{3,128},{4,135},{5,134},{6,133},{7,132},{8... | collective-permute-start | bytes 61448 | tf_op jit(solution)/shard_map/ppermute | solution.py:34
  99.5 4.7 %copy-start.1 = (bf16[4,64,4096]{2,1,0:T(8,128)(2,1)S(1)}, bf16[4,64,4096]{2,1,0:T(8,128)(2,1)}, u32[]{:S(2)}) copy-start(bf16[4,64,4096]{2,1,0:T(8,128)(2,1)} %w3.3) | copy-start | bytes 6291460
  99.5 4.7 %copy-start.5 = (bf16[128,4096]{1,0:T(8,128)(2,1)S(1)}, bf16[128,4096]{1,0:T(8,128)(2,1)}, u32[]{:S(2)}) copy-start(bf16[128,4096]{1,0:T(8,128)(2,1)} %w_env.3) | copy-start | bytes 3145732
  99.5 4.7 %copy-start.6 = (bf16[4096,64]{0,1:T(8,128)(2,1)S(1)}, bf16[4096,64]{0,1:T(8,128)(2,1)}, u32[]{:S(2)}) copy-start(bf16[4096,64]{0,1:T(8,128)(2,1)} %param.23) | copy-start | bytes 1572868
  99.5 4.7 %copy-start.7 = (bf16[2,4096]{1,0:T(2,128)(2,1)S(1)}, bf16[2,4096]{1,0:T(2,128)(2,1)}, u32[]{:S(2)}) copy-start(bf16[2,4096]{1,0:T(2,128)(2,1)} %scale.3) | copy-start | bytes 49156
  (2 other events, 5.4 us)

commit v8 on v7

--- a/solution.py
+++ b/solution.py
@@ -107,13 +107,13 @@
         copy.wait()
 
 
-def first_kernel(place, q, same, cross, arrive):
-    me = place[0]
-    rows = pl.ds(0, same.shape[0])
-    copies = [
-        pltpu.make_async_copy(q.at[me, rows], same, arrive.at[0]),
-        pltpu.make_async_copy(q.at[1 - me, rows], cross, arrive.at[1]),
-    ]
+def first_kernel(other, place, q, out, arrive):
+    group = 1 - place[0] if other else place[0]
+    half = out.shape[0] // 2
+    copies = []
+    for n in range(2):
+        rows = pl.ds(n * half, half)
+        copies.append(pltpu.make_async_copy(q.at[group, rows], out.at[rows], arrive.at[n]))
     for copy in copies:
         copy.start()
     for copy in copies:
@@ -124,7 +124,8 @@
     me = place[0]
     count, width = sb.shape
     start = q.shape[1] - 2 * count
-    left, right = pl.ds(0, width // 2), pl.ds(width // 2, width // 2)
+    ahead = s1.shape[1]
+    left, right = pl.ds(0, ahead), pl.ds(ahead, width - ahead)
     pieces = [(a.at[1 - me], held.at[n], bundle.at[n]) for n, a in enumerate((q, k, v))]
     for n, group, same, first, later in ((0, me, sb, s1, s2), (1, 1 - me, cb, c1, c2)):
         span = pl.ds(start, count)
@@ -239,7 +240,7 @@
 def last_kernel(stage, place, qs, qd, k, kx, vw, home, *refs):
     prior, outs, (acc, share, near) = refs[:stage], refs[stage:-3], refs[-3:]
     me = place[0]
-    base = vw.shape[0] // 2 if stage == 2 else 0
+    base = vw.shape[0] - qs.shape[1] // HD if stage == 2 else 0
     heads = base + qs.shape[1] // HD
     near[...] = halves(home[:, 256:384], home[:, 384:512])[1 if stage else 0]
     zero = jnp.zeros((2 * qs.shape[0], HD), jnp.bfloat16)
@@ -466,6 +467,7 @@
     heads = width // HD
     first = rows // 2
     piece = rows // 4
+    soon = 3 * heads // 4
     patch = w_attr.shape[2]
     lights, model = mod_scale.shape
     channels = w_embed_env.shape[0]
@@ -476,16 +478,21 @@
     side = grp.reshape(1).astype(jnp.int32)
     scalar = pl.BlockSpec(memory_space=pltpu.SMEM)
     remain = pl.BlockSpec(memory_space=pltpu.HBM)
-    ahead, behind = pl.pallas_call(
-        first_kernel,
-        in_specs=[scalar, remain],
-        out_specs=[RESIDENT] * 2,
-        out_shape=[pltpu.VMEM((first, width), jnp.bfloat16)] * 2,
-        scratch_shapes=[pltpu.SemaphoreType.DMA((2,))],
-        compiler_params=LIMIT,
-        name="first",
-    )(place, stay(q_inv))
+
+    def cut(other):
+        return pl.pallas_call(
+            lambda *refs: first_kernel(other, *refs),
+            in_specs=[scalar, remain],
+            out_specs=RESIDENT,
+            out_shape=pltpu.VMEM((first, width), jnp.bfloat16),
+            scratch_shapes=[pltpu.SemaphoreType.DMA((2,))],
+            compiler_params=LIMIT,
+            name="first",
+        )(place, stay(q_inv))
+
+    ahead = cut(False)
     same0 = seq_swap(ahead, 2)
+    behind = cut(True)
     cross0 = seq_swap(behind, 3)
     bundle, same1, cross1, *late = pl.pallas_call(
         second_kernel,
@@ -493,7 +500,7 @@
         out_specs=[remain] * 7,
         out_shape=[pltpu.HBM((3, rows, width), jnp.bfloat16)]
         + [pltpu.HBM((piece, width), jnp.bfloat16)] * 2
-        + [pltpu.HBM((piece, width // 2), jnp.bfloat16)] * 4,
+        + [pltpu.HBM((piece, n * HD), jnp.bfloat16) for n in (soon, heads - soon) for _ in range(2)],
         scratch_shapes=[
             pltpu.VMEM((3, rows, width), jnp.bfloat16),
             pltpu.VMEM((4, piece, width), jnp.bfloat16),

time: 109 us -> 116 us (1.064)
  waiting for transfers between devices: 16.8 us -> 23.7 us
  starting transfers between devices: 23.7 us -> 21 us
  Pallas kernels: 63.6 us -> 66.1 us
    ppermute x15, waiting for transfers between devices: 16.8 us -> 23.7 us  [seq_swap(): return lax.ppermute(block, 'seq', [(i, i ^ flip) for i in range(count)])]
    ppermute x4, starting transfers between devices: 5.95 us -> 2.48 us  [both_swap(): return lax.ppermute(block, ('grp', 'seq'), route)]
    ppermute x2, starting transfers between devices: 1.29 us -> 3.08 us  [grp_swap(): return lax.ppermute(block, 'grp', [(0, 1), (1, 0)])]
    pallas_call x1 -> x2, Pallas kernels: 2.18 us -> 3.73 us  [cut(): pl.pallas_call(lambda *refs: first_kernel(other, *refs), in_specs=[scalar...]
  transfers between devices with their start and end apart: 21 -> 21, of which waited for: 3 -> 5; matrix products, arithmetic and copies ran while one was open for 3% -> 3% of each run, Pallas kernels for 43% -> 43%
where the time goes in v8:
time: 116 us
  Pallas kernels  66.1 us (57%)
  waiting for transfers between devices  23.7 us (20%)
  starting transfers between devices  21 us (18%)
  local copies, waits for them, and re-layouts  3.98 us (3%)
    ppermute x15, waiting for transfers between devices, seq_swap(): return lax.ppermute(block, 'seq', [(i, i ^ flip) for i in range(count)])  23.7 us
    pallas_call x1, Pallas kernels, on_device(): pl.pallas_call(local_kernel, grid_spec=pltpu.PrefetchScalarGridSpec(num_s...  21.9 us
    pallas_call x3, Pallas kernels, attend(): pl.pallas_call(lambda *refs: last_kernel(stage, *refs), in_specs=[scalar]...  15.6 us
    ppermute x15, starting transfers between devices, seq_swap(): return lax.ppermute(block, 'seq', [(i, i ^ flip) for i in range(count)])  15.4 us
    pallas_call x1, Pallas kernels, remote(): pl.pallas_call(lambda *refs: remote_kernel(spans, *refs), grid_spec=pltpu...  11.8 us
    pallas_call x1, Pallas kernels, on_device(): pl.pallas_call(begin_kernel, grid_spec=pltpu.PrefetchScalarGridSpec(num_s...  4.62 us
    pallas_call x1, Pallas kernels, on_device(): pl.pallas_call(prepare_kernel, grid_spec=pltpu.PrefetchScalarGridSpec(num...  3.77 us
    pallas_call x2, Pallas kernels, cut(): pl.pallas_call(lambda *refs: first_kernel(other, *refs), in_specs=[scalar...  3.73 us
  transfers between devices with their start and end apart: 21, of which 5 were waited for; matrix products, arithmetic and copies ran while one was open for 3% of the time, Pallas kernels for 43%

profile of v8, /device:TPU:1, one launch (start us, length us, event | category | flops | bytes accessed | tf_op | source)
XLA Modules:
  0.0 115.9 jit_solution(13630876056896049473)
XLA Ops:
  0.7 3.5 %second.1 = (bf16[3,256,2048]{2,1,0:T(8,128)(2,1)}, bf16[64,2048]{1,0:T(8,128)(2,1)}, bf16[64,2048]{1,0:T(8,128)(2,1)}, bf16[64,1536]{1,0:T(8,128)(2,1)}, bf16[6...) custom-call(s32[1]{0:T(128)} %bitcast.refs_0_.place.me, bf16[2,256,2048]{2,1,0:T(8,128)(2,1)} %q.3, ...), custom_call_target="tpu_custom_call" | custom-call | tf_op jit(solution)/shard_map/second/pallas_call | solution.py:497
  4.1 3.3 %collective-permute-start.2 = (bf16[3,256,2048]{2,1,0:T(8,128)(2,1)}, bf16[3,256,2048]{2,1,0:T(8,128)(2,1)}, u32[]{:S(2)}, u32[]{:S(2)}) collective-permute-start(bf16[3,256,2048]{2,1,0:T(8,128)(2,1)} %get-tuple-element.38), channel_id=1, source_target_pairs={{0,1},{1,0},{2,3},{3,2},{4,5},{5,4},{6,7},{7,6},{8,9},{9,8},{10,11... | collective-permute-start | bytes 9437192 | tf_op jit(solution)/shard_map/ppermute | solution.py:22
  7.4 1.8 %first.2 = bf16[128,2048]{1,0:T(8,128)(2,1)} custom-call(s32[1]{0:T(128)} %bitcast.refs_0_.place.me, bf16[2,256,2048]{2,1,0:T(8,128)(2,1)} %q.3), custom_call_target="tpu_custom_call" | custom-call | tf_op jit(solution)/shard_map/first/pallas_call | solution.py:483
  9.4 1.9 %first.3 = bf16[128,2048]{1,0:T(8,128)(2,1)} custom-call(s32[1]{0:T(128)} %bitcast.refs_0_.place.me, bf16[2,256,2048]{2,1,0:T(8,128)(2,1)} %q.3), custom_call_target="tpu_custom_call" | custom-call | tf_op jit(solution)/shard_map/first/pallas_call | solution.py:483
  11.3 1.7 %collective-permute-start.1 = (bf16[128,2048]{1,0:T(8,128)(2,1)}, bf16[128,2048]{1,0:T(8,128)(2,1)}, u32[]{:S(2)}, u32[]{:S(2)}) collective-permute-start(bf16[128,2048]{1,0:T(8,128)(2,1)} %first.3), channel_id=1, source_target_pairs={{0,3},{1,2},{2,1},{3,0},{4,7},{5,6},{6,5},{7,4},{8,11},{9,10},{10,... | collective-permute-start | bytes 1572872 | tf_op jit(solution)/shard_map/ppermute | solution.py:22
  13.1 21.9 %local.1 = (bf16[16,80,512]{2,1,0:T(8,128)(2,1)S(1)}, f32[16,64,256]{2,1,0:T(8,128)S(1)}, bf16[16,64,128]{2,1,0:T(8,128)(2,1)S(1)}, bf16[16,64,128]{2,1,0:T(8,128)(2,1)S(1)}, f32[16,512]{1,0:T(8,128)S(1)}) custom-call(s32[1]{0:T(128)} %bitcast.refs_0_.place.me, s32[1]{0:T(128)} %bitcast.1.grp, s32[4]{0:T(128)S(1)} %copy-done.9, bf16[2,256,2048]{2,1,0:T(8,128)(2,1)} %q.3, ...), custom_call_target="tpu_custom_call" | custom-call | tf_op jit(solution)/shard_map/local/pallas_call | solution.py:563
  35.0 0.7 copy-done.10
  35.7 2.7 %collective-permute-done.3.refs_6_ = f32[16,512]{1,0:T(8,128)S(1)} collective-permute-done((f32[16,512]{1,0:T(8,128)S(1)}, f32[16,512]{1,0:T(8,128)S(1)}, u32[]{:S(2)}, u32[]{:S(2)}) %collective-permute-start.3) | collective-permute-done | bytes 32800 | tf_op jit(solution)/shard_map/ppermute | solution.py:22
  38.4 11.8 %remote.1 = bf16[80,256]{1,0:T(8,128)(2,1)S(1)} custom-call(s32[1]{0:T(128)} %bitcast.refs_0_.place.me, bf16[128,2048]{1,0:T(8,128)(2,1)} %collective-permute-done.refs_1_, bf16[128,2048]{1,0:T(8,128)(2,1)} %collective-permute-done.1.refs_2_, bf16[2,256,2048]{2,1,0:T(8,128)(2,1)S(1)} %copy-done.2, ...), custom_call_target="tpu_custom_call" | custom-call | tf_op jit(solution)/shard_map/remote/pallas_call | solution.py:647
  50.3 2.8 %collective-permute-done.4.remote = bf16[80,256]{1,0:T(8,128)(2,1)S(1)} collective-permute-done((bf16[80,256]{1,0:T(8,128)(2,1)S(1)}, bf16[80,256]{1,0:T(8,128)(2,1)S(1)}, u32[]{:S(2)}, u32[]{:S(2)}) %collective-permute-start.4) | collective-permute-done | bytes 40992 | tf_op jit(solution)/shard_map/ppermute | solution.py:22
  53.3 2.8 %collective-permute-start.5 = (bf16[64,128]{1,0:T(8,128)(2,1)S(1)}, bf16[64,128]{1,0:T(8,128)(2,1)S(1)}, u32[]{:S(2)}, u32[]{:S(2)}) collective-permute-start(bf16[64,128]{1,0:T(8,128)(2,1)S(1)} %get-tuple-element.51), channel_id=1, source_target_pairs={{0,1},{1,0},{2,3},{3,2},{4,5},{5,4},{6,7},{7,6},{8,9},{9,8},{10,11... | collective-permute-start | bytes 49160 | tf_op jit(solution)/shard_map/ppermute | solution.py:22
  56.0 1.7 %collective-permute-start.11 = (bf16[64,2048]{1,0:T(8,128)(2,1)}, bf16[64,2048]{1,0:T(8,128)(2,1)}, u32[]{:S(2)}, u32[]{:S(2)}) collective-permute-start(bf16[64,2048]{1,0:T(8,128)(2,1)} %get-tuple-element.55), channel_id=1, source_target_pairs={{0,3},{1,2},{2,1},{3,0},{4,7},{5,6},{6,5},{7,4},{8,11},{9,10},{10,... | collective-permute-start | bytes 786440 | tf_op jit(solution)/shard_map/ppermute | solution.py:22
  57.8 1.5 %collective-permute-start.12 = (bf16[64,1536]{1,0:T(8,128)(2,1)}, bf16[64,1536]{1,0:T(8,128)(2,1)}, u32[]{:S(2)}, u32[]{:S(2)}) collective-permute-start(bf16[64,1536]{1,0:T(8,128)(2,1)} %get-tuple-element.56), channel_id=1, source_target_pairs={{0,2},{1,3},{2,0},{3,1},{4,6},{5,7},{6,4},{7,5},{8,10},{9,11},{10,... | collective-permute-start | bytes 589832 | tf_op jit(solution)/shard_map/ppermute | solution.py:22
  59.3 0.7 collective-permute-start.13
  59.9 11.1 %collective-permute-done.8.refs_1_ = bf16[64,512]{1,0:T(8,128)(2,1)S(1)} collective-permute-done((bf16[64,512]{1,0:T(8,128)(2,1)S(1)}, bf16[64,512]{1,0:T(8,128)(2,1)S(1)}, u32[]{:S(2)}, u32[]{:S(2)}) %collective-permute-start.8) | collective-permute-done | bytes 65568 | tf_op jit(solution)/shard_map/ppermute | solution.py:22
  71.0 1.4 %collective-permute-start.9 = (bf16[64,512]{1,0:T(8,128)(2,1)}, bf16[64,512]{1,0:T(8,128)(2,1)}, u32[]{:S(2)}, u32[]{:S(2)}) collective-permute-start(bf16[64,512]{1,0:T(8,128)(2,1)} %get-tuple-element.53), channel_id=1, source_target_pairs={{0,3},{1,2},{2,1},{3,0},{4,7},{5,6},{6,5},{7,4},{8,11},{9,10},{10,... | collective-permute-start | bytes 196616 | tf_op jit(solution)/shard_map/ppermute | solution.py:22
  72.4 1.9 %gather_fusion = bf16[512,128]{1,0:T(8,128)(2,1)} fusion(bf16[4096,128]{1,0:T(8,128)(2,1)S(1)} %copy-done, s32[1024]{0:T(1024)S(1)} %pad_clamp_fusion), kind=kCustom, calls=%fused_computation | custom fusion | bytes 264192 | tf_op jit(solution)/shard_map/jit(_take)/gather | solution.py:619
  74.3 6.9 %collective-permute-done.9.refs_2_ = bf16[64,512]{1,0:T(8,128)(2,1)} collective-permute-done((bf16[64,512]{1,0:T(8,128)(2,1)}, bf16[64,512]{1,0:T(8,128)(2,1)}, u32[]{:S(2)}, u32[]{:S(2)}) %collective-permute-start.9) | collective-permute-done | bytes 65568 | tf_op jit(solution)/shard_map/ppermute | solution.py:22
  81.4 1.7 %collective-permute-start.19 = (bf16[16,64,128]{2,1,0:T(8,128)(2,1)S(1)}, bf16[16,64,128]{2,1,0:T(8,128)(2,1)S(1)}, u32[]{:S(2)}, u32[]{:S(2)}) collective-permute-start(bf16[16,64,128]{2,1,0:T(8,128)(2,1)S(1)} %get-tuple-element.60.refs_8_), channel_id=1, source_target_pairs={{0,128},{128,0},{1,129},{129,1},{2,130},{130,2},{3,131},{131,3},{4... | collective-permute-start | bytes 786440 | tf_op jit(solution)/shard_map/ppermute | solution.py:26
  83.1 0.4 collective-permute-start.7
  83.5 1.4 %collective-permute-start.6 = (bf16[64,128]{1,0:T(8,128)(2,1)S(1)}, bf16[64,128]{1,0:T(8,128)(2,1)S(1)}, u32[]{:S(2)}, u32[]{:S(2)}) collective-permute-start(bf16[64,128]{1,0:T(8,128)(2,1)S(1)} %get-tuple-element.50.refs_0_), channel_id=1, source_target_pairs={{0,128},{128,0},{1,129},{129,1},{2,130},{130,2},{3,131},{131,3},{4... | collective-permute-start | bytes 49160 | tf_op jit(solution)/shard_map/ppermute | solution.py:26
  84.9 1.3 %slice_bitcast_fusion.refs_4_ = bf16[256,2048]{1,0:T(8,128)(2,1)S(1)} fusion(bf16[3,256,2048]{2,1,0:T(8,128)(2,1)} %collective-permute-done.2.qx.kx.vx.refs_4_), kind=kLoop, calls=%fused_computation.1 | loop fusion | bytes 2097152 | tf_op jit(solution)/shard_map/squeeze | solution.py:617
  86.2 7.2 %last.3.refs_7_ = f32[80,128]{1,0:T(8,128)S(1)} custom-call(s32[1]{0:T(128)} %bitcast.refs_0_.place.me, bf16[64,2048]{1,0:T(8,128)(2,1)} %collective-permute-done.10.refs_1_, bf16[64,2048]{1,0:T(8,128)(2,1)} %collective-permute-done.11.refs_2_, bf16[2,256,2048]{2,1,0:T(8,128)(2,1)S(1)} %copy-done.2, bf16[256,2048]{1,0:T(8,128)(2,1)S(1)} %slice_bitcast_fusion.refs_4_, ...), custom_call_target="tpu_custom_call" | custom-call | tf_op jit(solution)/shard_map/last/pallas_call | solution.py:681
  93.3 5.7 %last.4.refs_8_ = f32[80,128]{1,0:T(8,128)S(1)} custom-call(s32[1]{0:T(128)} %bitcast.refs_0_.place.me, bf16[64,1536]{1,0:T(8,128)(2,1)} %collective-permute-done.12.refs_1_, bf16[64,1536]{1,0:T(8,128)(2,1)} %collective-permute-done.13.refs_2_, bf16[2,256,2048]{2,1,0:T(8,128)(2,1)S(1)} %copy-done.2, bf16[256,2048]{1,0:T(8,128)(2,1)S(1)} %slice_bitcast_fusion.refs_4_, ...), custom_call_target="tpu_custom_call" | custom-call | tf_op jit(solution)/shard_map/last/pallas_call | solution.py:681
  99.1 2.7 %last.5 = (bf16[80,128]{1,0:T(8,128)(2,1)S(1)}, bf16[80,128]{1,0:T(8,128)(2,1)S(1)}) custom-call(s32[1]{0:T(128)} %bitcast.refs_0_.place.me, bf16[64,512]{1,0:T(8,128)(2,1)S(1)} %collective-permute-done.8.refs_1_, bf16[64,512]{1,0:T(8,128)(2,1)} %collective-permute-done.9.refs_2_, bf16[2,256,2048]{2,1,0:T(8,128)(2,1)S(1)} %copy-done.2, ...), custom_call_target="tpu_custom_call" | custom-call | tf_op jit(solution)/shard_map/last/pallas_call | solution.py:681
  101.8 0.2 collective-permute-start.14
  102.0 1.2 %collective-permute-start.16 = (bf16[80,128]{1,0:T(8,128)(2,1)S(1)}, bf16[80,128]{1,0:T(8,128)(2,1)S(1)}, u32[]{:S(2)}, u32[]{:S(2)}) collective-permute-start(bf16[80,128]{1,0:T(8,128)(2,1)S(1)} %get-tuple-element.58), channel_id=1, source_target_pairs={{0,130},{1,131},{2,128},{3,129},{4,134},{5,135},{6,132},{7,133},{8... | collective-permute-start | bytes 61448 | tf_op jit(solution)/shard_map/ppermute | solution.py:34
  103.2 2.0 %collective-permute-start.15 = (bf16[80,128]{1,0:T(8,128)(2,1)S(1)}, bf16[80,128]{1,0:T(8,128)(2,1)S(1)}, u32[]{:S(2)}, u32[]{:S(2)}) collective-permute-start(bf16[80,128]{1,0:T(8,128)(2,1)S(1)} %get-tuple-element.59), channel_id=1, source_target_pairs={{0,3},{1,2},{2,1},{3,0},{4,7},{5,6},{6,5},{7,4},{8,11},{9,10},{10,... | collective-permute-start | bytes 61448 | tf_op jit(solution)/shard_map/ppermute | solution.py:22
  105.1 0.9 collective-permute-start.17
  106.2 4.6 %begin.1 = (f32[272,384]{1,0:T(8,128)S(1)}, f32[384,384]{1,0:T(8,128)S(1)}, f32[384,128]{1,0:T(8,128)S(1)}, f32[2,64,128]{2,1,0:T(8,128)S(1)}, f32[2,64,128]{2,1,0:T(8,128)S(1)}) custom-call(s32[1]{0:T(128)} %bitcast.refs_0_.place.me, s32[1]{0:T(128)} %bitcast.1.grp, s32[4]{0:T(128)S(1)} %copy-done.9, bf16[4,64,4096]{2,1,0:T(8,128)(2,1)} %w3.3, ...), custom_call_target="tpu_custom_call" | custom-call | tf_op jit(solution)/shard_map/begin/pallas_call | solution.py:543
  110.9 3.8 %prepare.1 = (bf16[768,256]{1,0:T(8,128)(2,1)S(1)}, f32[2,256,256]{2,1,0:T(8,128)S(1)}, f32[2,64,256]{2,1,0:T(8,128)S(1)}, f32[2,8,256]{2,1,0:T(8,128)S(1)}, f32[2,64,128]{2,1,0:T(8,128)S(1)}) custom-call(s32[1]{0:T(128)} %bitcast.refs_0_.place.me, s32[1]{0:T(128)} %bitcast.1.grp, s32[4]{0:T(128)S(1)} %copy-done.9, bf16[4,64,4096]{2,1,0:T(8,128)(2,1)S(1)} %copy-done.1, ...), custom_call_target="tpu_custom_call" | custom-call | tf_op jit(solution)/shard_map/prepare/pallas_call | solution.py:627
  114.7 1.2 %render.1 = (bf16[2,64,256]{2,1,0:T(8,128)(2,1)}, bf16[2,64,256]{2,1,0:T(8,128)(2,1)}) custom-call(s32[1]{0:T(128)} %bitcast.refs_0_.place.me, bf16[64,128]{1,0:T(8,128)(2,1)S(1)} %get-tuple-element.50.refs_0_, bf16[64,128]{1,0:T(8,128)(2,1)S(1)} %collective-permute-done.5.refs_1_, bf16[64,128]{1,0:T(8,128)(2,1)S(1)} %collective-permute-done.6.refs_2_, ...), custom_call_target="tpu_custom_call" | custom-call | tf_op jit(solution)/shard_map/render/pallas_call | solution.py:709
  (59 shorter events, 0.8 us)
Async XLA Ops:
  0.6 71.8 %copy-start = (bf16[4096,128]{1,0:T(8,128)(2,1)S(1)}, bf16[4096,128]{1,0:T(8,128)(2,1)}, u32[]{:S(2)}) copy-start(bf16[4096,128]{1,0:T(8,128)(2,1)} %param.18) | copy-start | bytes 3145732
  4.1 8.9 %copy-start.9 = (s32[4]{0:T(128)S(1)}, s32[4]{0:T(128)}, u32[]{:S(2)}) copy-start(s32[4]{0:T(128)} %kinds.5) | copy-start | bytes 52
  4.1 8.9 %collective-permute-start.2 = (bf16[3,256,2048]{2,1,0:T(8,128)(2,1)}, bf16[3,256,2048]{2,1,0:T(8,128)(2,1)}, u32[]{:S(2)}, u32[]{:S(2)}) collective-permute-start(bf16[3,256,2048]{2,1,0:T(8,128)(2,1)} %get-tuple-element.38), channel_id=1, source_target_pairs={{0,1},{1,0},{2,3},{3,2},{4,5},{5,4},{6,7},{7,6},{8,9},{9,8},{10,11... | collective-permute-start | bytes 9437192 | tf_op jit(solution)/shard_map/ppermute | solution.py:22
  9.3 26.4 %collective-permute-start = (bf16[128,2048]{1,0:T(8,128)(2,1)}, bf16[128,2048]{1,0:T(8,128)(2,1)}, u32[]{:S(2)}, u32[]{:S(2)}) collective-permute-start(bf16[128,2048]{1,0:T(8,128)(2,1)} %first.2), channel_id=1, source_target_pairs={{0,2},{1,3},{2,0},{3,1},{4,6},{5,7},{6,4},{7,5},{8,10},{9,11},{10,... | collective-permute-start | bytes 1572872 | tf_op jit(solution)/shard_map/ppermute | solution.py:22
  11.3 24.4 %collective-permute-start.1 = (bf16[128,2048]{1,0:T(8,128)(2,1)}, bf16[128,2048]{1,0:T(8,128)(2,1)}, u32[]{:S(2)}, u32[]{:S(2)}) collective-permute-start(bf16[128,2048]{1,0:T(8,128)(2,1)} %first.3), channel_id=1, source_target_pairs={{0,3},{1,2},{2,1},{3,0},{4,7},{5,6},{6,5},{7,4},{8,11},{9,10},{10,... | collective-permute-start | bytes 1572872 | tf_op jit(solution)/shard_map/ppermute | solution.py:22
  13.1 25.4 %copy-start.2 = (bf16[2,256,2048]{2,1,0:T(8,128)(2,1)S(1)}, bf16[2,256,2048]{2,1,0:T(8,128)(2,1)}, u32[]{:S(2)}) copy-start(bf16[2,256,2048]{2,1,0:T(8,128)(2,1)} %refs_3_.7) | copy-start | bytes 6291460
  35.7 14.5 %copy-start.3 = (bf16[16,80,512]{2,1,0:T(8,128)(2,1)}, bf16[16,80,512]{2,1,0:T(8,128)(2,1)S(1)}, u32[]{:S(2)}) copy-start(bf16[16,80,512]{2,1,0:T(8,128)(2,1)S(1)} %get-tuple-element.39.refs_5_) | copy-start | bytes 3932164
  35.7 2.8 %collective-permute-start.3 = (f32[16,512]{1,0:T(8,128)S(1)}, f32[16,512]{1,0:T(8,128)S(1)}, u32[]{:S(2)}, u32[]{:S(2)}) collective-permute-start(f32[16,512]{1,0:T(8,128)S(1)} %get-tuple-element.43), channel_id=1, source_target_pairs={{0,2},{1,3},{2,0},{3,1},{4,6},{5,7},{6,4},{7,5},{8,10},{9,11},{10,... | collective-permute-start | bytes 98312 | tf_op jit(solution)/shard_map/ppermute | solution.py:22
  38.4 17.6 %copy-start.13 = (s32[2,256]{1,0:T(2,128)S(1)}, s32[2,256]{1,0:T(2,128)}, u32[]{:S(2)}) copy-start(s32[2,256]{1,0:T(2,128)} %param.17) | copy-start | bytes 6148
  38.4 19.3 %copy-start.14 = (bf16[64,512]{1,0:T(8,128)(2,1)S(1)}, bf16[64,512]{1,0:T(8,128)(2,1)}, u32[]{:S(2)}) copy-start(bf16[64,512]{1,0:T(8,128)(2,1)} %get-tuple-element.52) | copy-start | bytes 196612
  50.2 2.9 %collective-permute-start.4 = (bf16[80,256]{1,0:T(8,128)(2,1)S(1)}, bf16[80,256]{1,0:T(8,128)(2,1)S(1)}, u32[]{:S(2)}, u32[]{:S(2)}) collective-permute-start(bf16[80,256]{1,0:T(8,128)(2,1)S(1)} %remote.1), channel_id=1, source_target_pairs={{0,2},{1,3},{2,0},{3,1},{4,6},{5,7},{6,4},{7,5},{8,10},{9,11},{10,... | collective-permute-start | bytes 122888 | tf_op jit(solution)/shard_map/ppermute | solution.py:22
  53.3 17.8 %copy-start.11 = (bf16[64,128]{1,0:T(8,128)(2,1)}, bf16[64,128]{1,0:T(8,128)(2,1)S(1)}, u32[]{:S(2)}) copy-start(bf16[64,128]{1,0:T(8,128)(2,1)S(1)} %get-tuple-element.51) | copy-start | bytes 49156
  53.3 6.0 %collective-permute-start.5 = (bf16[64,128]{1,0:T(8,128)(2,1)S(1)}, bf16[64,128]{1,0:T(8,128)(2,1)S(1)}, u32[]{:S(2)}, u32[]{:S(2)}) collective-permute-start(bf16[64,128]{1,0:T(8,128)(2,1)S(1)} %get-tuple-element.51), channel_id=1, source_target_pairs={{0,1},{1,0},{2,3},{3,2},{4,5},{5,4},{6,7},{7,6},{8,9},{9,8},{10,11... | collective-permute-start | bytes 49160 | tf_op jit(solution)/shard_map/ppermute | solution.py:22
  56.0 27.1 %collective-permute-start.10 = (bf16[64,2048]{1,0:T(8,128)(2,1)}, bf16[64,2048]{1,0:T(8,128)(2,1)}, u32[]{:S(2)}, u32[]{:S(2)}) collective-permute-start(bf16[64,2048]{1,0:T(8,128)(2,1)} %get-tuple-element.54), channel_id=1, source_target_pairs={{0,2},{1,3},{2,0},{3,1},{4,6},{5,7},{6,4},{7,5},{8,10},{9,11},{10,... | collective-permute-start | bytes 786440 | tf_op jit(solution)/shard_map/ppermute | solution.py:22
  56.0 27.4 %collective-permute-start.11 = (bf16[64,2048]{1,0:T(8,128)(2,1)}, bf16[64,2048]{1,0:T(8,128)(2,1)}, u32[]{:S(2)}, u32[]{:S(2)}) collective-permute-start(bf16[64,2048]{1,0:T(8,128)(2,1)} %get-tuple-element.55), channel_id=1, source_target_pairs={{0,3},{1,2},{2,1},{3,0},{4,7},{5,6},{6,5},{7,4},{8,11},{9,10},{10,... | collective-permute-start | bytes 786440 | tf_op jit(solution)/shard_map/ppermute | solution.py:22
  57.8 13.2 %collective-permute-start.8 = (bf16[64,512]{1,0:T(8,128)(2,1)S(1)}, bf16[64,512]{1,0:T(8,128)(2,1)S(1)}, u32[]{:S(2)}, u32[]{:S(2)}) collective-permute-start(bf16[64,512]{1,0:T(8,128)(2,1)S(1)} %copy-done.14), channel_id=1, source_target_pairs={{0,2},{1,3},{2,0},{3,1},{4,6},{5,7},{6,4},{7,5},{8,10},{9,11},{10,... | collective-permute-start | bytes 196616 | tf_op jit(solution)/shard_map/ppermute | solution.py:22
  57.8 23.6 %collective-permute-start.12 = (bf16[64,1536]{1,0:T(8,128)(2,1)}, bf16[64,1536]{1,0:T(8,128)(2,1)}, u32[]{:S(2)}, u32[]{:S(2)}) collective-permute-start(bf16[64,1536]{1,0:T(8,128)(2,1)} %get-tuple-element.56), channel_id=1, source_target_pairs={{0,2},{1,3},{2,0},{3,1},{4,6},{5,7},{6,4},{7,5},{8,10},{9,11},{10,... | collective-permute-start | bytes 589832 | tf_op jit(solution)/shard_map/ppermute | solution.py:22
  59.3 22.1 %collective-permute-start.13 = (bf16[64,1536]{1,0:T(8,128)(2,1)}, bf16[64,1536]{1,0:T(8,128)(2,1)}, u32[]{:S(2)}, u32[]{:S(2)}) collective-permute-start(bf16[64,1536]{1,0:T(8,128)(2,1)} %get-tuple-element.57), channel_id=1, source_target_pairs={{0,3},{1,2},{2,1},{3,0},{4,7},{5,6},{6,5},{7,4},{8,11},{9,10},{10,... | collective-permute-start | bytes 589832 | tf_op jit(solution)/shard_map/ppermute | solution.py:22
  71.0 10.2 %collective-permute-start.9 = (bf16[64,512]{1,0:T(8,128)(2,1)}, bf16[64,512]{1,0:T(8,128)(2,1)}, u32[]{:S(2)}, u32[]{:S(2)}) collective-permute-start(bf16[64,512]{1,0:T(8,128)(2,1)} %get-tuple-element.53), channel_id=1, source_target_pairs={{0,3},{1,2},{2,1},{3,0},{4,7},{5,6},{6,5},{7,4},{8,11},{9,10},{10,... | collective-permute-start | bytes 196616 | tf_op jit(solution)/shard_map/ppermute | solution.py:22
  74.3 11.9 %copy-start.4 = (bf16[16,80,512]{2,1,0:T(8,128)(2,1)S(1)}, bf16[16,80,512]{2,1,0:T(8,128)(2,1)}, u32[]{:S(2)}) copy-start(bf16[16,80,512]{2,1,0:T(8,128)(2,1)} %copy-done.3) | copy-start | bytes 3932164
  81.2 21.9 %collective-permute-start.18 = (bf16[16,64,128]{2,1,0:T(8,128)(2,1)}, bf16[16,64,128]{2,1,0:T(8,128)(2,1)S(1)}, u32[]{:S(2)}, u32[]{:S(2)}) collective-permute-start(bf16[16,64,128]{2,1,0:T(8,128)(2,1)} %copy-done.10), channel_id=1, source_target_pairs={{0,1},{1,0},{2,3},{3,2},{4,5},{5,4},{6,7},{7,6},{8,9},{9,8},{10,11... | collective-permute-start | bytes 786440 | tf_op jit(solution)/shard_map/ppermute | solution.py:22
  81.4 33.3 %collective-permute-start.20 = (bf16[16,64,128]{2,1,0:T(8,128)(2,1)}, bf16[16,64,128]{2,1,0:T(8,128)(2,1)S(1)}, u32[]{:S(2)}, u32[]{:S(2)}) collective-permute-start(bf16[16,64,128]{2,1,0:T(8,128)(2,1)} %copy-done.10), channel_id=1, source_target_pairs={{0,129},{1,128},{2,131},{3,130},{4,133},{5,132},{6,135},{7,134},{8... | collective-permute-start | bytes 786440 | tf_op jit(solution)/shard_map/ppermute | solution.py:34
  81.4 23.7 %collective-permute-start.19 = (bf16[16,64,128]{2,1,0:T(8,128)(2,1)S(1)}, bf16[16,64,128]{2,1,0:T(8,128)(2,1)S(1)}, u32[]{:S(2)}, u32[]{:S(2)}) collective-permute-start(bf16[16,64,128]{2,1,0:T(8,128)(2,1)S(1)} %get-tuple-element.60.refs_8_), channel_id=1, source_target_pairs={{0,128},{128,0},{1,129},{129,1},{2,130},{130,2},{3,131},{131,3},{4... | collective-permute-start | bytes 786440 | tf_op jit(solution)/shard_map/ppermute | solution.py:26
  83.1 18.8 %collective-permute-start.7 = (bf16[64,128]{1,0:T(8,128)(2,1)}, bf16[64,128]{1,0:T(8,128)(2,1)S(1)}, u32[]{:S(2)}, u32[]{:S(2)}) collective-permute-start(bf16[64,128]{1,0:T(8,128)(2,1)} %copy-done.11), channel_id=1, source_target_pairs={{0,129},{1,128},{2,131},{3,130},{4,133},{5,132},{6,135},{7,134},{8... | collective-permute-start | bytes 49160 | tf_op jit(solution)/shard_map/ppermute | solution.py:34
  83.5 18.3 %collective-permute-start.6 = (bf16[64,128]{1,0:T(8,128)(2,1)S(1)}, bf16[64,128]{1,0:T(8,128)(2,1)S(1)}, u32[]{:S(2)}, u32[]{:S(2)}) collective-permute-start(bf16[64,128]{1,0:T(8,128)(2,1)S(1)} %get-tuple-element.50.refs_0_), channel_id=1, source_target_pairs={{0,128},{128,0},{1,129},{129,1},{2,130},{130,2},{3,131},{131,3},{4... | collective-permute-start | bytes 49160 | tf_op jit(solution)/shard_map/ppermute | solution.py:26
  99.1 6.9 %copy-start.12 = (bf16[512,128]{1,0:T(8,128)(2,1)S(1)}, bf16[512,128]{1,0:T(8,128)(2,1)}, u32[]{:S(2)}) copy-start(bf16[512,128]{1,0:T(8,128)(2,1)} %gather_fusion) | copy-start | bytes 393220
  101.8 12.9 %collective-permute-start.14 = (bf16[80,128]{1,0:T(8,128)(2,1)S(1)}, bf16[80,128]{1,0:T(8,128)(2,1)S(1)}, u32[]{:S(2)}, u32[]{:S(2)}) collective-permute-start(bf16[80,128]{1,0:T(8,128)(2,1)S(1)} %get-tuple-element.58), channel_id=1, source_target_pairs={{0,2},{1,3},{2,0},{3,1},{4,6},{5,7},{6,4},{7,5},{8,10},{9,11},{10,... | collective-permute-start | bytes 61448 | tf_op jit(solution)/shard_map/ppermute | solution.py:22
  102.0 12.7 %collective-permute-start.16 = (bf16[80,128]{1,0:T(8,128)(2,1)S(1)}, bf16[80,128]{1,0:T(8,128)(2,1)S(1)}, u32[]{:S(2)}, u32[]{:S(2)}) collective-permute-start(bf16[80,128]{1,0:T(8,128)(2,1)S(1)} %get-tuple-element.58), channel_id=1, source_target_pairs={{0,130},{1,131},{2,128},{3,129},{4,134},{5,135},{6,132},{7,133},{8... | collective-permute-start | bytes 61448 | tf_op jit(solution)/shard_map/ppermute | solution.py:34
  103.2 11.5 %collective-permute-start.15 = (bf16[80,128]{1,0:T(8,128)(2,1)S(1)}, bf16[80,128]{1,0:T(8,128)(2,1)S(1)}, u32[]{:S(2)}, u32[]{:S(2)}) collective-permute-start(bf16[80,128]{1,0:T(8,128)(2,1)S(1)} %get-tuple-element.59), channel_id=1, source_target_pairs={{0,3},{1,2},{2,1},{3,0},{4,7},{5,6},{6,5},{7,4},{8,11},{9,10},{10,... | collective-permute-start | bytes 61448 | tf_op jit(solution)/shard_map/ppermute | solution.py:22
  105.1 9.6 %collective-permute-start.17 = (bf16[80,128]{1,0:T(8,128)(2,1)S(1)}, bf16[80,128]{1,0:T(8,128)(2,1)S(1)}, u32[]{:S(2)}, u32[]{:S(2)}) collective-permute-start(bf16[80,128]{1,0:T(8,128)(2,1)S(1)} %get-tuple-element.59), channel_id=1, source_target_pairs={{0,131},{1,130},{2,129},{3,128},{4,135},{5,134},{6,133},{7,132},{8... | collective-permute-start | bytes 61448 | tf_op jit(solution)/shard_map/ppermute | solution.py:34
  106.1 4.7 %copy-start.1 = (bf16[4,64,4096]{2,1,0:T(8,128)(2,1)S(1)}, bf16[4,64,4096]{2,1,0:T(8,128)(2,1)}, u32[]{:S(2)}) copy-start(bf16[4,64,4096]{2,1,0:T(8,128)(2,1)} %w3.3) | copy-start | bytes 6291460
  106.2 4.7 %copy-start.5 = (bf16[128,4096]{1,0:T(8,128)(2,1)S(1)}, bf16[128,4096]{1,0:T(8,128)(2,1)}, u32[]{:S(2)}) copy-start(bf16[128,4096]{1,0:T(8,128)(2,1)} %w_env.3) | copy-start | bytes 3145732
  (4 other events, 14.8 us)
